TPU v7x, 128 devices: a whole 4x4x4 slice. The times are simulated.
128 devices in a mesh: slab: 4 (over z), mode: 32 (over x, y, core).
Axes of the slice: x: 4, y: 4, z: 4, core: 2. Of those that a mesh axis runs over, the one named last changes fastest.
Arguments:
- field: bfloat16 [1024, 8, 32, 256], P('mode', 'slab'), may hold values from -6 to 6
- coefficient: float32 [9, 8, 32, 256], P(None, 'slab'), may hold values from 0.1 to 1
- slot_mode: int32 [1024], replicated, may hold values from 0 to 495, as said below
- couplings: int32 [2640, 4], replicated, may hold values from -8 to 494, as said below
Outputs:
- images: float32 [1024, 8, 32, 256], P('mode', 'slab')
Inputs may be any that keep to these rules, and one draw needn't show every extreme that they name: `slot_mode`: slot s belongs to group s // 32. A value 495 marks an empty slot; every mode stands in exactly one slot; a group's occupied slots come first in it; every group holds at least one mode and one group fills all 32 of its slots. `couplings`: columns are mode k, mode i (k != i), term t from 1 to 8, and a nonzero weight; every row (k, i, t, w) stands beside its mirror (i, k, t, w).
All inputs are finite; a program needn't handle non-finite values.
Results may differ from a plain program's by a relative error of at most 0.0003.
Values may be sent and summed in bfloat16 or wider, within the bound.
A program may use at most 192 MiB of HBM per device.

v0:
```python
import jax
import jax.numpy as jnp
from jax import lax
from jax.sharding import PartitionSpec as P

MODES = 495


def with_halo(block, sides, width):
    for axis, dim in sides:
        count = lax.axis_size(axis)
        forward = [(i, i + 1) for i in range(count - 1)]
        backward = [(target, source) for source, target in forward]
        low = lax.ppermute(
            lax.slice_in_dim(block, block.shape[dim] - width, None, axis=dim), axis, forward
        )
        high = lax.ppermute(lax.slice_in_dim(block, 0, width, axis=dim), axis, backward)
        block = jnp.concatenate([low, block, high], axis=dim)
    return block


def extended(shard, sides, width):
    edges = {}
    for axis, dim in sides:
        size, length = (lax.axis_size(axis), shard.shape[dim])
        up = [(i, (i + 1) % size) for i in range(size - 1)]
        last = lax.slice_in_dim(shard, length - width, length, axis=dim)
        initial = lax.slice_in_dim(shard, 0, width, axis=dim)
        edges[dim] = (
            lax.ppermute(last, axis, up),
            lax.ppermute(initial, axis, [(b, a) for a, b in up]),
        )
    done = []
    for _, dim in sides:
        low, high = edges[dim]
        around = [(width, width) if d in done else (0, 0) for d in range(shard.ndim)]
        shard = jnp.concatenate([jnp.pad(low, around), shard, jnp.pad(high, around)], axis=dim)
        done.append(dim)
    return shard


def modes_image(val_ext, coef_ext):
    center_coef = coef_ext[1:-1, 1:-1]
    center_vals = val_ext[1:-1, 1:-1]
    summed = 0.5 * (center_coef + coef_ext[2:, 1:-1]) * (center_vals - val_ext[2:, 1:-1])
    summed = summed + 0.5 * (center_coef + coef_ext[:-2, 1:-1]) * (center_vals - val_ext[:-2, 1:-1])
    summed = summed + 0.5 * (center_coef + coef_ext[1:-1, 2:]) * (center_vals - val_ext[1:-1, 2:])
    summed = summed + 0.5 * (center_coef + coef_ext[1:-1, :-2]) * (center_vals - val_ext[1:-1, :-2])
    padded_coef = jnp.pad(center_coef, ((0, 0), (0, 0), (0, 0), (1, 1)))
    padded_vals = jnp.pad(center_vals, ((0, 0), (0, 0), (0, 0), (1, 1)))
    summed = summed + 0.5 * (center_coef + padded_coef[:, :, :, 2:]) * (
        center_vals - padded_vals[:, :, :, 2:]
    )
    summed = summed + 0.5 * (center_coef + padded_coef[:, :, :, :-2]) * (
        center_vals - padded_vals[:, :, :, :-2]
    )
    return summed


def coupling_matrix(couplings, term_count):
    mode_ids = jnp.arange(MODES, dtype=jnp.int32)
    column_ids = jnp.arange(term_count * MODES, dtype=jnp.int32)
    target = (couplings[:, 0:1] == mode_ids[None, :]).astype(jnp.bfloat16)
    column = couplings[:, 2] * MODES + couplings[:, 1]
    weight = (couplings[:, 3].astype(jnp.float32) * 0.125).astype(jnp.bfloat16)
    scaled = jnp.where(
        column[:, None] == column_ids[None, :], weight[:, None], jnp.zeros((), jnp.bfloat16)
    )
    galerkin = lax.dot_general(
        target, scaled, (((0,), (0,)), ((), ())), preferred_element_type=jnp.float32
    )
    identity = (column_ids[None, :] == mode_ids[:, None]).astype(jnp.float32)
    return galerkin + identity


def on_device(field, coefficient, slot_mode, couplings):
    groups = lax.axis_size("mode")
    group = lax.axis_index("mode")
    slots = field.shape[0]
    spatial = field.shape[1:]
    term_count = coefficient.shape[0]
    coef_planes = with_halo(coefficient, (("slab", 1),), 1)
    all_slots = jnp.arange(groups * slots, dtype=jnp.int32)
    slot_of_mode = jnp.zeros((MODES + 1,), jnp.int32).at[slot_mode].set(all_slots)[:MODES]
    galerkin = coupling_matrix(couplings, term_count)
    whole_slots = lax.all_to_all(field, "mode", split_axis=2, concat_axis=0, tiled=True)
    row_count = whole_slots.shape[2]
    chosen = jnp.take(whole_slots, slot_of_mode, axis=0).transpose(1, 2, 0, 3)
    val_ext = extended(chosen, (("slab", 0), ("mode", 1)), 1).astype(jnp.float32)
    coef_rows = jnp.pad(coef_planes, ((0, 0), (0, 0), (1, 1), (0, 0)))
    coef_rows = lax.dynamic_slice_in_dim(coef_rows, group * row_count, row_count + 2, 2)
    stacked = jnp.stack(
        [
            modes_image(val_ext, coef_rows[term_index][:, :, None, :])
            for term_index in range(term_count)
        ]
    )
    galerkin_cube = galerkin.reshape(MODES, term_count, MODES)
    coupled = jnp.einsum(
        "kti,txrin->xrkn",
        galerkin_cube,
        stacked,
        precision=lax.Precision.HIGHEST,
        preferred_element_type=jnp.float32,
    )
    empty_row = jnp.zeros((spatial[0], row_count, 1, spatial[2]), jnp.float32)
    coupled = jnp.concatenate([coupled, empty_row], axis=2)
    coupled = jnp.take(coupled, slot_mode, axis=2).transpose(2, 0, 1, 3)
    return lax.all_to_all(coupled, "mode", split_axis=0, concat_axis=2, tiled=True)


def solution(mesh):
    in_specs = (P("mode", "slab", None, None), P(None, "slab", None, None), P(), P())
    out_specs = P("mode", "slab", None, None)
    return jax.shard_map(
        on_device, mesh=mesh, in_specs=in_specs, out_specs=out_specs, check_vma=False
    )
```

profile of v0, /device:TPU:1, one launch (start us, length us, event | category | flops | bytes accessed | tf_op | source)
XLA Modules:
  0.0 183.5 jit_solution(6672897734824196080)
XLA Ops:
  0.0 1.1 fusion.111
  1.1 4.4 %collective-permute-start = (f32[9,1,32,256]{3,2,1,0:T(8,128)S(1)}, f32[9,1,32,256]{3,2,1,0:T(8,128)S(1)}, u32[]{:S(2)}, u32[]{:S(2)}) collective-permute-start(f32[9,1,32,256]{3,2,1,0:T(8,128)S(1)} %get-tuple-element.15), channel_id=1, source_target_pairs={{0,32},{32,64},{64,96},{1,33},{33,65},{65,97},{2,34},{34,66},{66,9... | collective-permute-start | bytes 884744 | tf_op jit(solution)/shard_map/ppermute | solution.py:14
  5.5 1.3 collective-permute-start.1
  6.8 2.8 %copy.30 = bf16[32,2,32,256]{3,0,1,2:T(8,128)(2,1)} copy(bf16[32,2,32,256]{3,2,1,0:T(8,128)(2,1)} %param.4) | data formatting | bytes 2097152 | tf_op args[0]
  9.6 8.0 %all-to-all-start = ((bf16[32,2,32,256]{3,0,1,2:T(8,128)(2,1)}), bf16[32,2,32,256]{3,0,1,2:T(8,128)(2,1)S(1)}, u32[]{:S(2)}, u32[]{:S(2)}) async-start(bf16[32,2,32,256]{3,0,1,2:T(8,128)(2,1)} %copy.30), calls=%async_computation | async-start | bytes 2097152 | tf_op jit(solution)/shard_map/all_to_all | solution.py:86
  17.6 0.7 broadcast_clamp_fusion
  18.3 4.5 %scatter_custom_fusion = s32[496]{0:T(512)S(1)} fusion(s32[1024]{0:T(1024)S(1)} %get-tuple-element.73, s32[1024]{0:T(1024)S(1)} %iota.15, s32[]{:T(128)} %constant.15.clone.1), kind=kCustom, calls=%fused_computation.257 | custom fusion | bytes 1988 | tf_op jit(solution)/shard_map/scatter | solution.py:84
  22.8 1.0 slice_reduce_fusion
  23.8 0.8 convert_reduce_fusion
  24.6 17.7 %convert_add_fusion = f32[495,4455]{1,0:T(8,128)} fusion(s32[2640]{0:T(1024)S(1)} %get-tuple-element.6, bf16[2640]{0:T(1024)(128)(2,1)S(1)} %convert_reduce_fusion, s32[2640]{0:T(1024)S(1)} %get-tuple-element.5), kind=kOutput, calls=%fused_computation.12 | convolution fusion | flops 11675033600 | bytes 8847300 | tf_op jit(solution)/shard_map/dot_general | solution.py:69
  42.3 14.9 %reshape.177 = f32[495,9,495]{2,1,0:T(8,128)} reshape(f32[495,4455]{1,0:T(8,128)} %convert_add_fusion) | data formatting | bytes 17641800 | tf_op jit(solution)/shard_map/reshape | solution.py:98
  57.2 0.1 fusion.28
  57.4 0.1 fusion.105
  57.5 0.1 fusion.103
  57.6 0.1 fusion.101
  57.7 0.1 fusion.99
  57.7 0.1 fusion.97
  57.9 0.1 fusion.95
  57.9 0.1 fusion.93
  58.0 0.1 fusion.91
  58.1 0.1 copy.31
  58.2 1.1 copy.32
  59.3 2.8 %gather_fusion = bf16[495,2,256]{2,1,0:T(2,128)(2,1)S(1)} fusion(bf16[1024,2,256]{2,1,0:T(2,128)(2,1)S(1)} %copy.32, s32[1024]{0:T(1024)S(1)} %pad_clamp_fusion), kind=kCustom, calls=%fused_computation | custom fusion | bytes 1015740 | tf_op jit(solution)/shard_map/jit(_take)/gather | solution.py:88
  62.1 0.1 fusion.25
  62.2 3.5 %collective-permute-start.2 = (bf16[2,1,495,256]{3,2,0,1:T(8,128)(2,1)S(1)}, bf16[2,1,495,256]{3,2,0,1:T(8,128)(2,1)S(1)}, u32[]{:S(2)}, u32[]{:S(2)}) collective-permute-start(bf16[2,1,495,256]{3,2,0,1:T(8,128)(2,1)S(1)} %fusion.25), channel_id=1, source_target_pairs={{0,1},{1,2},{2,3},{3,4},{4,5},{5,6},{6,7},{7,8},{8,9},{9,10},{10,1... | collective-permute-start | bytes 1520648 | tf_op jit(solution)/shard_map/ppermute | solution.py:30
  65.8 1.9 %collective-permute-start.5 = (bf16[2,1,495,256]{3,2,0,1:T(8,128)(2,1)S(1)}, bf16[2,1,495,256]{3,2,0,1:T(8,128)(2,1)S(1)}, u32[]{:S(2)}, u32[]{:S(2)}) collective-permute-start(bf16[2,1,495,256]{3,2,0,1:T(8,128)(2,1)S(1)} %fusion.25), channel_id=1, source_target_pairs={{1,0},{2,1},{3,2},{4,3},{5,4},{6,5},{7,6},{8,7},{9,8},{10,9},{11,1... | collective-permute-start | bytes 1520648 | tf_op jit(solution)/shard_map/ppermute | solution.py:31
  67.8 4.3 %collective-permute-start.3 = (bf16[1,1,495,256]{3,2,0,1:T(8,128)(2,1)S(1)}, bf16[1,1,495,256]{3,2,0,1:T(8,128)(2,1)S(1)}, u32[]{:S(2)}, u32[]{:S(2)}) collective-permute-start(bf16[1,1,495,256]{3,2,0,1:T(8,128)(2,1)S(1)} %get-tuple-element.16), channel_id=1, source_target_pairs={{0,32},{32,64},{64,96},{1,33},{33,65},{65,97},{2,34},{34,66},{66,9... | collective-permute-start | bytes 760328 | tf_op jit(solution)/shard_map/ppermute | solution.py:30
  72.1 1.3 collective-permute-start.4
  73.4 0.1 fusion.89
  73.9 2.8 %collective-permute-done.3 = bf16[1,1,495,256]{3,2,0,1:T(8,128)(2,1)S(1)} collective-permute-done((bf16[1,1,495,256]{3,2,0,1:T(8,128)(2,1)S(1)}, bf16[1,1,495,256]{3,2,0,1:T(8,128)(2,1)S(1)}, u32[]{:S(2)}, u32[]{:S(2)}) %collective-permute-start.3) | collective-permute-done | bytes 253472 | tf_op jit(solution)/shard_map/ppermute | solution.py:30
  76.7 4.1 %collective-permute-done.4 = bf16[1,1,495,256]{3,2,0,1:T(8,128)(2,1)S(1)} collective-permute-done((bf16[1,1,495,256]{3,2,0,1:T(8,128)(2,1)S(1)}, bf16[1,1,495,256]{3,2,0,1:T(8,128)(2,1)S(1)}, u32[]{:S(2)}, u32[]{:S(2)}) %collective-permute-start.4) | collective-permute-done | bytes 253472 | tf_op jit(solution)/shard_map/ppermute | solution.py:31
  80.8 0.6 fusion.14
  81.5 1.8 %bitcast_dynamic-update-slice_fusion.7 = (f32[9,2,1,495,256]{4,3,0,1,2:T(8,128)}, f32[2,1,495,256]{3,2,0,1:T(8,128)S(1)}, f32[2,1,495,256]{3,2,0,1:T(8,128)S(1)}...) fusion(f32[2,256]{1,0:T(2,128)S(1)} %get-tuple-element.116, ...), kind=kLoop, calls=%fused_computation.45 | loop fusion | flops 4308479 | bytes 13193216
  83.3 1.4 bitcast_dynamic-update-slice_fusion.6
  84.8 1.4 bitcast_dynamic-update-slice_fusion.5
  86.2 1.4 bitcast_dynamic-update-slice_fusion.4
  87.6 1.4 bitcast_dynamic-update-slice_fusion.3
  89.0 1.4 bitcast_dynamic-update-slice_fusion.2
  90.4 1.4 bitcast_dynamic-update-slice_fusion.1
  91.8 1.4 bitcast_dynamic-update-slice_fusion
  93.2 1.5 bitcast_dynamic-update-slice_fusion.8
  94.7 0.3 slice-done.3
  95.0 40.6 %fusion.18 = f32[2,1,495,256]{3,2,0,1:T(8,128)S(1)} fusion(f32[495,9,495,1]{2,1,0,3:T(8,128)S(1)} %bitcast.251, f32[9,2,1,495,256]{4,3,0,1,2:T(8,128)} %bitcast_dynamic-update-slice_fusion.8), kind=kOutput, calls=%fused_computation.31 | convolution fusion | flops 13548902400 | bytes 18958500 | tf_op jit(solution)/shard_map/kti,txrin->xrkn/dot_general | solution.py:99
  135.7 0.8 copy.44
  136.5 4.1 %gather_fusion.1 = f32[1024,2,256]{2,1,0:T(2,128)S(1)} fusion(f32[2,496,256]{2,0,1:T(2,128)S(1)} %copy.44, s32[1024]{0:T(1024)S(1)} %get-tuple-element.72), kind=kCustom, calls=%fused_computation.1 | custom fusion | bytes 4198400 | tf_op jit(solution)/shard_map/jit(_take)/gather | solution.py:108
  140.7 3.7 %fusion.17 = f32[1024,2,1,256]{3,1,2,0:T(2,128)S(1)} fusion(f32[1024,2,256]{2,1,0:T(2,128)S(1)} %gather_fusion.1, pred[1024]{0:T(1024)(128)(4,1)S(1)} %compare_and_fusion), kind=kLoop, calls=%fused_computation.24 | loop fusion | flops 524288 | bytes 4195328 | tf_op jit(solution)/shard_map/transpose | solution.py:108
  144.4 36.3 %all_to_all.36 = f32[1024,2,1,256]{3,1,2,0:T(2,128)S(1)} all-to-all(f32[1024,2,1,256]{3,1,2,0:T(2,128)S(1)} %fusion.17), channel_id=1, replica_groups=mesh['slab'=4,'mode'=32] {'mode'}, dimensions={0} | all-to-all | bytes 4194304 | tf_op jit(solution)/shard_map/all_to_all | solution.py:109
  180.7 2.5 %copy.167 = f32[32,32,2,1,256]{4,0,2,1,3:T(8,128)} copy(f32[32,32,2,1,256]{4,2,1,0,3:T(2,128)S(1)} %bitcast.252) | data formatting | bytes 4194304 | tf_op jit(solution)/shard_map/all_to_all | solution.py:109
  (82 shorter events, 0.5 us)
Async XLA Ops:
  1.1 56.1 %collective-permute-start = (f32[9,1,32,256]{3,2,1,0:T(8,128)S(1)}, f32[9,1,32,256]{3,2,1,0:T(8,128)S(1)}, u32[]{:S(2)}, u32[]{:S(2)}) collective-permute-start(f32[9,1,32,256]{3,2,1,0:T(8,128)S(1)} %get-tuple-element.15), channel_id=1, source_target_pairs={{0,32},{32,64},{64,96},{1,33},{33,65},{65,97},{2,34},{34,66},{66,9... | collective-permute-start | bytes 884744 | tf_op jit(solution)/shard_map/ppermute | solution.py:14
  5.5 51.7 %collective-permute-start.1 = (f32[9,1,32,256]{3,2,1,0:T(8,128)S(1)}, f32[9,1,32,256]{3,2,1,0:T(8,128)S(1)}, u32[]{:S(2)}, u32[]{:S(2)}) collective-permute-start(f32[9,1,32,256]{3,2,1,0:T(8,128)S(1)} %get-tuple-element.14), channel_id=1, source_target_pairs={{32,0},{64,32},{96,64},{33,1},{65,33},{97,65},{34,2},{66,34},{98,6... | collective-permute-start | bytes 884744 | tf_op jit(solution)/shard_map/ppermute | solution.py:17
  9.6 48.6 %all-to-all-start = ((bf16[32,2,32,256]{3,0,1,2:T(8,128)(2,1)}), bf16[32,2,32,256]{3,0,1,2:T(8,128)(2,1)S(1)}, u32[]{:S(2)}, u32[]{:S(2)}) async-start(bf16[32,2,32,256]{3,0,1,2:T(8,128)(2,1)} %copy.30), calls=%async_computation | async-start | bytes 2097152 | tf_op jit(solution)/shard_map/all_to_all | solution.py:86
  42.3 14.9 %copy-start.1 = (s32[1024]{0:T(1024)S(1)}, s32[1024]{0:T(1024)}, u32[]{:S(2)}) copy-start(s32[1024]{0:T(1024)} %param.6) | copy-start | bytes 12292
  42.3 14.9 %copy-start = (f32[9,2,32,256]{3,2,1,0:T(8,128)S(1)}, f32[9,2,32,256]{3,2,1,0:T(8,128)}, u32[]{:S(2)}) copy-start(f32[9,2,32,256]{3,2,1,0:T(8,128)} %param.5) | copy-start | bytes 1769476
  62.2 18.6 %collective-permute-start.2 = (bf16[2,1,495,256]{3,2,0,1:T(8,128)(2,1)S(1)}, bf16[2,1,495,256]{3,2,0,1:T(8,128)(2,1)S(1)}, u32[]{:S(2)}, u32[]{:S(2)}) collective-permute-start(bf16[2,1,495,256]{3,2,0,1:T(8,128)(2,1)S(1)} %fusion.25), channel_id=1, source_target_pairs={{0,1},{1,2},{2,3},{3,4},{4,5},{5,6},{6,7},{7,8},{8,9},{9,10},{10,1... | collective-permute-start | bytes 1520648 | tf_op jit(solution)/shard_map/ppermute | solution.py:30
  65.8 15.0 %collective-permute-start.5 = (bf16[2,1,495,256]{3,2,0,1:T(8,128)(2,1)S(1)}, bf16[2,1,495,256]{3,2,0,1:T(8,128)(2,1)S(1)}, u32[]{:S(2)}, u32[]{:S(2)}) collective-permute-start(bf16[2,1,495,256]{3,2,0,1:T(8,128)(2,1)S(1)} %fusion.25), channel_id=1, source_target_pairs={{1,0},{2,1},{3,2},{4,3},{5,4},{6,5},{7,6},{8,7},{9,8},{10,9},{11,1... | collective-permute-start | bytes 1520648 | tf_op jit(solution)/shard_map/ppermute | solution.py:31
  67.8 8.9 %collective-permute-start.3 = (bf16[1,1,495,256]{3,2,0,1:T(8,128)(2,1)S(1)}, bf16[1,1,495,256]{3,2,0,1:T(8,128)(2,1)S(1)}, u32[]{:S(2)}, u32[]{:S(2)}) collective-permute-start(bf16[1,1,495,256]{3,2,0,1:T(8,128)(2,1)S(1)} %get-tuple-element.16), channel_id=1, source_target_pairs={{0,32},{32,64},{64,96},{1,33},{33,65},{65,97},{2,34},{34,66},{66,9... | collective-permute-start | bytes 760328 | tf_op jit(solution)/shard_map/ppermute | solution.py:30
  72.1 8.8 %collective-permute-start.4 = (bf16[1,1,495,256]{3,2,0,1:T(8,128)(2,1)S(1)}, bf16[1,1,495,256]{3,2,0,1:T(8,128)(2,1)S(1)}, u32[]{:S(2)}, u32[]{:S(2)}) collective-permute-start(bf16[1,1,495,256]{3,2,0,1:T(8,128)(2,1)S(1)} %get-tuple-element.17), channel_id=1, source_target_pairs={{32,0},{64,32},{96,64},{33,1},{65,33},{97,65},{34,2},{66,34},{98,6... | collective-permute-start | bytes 760328 | tf_op jit(solution)/shard_map/ppermute | solution.py:31
  87.6 7.1 %slice-start = ((s8[16220160]{0:T(1024)(128)(4,1)}), s8[4194304]{0:T(1024)(128)(4,1)S(1)}, s32[]{:S(2)}) async-start(s8[16220160]{0:T(1024)(128)(4,1)} %bitcast.249), calls=%async_computation.2 | async-start | bytes 8388608
  89.0 5.7 %slice-start.1 = ((s8[16220160]{0:T(1024)(128)(4,1)}), s8[4194304]{0:T(1024)(128)(4,1)S(1)}, s32[]{:S(2)}) async-start(s8[16220160]{0:T(1024)(128)(4,1)} %bitcast.249), calls=%async_computation.3 | async-start | bytes 8388608
  90.4 4.3 %slice-start.2 = ((s8[16220160]{0:T(1024)(128)(4,1)}), s8[4194304]{0:T(1024)(128)(4,1)S(1)}, s32[]{:S(2)}) async-start(s8[16220160]{0:T(1024)(128)(4,1)} %bitcast.249), calls=%async_computation.4 | async-start | bytes 8388608
  91.8 3.2 %slice-start.3 = ((s8[16220160]{0:T(1024)(128)(4,1)}), s8[3637248]{0:T(1024)(128)(4,1)S(1)}, s32[]{:S(2)}) async-start(s8[16220160]{0:T(1024)(128)(4,1)} %bitcast.249), calls=%async_computation.5 | async-start | bytes 7274496
where the time goes:
time: 187 us; the launch traced here: 183 us
  matrix products  58.3 us (31%)
  blocking collectives  36.3 us (19%)
  local copies, waits for them, and re-layouts  35.3 us (19%)
  starting transfers between devices  24.7 us (13%)
  other arithmetic  21 us (11%)
  waiting for transfers between devices  6.9 us (4%)
    dot_general x1, matrix products, on_device(): jnp.einsum('kti,txrin->xrkn', galerkin_cube, stacked, precision=lax.Preci...  40.6 us
    all_to_all x1, blocking collectives, on_device(): lax.all_to_all(coupled, 'mode', split_axis=0, concat_axis=2, tiled=True)  36.3 us
    dot_general x1, matrix products, coupling_matrix(): lax.dot_general(target, scaled, (((0,), (0,)), ((), ())), preferred_eleme...  17.7 us
    reshape x1, local copies, waits for them, and re-layouts, on_device(): galerkin_cube = galerkin.reshape(MODES, term_count, MODES)  14.9 us
    unnamed x9, other arithmetic  11.7 us
    all_to_all x1, starting transfers between devices, on_device(): lax.all_to_all(field, 'mode', split_axis=2, concat_axis=0, tiled=True)  8.04 us
    ppermute x2, starting transfers between devices, extended(): lax.ppermute(last, axis, up)  7.82 us
    scatter x1, local copies, waits for them, and re-layouts, on_device(): jnp.zeros((MODES + 1,), jnp.int32).at[slot_mode].set(all_slots)[:MODES]  4.48 us
  transfers between devices with their start and end apart: 7, of which 2 were waited for; matrix products, arithmetic and copies ran while one was open for 24% of the time, Pallas kernels for 0%

commit v1 on v0

v1 whole, which is shorter than its diff:
```python
import jax
import jax.numpy as jnp
from jax import lax
from jax.experimental import pallas as pl
from jax.experimental.pallas import tpu as pltpu
from jax.sharding import PartitionSpec as P

MODES = 495
HELD = 512
TERMS = 9
ROWS = 4 * HELD
LANES = 8
MESH = pl.DeviceIdType.MESH
VMEM = pl.BlockSpec(memory_space=pltpu.VMEM)
SMEM = pl.BlockSpec(memory_space=pltpu.SMEM)
LIMIT = 60 * 1024 * 1024


def shape_of(shape, dtype):
    return jax.ShapeDtypeStruct(shape, dtype)


def greet(count):
    slab, me = lax.axis_index("slab"), lax.axis_index("mode")
    barrier = pltpu.get_barrier_semaphore()

    def tell(step, carry):
        peer = lax.rem(me + step, count)
        pl.semaphore_signal(barrier, inc=1, device_id=(slab, peer), device_id_type=MESH)
        return carry

    lax.fori_loop(1, count, tell, 0)
    pl.semaphore_wait(barrier, count - 1)


def gather_kernel(count, inverse, blocks, held, planes, raw, wide, wide_planes, own_sem, send_sem, recv_sem):
    slab, me = lax.axis_index("slab"), lax.axis_index("mode")
    slots = blocks.shape[1]
    greet(count)

    def copy_to(step):
        peer = lax.rem(me + step, count)
        return pltpu.make_async_remote_copy(
            src_ref=blocks.at[peer],
            dst_ref=raw.at[pl.ds(me * slots, slots)],
            send_sem=send_sem.at[step],
            recv_sem=recv_sem.at[step],
            device_id=(slab, peer),
            device_id_type=MESH,
        )

    def start(step, carry):
        copy_to(step).start()
        return carry

    lax.fori_loop(1, count, start, 0)
    own = pltpu.make_async_copy(blocks.at[me], raw.at[pl.ds(me * slots, slots)], own_sem)
    own.start()
    own.wait()

    def finish(step, carry):
        copy_to(step).wait()
        return carry

    lax.fori_loop(1, count, finish, 0)

    def pick(step, carry):
        for part in range(8):
            mode = step * 8 + part
            value = raw[inverse[mode]].astype(jnp.float32)
            wide[pl.ds(pl.multiple_of(4 * mode, 4), 4), :] = value
            wide_planes[0, pl.ds(pl.multiple_of(2 * mode, 2), 2), :] = value[0:2]
            wide_planes[1, pl.ds(pl.multiple_of(2 * mode, 2), 2), :] = value[2:4]
        return carry

    lax.fori_loop(0, HELD // 8, pick, 0)

    def narrow(step, carry):
        at = pl.ds(pl.multiple_of(step * 64, 64), 64)
        held[at, :] = wide[at, :].astype(jnp.bfloat16)
        return carry

    lax.fori_loop(0, ROWS // 64, narrow, 0)

    def narrow_planes(step, carry):
        at = pl.ds(pl.multiple_of(step * 64, 64), 64)
        planes[0, at, :] = wide_planes[0, at, :].astype(jnp.bfloat16)
        planes[1, at, :] = wide_planes[1, at, :].astype(jnp.bfloat16)
        return carry

    lax.fori_loop(0, ROWS // 128, narrow_planes, 0)


def halo_kernel(slabs, count, held, planes, coef, row_low, row_high, plane_low, plane_high, coef_low, coef_high, send_sem, recv_sem):
    slab, me = lax.axis_index("slab"), lax.axis_index("mode")
    above = (slab, lax.rem(me + 1, count))
    below = (slab, lax.rem(me + count - 1, count))
    right = (lax.rem(slab + 1, slabs), me)
    left = (lax.rem(slab + slabs - 1, slabs), me)
    barrier = pltpu.get_barrier_semaphore()
    for peer in (above, below, right, left):
        pl.semaphore_signal(barrier, inc=1, device_id=peer, device_id_type=MESH)
    pl.semaphore_wait(barrier, 4)
    copies = []
    for place, (source, target, peer) in enumerate(
        (
            (held, row_low, above),
            (held, row_high, below),
            (planes.at[1], plane_low, right),
            (planes.at[0], plane_high, left),
            (coef.at[1], coef_low, right),
            (coef.at[1], coef_high, left),
        )
    ):
        copy = pltpu.make_async_remote_copy(
            src_ref=source,
            dst_ref=target,
            send_sem=send_sem.at[place],
            recv_sem=recv_sem.at[place],
            device_id=peer,
            device_id_type=MESH,
        )
        copy.start()
        copies.append(copy)
    for copy in copies:
        copy.wait()


def neighbours(centre, plane, sub, lane):
    front = lax.rem(sub, 4) < 2
    second = lax.rem(sub, 2) == 1
    zero = jnp.zeros_like(centre)
    plane_low = jnp.where(front, plane, pltpu.roll(centre, 2, 0))
    plane_high = jnp.where(front, pltpu.roll(centre, 6, 0), plane)
    low = pltpu.roll(centre, 1, 1)
    high = pltpu.roll(centre, 127, 1)
    column_low = jnp.where(lane == 0, jnp.where(second, pltpu.roll(low, 1, 0), zero), low)
    column_high = jnp.where(lane == 127, jnp.where(second, zero, pltpu.roll(high, 7, 0)), high)
    return plane_low, plane_high, column_low, column_high


def apply_kernel(slabs, count, address, weight, slot_mode, held, row_low, row_high, plane_low, plane_high, coef, coef_low, coef_high, coded, scales, faces, plane_rows, image, *sums_and_picked):
    sums, picked = sums_and_picked[:LANES], sums_and_picked[LANES]
    slab, me = lax.axis_index("slab"), lax.axis_index("mode")
    sub = lax.broadcasted_iota(jnp.int32, (8, 128), 0)
    lane = lax.broadcasted_iota(jnp.int32, (8, 128), 1)
    front = lax.rem(sub, 4) < 2
    has_left = (slab > 0).astype(jnp.float32)
    has_right = (slab < slabs - 1).astype(jnp.float32)
    mask_plane = jnp.where(front, has_left, has_right)
    mask_low = (me > 0).astype(jnp.float32)
    mask_high = (me < count - 1).astype(jnp.float32)

    for term in range(TERMS):
        own = coef[1, term]
        outer = jnp.where(front, pltpu.roll(coef_low[term], 6, 0), pltpu.roll(coef_high[term], 2, 0)) * mask_plane
        around = neighbours(own, outer, sub, lane)
        around = around + (coef[0, term] * mask_low, coef[2, term] * mask_high)
        for place, other in enumerate(around):
            faces[6 * term + place] = 0.5 * (own + other)

    def interleave(step, carry):
        at = pl.ds(pl.multiple_of(step * 16, 16), 16)
        low = plane_low[at, :].astype(jnp.float32)
        high = plane_high[at, :].astype(jnp.float32)
        for part in range(8):
            base = pl.multiple_of(step * 32 + 4 * part, 4)
            plane_rows[pl.ds(base, 2), :] = low[2 * part : 2 * part + 2]
            plane_rows[pl.ds(base + 2, 2), :] = high[2 * part : 2 * part + 2]
        return carry

    lax.fori_loop(0, ROWS // 32, interleave, 0)

    def stencil(step, carry):
        at = pl.ds(pl.multiple_of(step * 16, 16), 16)
        centre = held[at, :].astype(jnp.float32)
        low = row_low[at, :].astype(jnp.float32)
        high = row_high[at, :].astype(jnp.float32)
        halves = []
        for half in range(2):
            part = slice(8 * half, 8 * half + 8)
            base = pl.multiple_of(step * 16 + 8 * half, 8)
            own = centre[part]
            outer = plane_rows[pl.ds(base, 8), :] * mask_plane
            around = neighbours(own, outer, sub, lane)
            around = around + (low[part] * mask_low, high[part] * mask_high)
            halves.append((base, [own - other for other in around]))
        for term in range(TERMS):
            face = [faces[6 * term + place] for place in range(6)]
            for base, drops in halves:
                total = face[0] * drops[0]
                for place in range(1, 6):
                    total = total + face[place] * drops[place]
                if term == 0:
                    sums[0][pl.ds(base, 8), :] = total
                else:
                    image[pl.ds(pl.multiple_of((term - 1) * ROWS + base, 8), 8), :] = total
        return carry

    lax.fori_loop(0, ROWS // 16, stencil, 0)

    def clear(step, carry):
        at = pl.ds(pl.multiple_of(step * 32, 32), 32)
        for total in sums[1:]:
            total[at, :] = jnp.zeros((32, 128), jnp.float32)
        return carry

    lax.fori_loop(0, ROWS // 32, clear, 0)

    def couple(step, carry):
        for part in range(LANES):
            place = step * LANES + part
            both = address[place]
            source = pl.ds(pl.multiple_of(lax.bitwise_and(both, 0xFFFF), 4), 4)
            target = pl.ds(pl.multiple_of(lax.shift_right_logical(both, 16), 4), 4)
            sums[part][target, :] = sums[part][target, :] + weight[place] * image[source, :]
        return carry

    lax.fori_loop(0, address.shape[0] // LANES, couple, 0)

    def join(step, carry):
        at = pl.ds(pl.multiple_of(step * 16, 16), 16)
        total = sums[0][at, :]
        for other in sums[1:]:
            total = total + other[at, :]
        sums[0][at, :] = total
        return carry

    lax.fori_loop(0, ROWS // 16, join, 0)
    sums[0][4 * MODES : 4 * MODES + 4, :] = jnp.zeros((4, 128), jnp.float32)

    def pick(step, carry):
        for part in range(8):
            slot = step * 8 + part
            source = pl.ds(pl.multiple_of(4 * slot_mode[slot], 4), 4)
            picked[pl.ds(pl.multiple_of(4 * slot, 4), 4), :] = sums[0][source, :]
        return carry

    lax.fori_loop(0, slot_mode.shape[0] // 8, pick, 0)

    sub16 = lax.broadcasted_iota(jnp.int32, (16, 128), 0)
    lane16 = lax.broadcasted_iota(jnp.int32, (16, 128), 1)

    def encode(group, carry):
        row = jnp.zeros((1, 128), jnp.float32)
        for part in range(8):
            at = pl.ds(pl.multiple_of(group * 128 + part * 16, 16), 16)
            value = picked[at, :]
            largest = jnp.max(jnp.abs(value), axis=1, keepdims=True)
            factor = jnp.where(largest > 0, 1.0 / jnp.where(largest > 0, largest, 1.0), 0.0)
            code = jnp.round((value * factor) * 32767.0).astype(jnp.int32)
            coded[at, :] = code.astype(jnp.int16)
            spread = jnp.where(lane16 == sub16 + 16 * part, largest * (1.0 / 32767.0), 0.0)
            row = row + jnp.sum(spread, axis=0, keepdims=True)
        scales[group] = row
        return carry

    lax.fori_loop(0, count, encode, 0)


def return_kernel(count, coded, scales, got, got_scales, own_sem, send_sem, recv_sem):
    slab, me = lax.axis_index("slab"), lax.axis_index("mode")
    greet(count)

    def copies_to(step):
        peer = lax.rem(me + step, count)
        return [
            pltpu.make_async_remote_copy(
                src_ref=source.at[peer],
                dst_ref=target.at[me],
                send_sem=send_sem.at[place, step],
                recv_sem=recv_sem.at[place, step],
                device_id=(slab, peer),
                device_id_type=MESH,
            )
            for place, (source, target) in enumerate(((coded, got), (scales, got_scales)))
        ]

    def start(step, carry):
        for copy in copies_to(step):
            copy.start()
        return carry

    lax.fori_loop(1, count, start, 0)
    own = [
        pltpu.make_async_copy(coded.at[me], got.at[me], own_sem.at[0]),
        pltpu.make_async_copy(scales.at[me], got_scales.at[me], own_sem.at[1]),
    ]
    for copy in own:
        copy.start()
    for copy in own:
        copy.wait()

    def finish(step, carry):
        for copy in copies_to(step):
            copy.wait()
        return carry

    lax.fori_loop(1, count, finish, 0)


def decode_kernel(got, got_scales, out, wide, scale):
    block = pl.program_id(0)
    count, rows = got.shape[0], got.shape[1]
    for source in range(count):
        scale[source : source + 1, :] = got_scales[source]

    def widen(source, carry):
        at = pl.ds(pl.multiple_of(source * rows, rows), rows)
        wide[at, :] = got[source].astype(jnp.int32).astype(jnp.float32)
        return carry

    lax.fori_loop(0, count, widen, 0)
    factors = pltpu.roll(scale[...], lax.rem(128 - block * rows, 128), 1)
    for place in range(rows):
        slot, plane, half = place // 4, (place // 2) % 2, place % 2
        value = wide[pl.ds(place, count, stride=rows), :]
        out[slot, plane, :, 128 * half : 128 * half + 128] = value * factors[:, place : place + 1]


def on_device(field, coefficient, slot_mode, couplings):
    slabs, count = lax.axis_size("slab"), lax.axis_size("mode")
    row = lax.axis_index("mode")
    slots, planes_here, rows_all, columns = field.shape
    f32, bf16, i16 = jnp.float32, jnp.bfloat16, jnp.int16
    dma = pltpu.SemaphoreType.DMA

    blocks = field.reshape(slots, planes_here, rows_all, 2, 128).transpose(2, 0, 1, 3, 4)
    blocks = blocks.reshape(rows_all, slots, 4, 128)
    mode_ids = jnp.arange(HELD, dtype=jnp.int32)
    slot_ids = jnp.arange(slots * count, dtype=jnp.int32)
    inverse = jnp.sum(jnp.where(slot_mode[None, :] == mode_ids[:, None], slot_ids[None, :], 0), axis=1)
    inverse = jnp.where(mode_ids < MODES, inverse, 0).astype(jnp.int32)
    near = jnp.stack([lax.dynamic_slice_in_dim(coefficient, row + shift, 1, 2) for shift in (-1, 0, 1)])
    near = near.reshape(3, TERMS, 4, 128)
    near = jnp.concatenate([near, near], axis=2)
    source = (couplings[:, 2] - 1) * ROWS + couplings[:, 1] * 4
    address = source + couplings[:, 0] * (4 << 16)
    weight = couplings[:, 3].astype(f32) * 0.125

    held, planes = pl.pallas_call(
        lambda *refs: gather_kernel(count, *refs),
        out_shape=(shape_of((ROWS, 128), bf16), shape_of((2, ROWS // 2, 128), bf16)),
        in_specs=[SMEM, VMEM],
        out_specs=(VMEM, VMEM),
        scratch_shapes=[
            pltpu.VMEM((slots * count, 4, 128), bf16),
            pltpu.VMEM((ROWS, 128), f32),
            pltpu.VMEM((2, ROWS // 2, 128), f32),
            dma,
            dma((count,)),
            dma((count,)),
        ],
        compiler_params=pltpu.CompilerParams(collective_id=0, has_side_effects=True, vmem_limit_bytes=LIMIT),
        name="gather",
    )(inverse, blocks)

    row_low, row_high, plane_low, plane_high, coef_low, coef_high = pl.pallas_call(
        lambda *refs: halo_kernel(slabs, count, *refs),
        out_shape=(
            shape_of((ROWS, 128), bf16),
            shape_of((ROWS, 128), bf16),
            shape_of((ROWS // 2, 128), bf16),
            shape_of((ROWS // 2, 128), bf16),
            shape_of((TERMS, 8, 128), f32),
            shape_of((TERMS, 8, 128), f32),
        ),
        in_specs=[VMEM] * 3,
        out_specs=(VMEM,) * 6,
        scratch_shapes=[dma((6,)), dma((6,))],
        compiler_params=pltpu.CompilerParams(collective_id=1, has_side_effects=True, vmem_limit_bytes=LIMIT),
        name="halo",
    )(held, planes, near)

    coded, scales = pl.pallas_call(
        lambda *refs: apply_kernel(slabs, count, *refs),
        out_shape=(shape_of((slots * count * 4, 128), i16), shape_of((count, 1, 128), f32)),
        in_specs=[SMEM] * 3 + [VMEM] * 8,
        out_specs=(VMEM, VMEM),
        scratch_shapes=[
            pltpu.VMEM((6 * TERMS, 8, 128), f32),
            pltpu.VMEM((ROWS, 128), f32),
            pltpu.VMEM(((TERMS - 1) * ROWS, 128), f32),
        ]
        + [pltpu.VMEM((ROWS, 128), f32)] * LANES
        + [pltpu.VMEM((slots * count * 4, 128), f32)],
        compiler_params=pltpu.CompilerParams(vmem_limit_bytes=LIMIT),
        name="apply",
    )(address, weight, slot_mode, held, row_low, row_high, plane_low, plane_high, near, coef_low, coef_high)

    got, got_scales = pl.pallas_call(
        lambda *refs: return_kernel(count, *refs),
        out_shape=(shape_of((count, slots * 4, 128), i16), shape_of((count, 1, 128), f32)),
        in_specs=[VMEM] * 2,
        out_specs=(VMEM, VMEM),
        scratch_shapes=[dma((2,)), dma((2, count)), dma((2, count))],
        compiler_params=pltpu.CompilerParams(collective_id=2, has_side_effects=True, vmem_limit_bytes=LIMIT),
        name="give",
    )(coded.reshape(count, slots * 4, 128), scales)

    step = 8
    return pl.pallas_call(
        decode_kernel,
        out_shape=shape_of((slots, planes_here, rows_all, columns), f32),
        grid=(slots // step,),
        in_specs=[
            pl.BlockSpec((count, 4 * step, 128), lambda i: (0, i, 0)),
            pl.BlockSpec((count, 1, 128), lambda i: (0, 0, 0)),
        ],
        out_specs=pl.BlockSpec((step, planes_here, rows_all, columns), lambda i: (i, 0, 0, 0)),
        scratch_shapes=[pltpu.VMEM((count * 4 * step, 128), f32), pltpu.VMEM((count, 128), f32)],
        compiler_params=pltpu.CompilerParams(vmem_limit_bytes=LIMIT),
        name="decode",
    )(got, got_scales)


def solution(mesh):
    in_specs = (P("mode", "slab", None, None), P(None, "slab", None, None), P(), P())
    return jax.shard_map(
        on_device,
        mesh=mesh,
        in_specs=in_specs,
        out_specs=P("mode", "slab", None, None),
        check_vma=False,
    )
```

time: 187 us -> 111 us (0.59)
  Pallas kernels: 0 us -> 99.3 us
  matrix products: 58.3 us -> 0 us
  blocking collectives: 36.3 us -> 0 us
  local copies, waits for them, and re-layouts: 35.3 us -> 4.54 us
  starting transfers between devices: 24.7 us -> 0 us
  other arithmetic: 21 us -> 5.2 us
  waiting for transfers between devices: 6.9 us -> 0 us
    pallas_call x0 -> x5, Pallas kernels: none -> 99.3 us  [the longest x1 29.4 us: on_device(): pl.pallas_call(lambda *refs: apply_kernel(slabs, count, *refs), out_shape...]
    dot_general x2 -> x0, matrix products: 58.3 us -> none  [the longest x1 40.6 us: on_device(): jnp.einsum('kti,txrin->xrkn', galerkin_cube, stacked, precision=lax.Preci...]
    all_to_all x1 -> x0, blocking collectives: 36.3 us -> none  [on_device(): lax.all_to_all(coupled, 'mode', split_axis=0, concat_axis=2, tiled=True)]
    ppermute x6 -> x0, starting transfers between devices: 16.7 us -> none  [the longest x2 7.82 us: extended(): lax.ppermute(last, axis, up)]
    unnamed x9 -> x0, other arithmetic: 11.7 us -> none
    reshape x1 -> x2, local copies, waits for them, and re-layouts: 14.9 us -> 3.42 us  [on_device(): field.reshape(slots, planes_here, rows_all, 2, 128).transpose(2, 0, 1, 3, 4)]
    all_to_all x1 -> x0, starting transfers between devices: 8.04 us -> none  [on_device(): lax.all_to_all(field, 'mode', split_axis=2, concat_axis=0, tiled=True)]
    gather x2 -> x0, local copies, waits for them, and re-layouts: 6.92 us -> none  [the longest x1 4.13 us: on_device(): coupled = jnp.take(coupled, slot_mode, axis=2).transpose(2, 0, 1, 3)]
  transfers between devices with their start and end apart: 7 -> 0, of which waited for: 2 -> 0; matrix products, arithmetic and copies ran while one was open for 24% -> 0% of each run, Pallas kernels for 0% -> 0%
where the time goes in v1:
time: 111 us; the launch traced here: 109 us
  Pallas kernels  99.3 us (89%)
  other arithmetic  5.2 us (5%)
  local copies, waits for them, and re-layouts  4.54 us (4%)
    pallas_call x1, Pallas kernels, on_device(): pl.pallas_call(lambda *refs: apply_kernel(slabs, count, *refs), out_shape...  29.4 us
    pallas_call x1, Pallas kernels, on_device(): pl.pallas_call(lambda *refs: return_kernel(count, *refs), out_shape=(shap...  25.3 us
    pallas_call x1, Pallas kernels, on_device(): pl.pallas_call(lambda *refs: gather_kernel(count, *refs), out_shape=(shap...  24.4 us
    pallas_call x1, Pallas kernels, on_device(): pl.pallas_call(lambda *refs: halo_kernel(slabs, count, *refs), out_shape=...  15.3 us
    pallas_call x1, Pallas kernels, on_device(): pl.pallas_call(decode_kernel, out_shape=shape_of((slots, planes_here, row...  4.81 us
    reshape x2, local copies, waits for them, and re-layouts, on_device(): field.reshape(slots, planes_here, rows_all, 2, 128).transpose(2, 0, 1, 3, 4)  3.42 us

profile of v1, /device:TPU:1, one launch (start us, length us, event | category | flops | bytes accessed | tf_op | source)
XLA Modules:
  0.0 109.1 jit_solution(14622437980604916055)
XLA Ops:
  0.0 1.0 select_reduce_fusion
  1.0 0.6 fusion.refs_0_
  1.6 1.4 %multiply_reduce_fusion.refs_1_ = f32[2640]{0:T(1024)} fusion(s32[2640,4]{0,1:T(4,128)} %param.7), kind=kLoop, calls=%fused_computation.3 | loop fusion | flops 5280 | bytes 21120 | tf_op jit(solution)/shard_map/mul | solution.py:339
  3.0 1.5 %add_reduce_fusion.refs_0_ = s32[2640]{0:T(1024)} fusion(s32[2640,4]{0,1:T(4,128)} %param.7), kind=kLoop, calls=%fused_computation.4 | loop fusion | flops 15840 | bytes 42240 | tf_op jit(solution)/shard_map/add | solution.py:338
  4.5 1.1 %constant_dynamic-slice_fusion.2 = (f32[9,2,1,256]{3,2,1,0:T(1,128)S(1)}, f32[9,2,1,256]{3,2,1,0:T(1,128)S(1)}, f32[9,2,1,256]{3,2,1,0:T(1,128)S(1)}) fusion(f32[9,2,32,256]{3,2,1,0:T(8,128)} %param.5, s32[]{:T(128)S(6)} %select_n.19, s32[]{:T(128)S(6)} %select_n.21, s32[]{:T(128)S(6)} %select_n.20), kind=kLoop, calls=%fused_computation.9 | loop fusion | bytes 110604 | tf_op jit(solution)/shard_map/dynamic_slice | solution.py:334
  5.7 0.7 maximum_maximum_fusion.refs_2_.refs_8_
  6.3 1.3 %reshape.30 = bf16[32,2,32,2,128]{4,3,2,1,0:T(2,128)(2,1)S(1)} reshape(bf16[32,2,32,256]{3,2,1,0:T(8,128)(2,1)} %param.4) | data formatting | bytes 2097152 | tf_op jit(solution)/shard_map/reshape | solution.py:328
  7.7 2.1 %copy.6 = bf16[32,2,32,2,128]{4,3,1,0,2:T(2,128)(2,1)} copy(bf16[32,2,32,2,128]{4,3,2,1,0:T(2,128)(2,1)S(1)} %reshape.30) | data formatting | bytes 2097152 | tf_op jit(solution)/shard_map/reshape | solution.py:328
  9.8 24.4 %gather.1 = (bf16[2048,128]{1,0:T(8,128)(2,1)}, bf16[2,1024,128]{2,1,0:T(8,128)(2,1)}) custom-call(s32[512]{0:T(512)} %fusion.refs_0_, bf16[32,32,4,128]{3,2,1,0:T(4,128)(2,1)} %bitcast.9), custom_call_target="tpu_custom_call" | custom-call | tf_op jit(solution)/shard_map/gather/pallas_call | solution.py:341
  34.1 15.3 %halo.1 = (bf16[2048,128]{1,0:T(8,128)(2,1)}, bf16[2048,128]{1,0:T(8,128)(2,1)}, bf16[1024,128]{1,0:T(8,128)(2,1)}, bf16[1024,128]{1,0:T(8,128)(2,1)}, f32[9,8,128]{2,1,0:T(8,128)}, /*index=5*/f32[9,8,128]{2,1,0:T(8,128)}) custom-call(bf16[2048,128]{1,0:T(8,128)(2,1)} %get-tuple-element.17.refs_0_.refs_3_, bf16[2,1024,128]{2,1,0:T(8,128)(2,1)} %get-tuple-element.18.refs_1_, ...), custom_call_target="tpu_custom_call" | custom-call | tf_op jit(solution)/shard_map/halo/pallas_call | solution.py:358
  49.5 29.4 %apply.1 = (s16[4096,128]{1,0:T(8,128)(2,1)}, f32[32,1,128]{2,1,0:T(1,128)}) custom-call(s32[2640]{0:T(1024)} %add_reduce_fusion.refs_0_, f32[2640]{0:T(1024)} %multiply_reduce_fusion.refs_1_, s32[1024]{0:T(1024)} %refs_2_.1, bf16[2048,128]{1,0:T(8,128)(2,1)} %get-tuple-element.17.refs_0_.refs_3_, bf16[2048,128]{1,0:T(8,128)(2,1)} %get-tuple-element.19.refs_4_, ...), custom_call_target="tpu_custom_call" | custom-call | tf_op jit(solution)/shard_map/apply/pallas_call | solution.py:375
  78.9 25.3 %give.1 = (s16[32,128,128]{2,1,0:T(8,128)(2,1)}, f32[32,1,128]{2,1,0:T(1,128)}) custom-call(s16[32,128,128]{2,1,0:T(8,128)(2,1)} %bitcast.10, f32[32,1,128]{2,1,0:T(1,128)} %get-tuple-element.26.refs_1_), custom_call_target="tpu_custom_call" | custom-call | tf_op jit(solution)/shard_map/give/pallas_call | solution.py:391
  104.3 4.8 %decode.1 = f32[32,2,32,256]{3,2,1,0:T(8,128)} custom-call(s16[32,128,128]{2,1,0:T(8,128)(2,1)} %get-tuple-element.27.got, f32[32,1,128]{2,1,0:T(1,128)} %get-tuple-element.28.got_scales), custom_call_target="tpu_custom_call" | custom-call | tf_op jit(solution)/shard_map/decode/pallas_call | solution.py:402

commit v2 on v1

v2 whole, which is shorter than its diff:
```python
import jax
import jax.numpy as jnp
from jax import lax
from jax.experimental import pallas as pl
from jax.experimental.pallas import tpu as pltpu
from jax.sharding import PartitionSpec as P

MODES = 495
HELD = 512
TERMS = 9
ROWS = 4 * HELD
LANES = 4
UNROLL = 16
CHUNKS = 4
TOP = 32700.0
SIDE = 4
MESH = pl.DeviceIdType.MESH
VMEM = pl.BlockSpec(memory_space=pltpu.VMEM)
SMEM = pl.BlockSpec(memory_space=pltpu.SMEM)
MIB = 1024 * 1024


def far_first():
    offsets = [(x, y, core) for x in range(SIDE) for y in range(SIDE) for core in range(2)]
    hops = lambda offset: min(offset[0], SIDE - offset[0]) + min(offset[1], SIDE - offset[1])
    return sorted(offsets[1:], key=hops, reverse=True)


OFFSETS = far_first()


def shape_of(shape, dtype):
    return jax.ShapeDtypeStruct(shape, dtype)


def moved(me, offset, sign=1):
    x, y, core = me // (2 * SIDE), (me // 2) % SIDE, me % 2
    x = lax.rem(x + (sign * offset[0]) % SIDE, SIDE)
    y = lax.rem(y + (sign * offset[1]) % SIDE, SIDE)
    return (x * SIDE + y) * 2 + lax.rem(core + offset[2], 2)


def rows_at(start, size):
    return pl.ds(pl.multiple_of(start, size), size)


def gather_kernel(
    slabs, count, slot_mode, field, coefficient, couplings,
    held, row_low, row_high, plane_low, plane_high, near, coef_low, coef_high, address, weight,
    turned, blocks, raw, wide_raw, planes, wide, wide_planes, found, inverse,
    own_sem, send_sem, recv_sem, halo_send, halo_recv,
):
    slab, me = lax.axis_index("slab"), lax.axis_index("mode")
    slots = field.shape[0]
    above = (slab, lax.rem(me + 1, count))
    below = (slab, lax.rem(me + count - 1, count))
    right = (lax.rem(slab + 1, slabs), me)
    left = (lax.rem(slab + slabs - 1, slabs), me)
    barrier = pltpu.get_barrier_semaphore()
    for offset in OFFSETS:
        pl.semaphore_signal(barrier, inc=1, device_id=(slab, moved(me, offset)), device_id_type=MESH)
    for peer in (right, left):
        pl.semaphore_signal(barrier, inc=1, device_id=peer, device_id_type=MESH)

    def turn(slot, carry):
        for part in range(4):
            plane, half = part // 2, part % 2
            value = field[slot, plane, :, 128 * half : 128 * half + 128].astype(jnp.float32)
            turned[pl.ds(4 * slot + part, count, stride=4 * slots), :] = value
        return carry

    lax.fori_loop(0, slots, turn, 0)

    def narrow_block(row, carry):
        blocks[row] = turned[rows_at(row * 4 * slots, 4 * slots), :].astype(jnp.bfloat16)
        return carry

    lax.fori_loop(0, count, narrow_block, 0)

    pl.semaphore_wait(barrier, len(OFFSETS) + 2)
    copies = []
    for place, offset in enumerate(OFFSETS):
        peer = moved(me, offset)
        copy = pltpu.make_async_remote_copy(
            src_ref=blocks.at[peer],
            dst_ref=raw.at[me],
            send_sem=send_sem.at[place],
            recv_sem=recv_sem.at[place],
            device_id=(slab, peer),
            device_id_type=MESH,
        )
        copy.start()
        copies.append(copy)
    own = pltpu.make_async_copy(blocks.at[me], raw.at[me], own_sem.at[0])
    own.start()

    ids = lax.broadcasted_iota(jnp.int32, (8, 128), 0) * 128 + lax.broadcasted_iota(jnp.int32, (8, 128), 1)

    def find(step, place):
        for part in range(8):
            slot = step * 8 + part
            place = jnp.where(ids == slot_mode[slot], slot, place)
        return place

    found[...] = lax.fori_loop(0, slots * count // 8, find, jnp.zeros((8, 128), jnp.int32))

    for shift in range(3):
        row = jnp.clip(me + shift - 1, 0, count - 1)
        for term in range(TERMS):
            for part in range(4):
                plane, half = part // 2, part % 2
                tile = coefficient[term, plane, rows_at(row // 8 * 8, 8), 128 * half : 128 * half + 128]
                value = pltpu.roll(tile, lax.rem(8 - row % 8, 8), 0)[0:1]
                near[shift, term, part : part + 1, :] = value
                near[shift, term, part + 4 : part + 5, :] = value

    listed = pltpu.make_async_copy(found, inverse, own_sem.at[1])
    listed.start()
    listed.wait()
    own.wait()

    def widen(source):
        for part in range(4):
            value = raw[source, 32 * part : 32 * part + 32, :].astype(jnp.float32)
            wide_raw[pl.ds(source * slots + 8 * part, 8)] = value.reshape(8, 4, 128)

    widen(me)
    for copy, offset in zip(copies, OFFSETS):
        copy.wait()
        widen(moved(me, offset, -1))

    modes = HELD // CHUNKS

    def pick(step, carry):
        for part in range(8):
            mode = step * 8 + part
            source = inverse[mode // 128, mode % 128]
            value = wide_raw[source]
            wide[rows_at(4 * mode, 4), :] = value
            wide_planes[0, rows_at(2 * mode, 2), :] = value[0:2]
            wide_planes[1, rows_at(2 * mode, 2), :] = value[2:4]
        return carry

    def narrow(step, carry):
        at = rows_at(step * 64, 64)
        held[at, :] = wide[at, :].astype(jnp.bfloat16)
        at = rows_at(step * 32, 32)
        planes[0, at, :] = wide_planes[0, at, :].astype(jnp.bfloat16)
        planes[1, at, :] = wide_planes[1, at, :].astype(jnp.bfloat16)
        return carry

    sent = []

    def send(place, source, target, peer):
        copy = pltpu.make_async_remote_copy(
            src_ref=source,
            dst_ref=target,
            send_sem=halo_send.at[place],
            recv_sem=halo_recv.at[place],
            device_id=peer,
            device_id_type=MESH,
        )
        copy.start()
        sent.append(copy)

    def send_chunk(chunk):
        at, half = pl.ds(chunk * 4 * modes, 4 * modes), pl.ds(chunk * 2 * modes, 2 * modes)
        send(4 * chunk, held.at[at], row_low.at[at], above)
        send(4 * chunk + 1, held.at[at], row_high.at[at], below)
        send(4 * chunk + 2, planes.at[1, half], plane_low.at[half], right)
        send(4 * chunk + 3, planes.at[0, half], plane_high.at[half], left)

    for chunk in range(CHUNKS):
        lax.fori_loop(chunk * modes // 8, (chunk + 1) * modes // 8, pick, 0)
        lax.fori_loop(chunk * modes // 16, (chunk + 1) * modes // 16, narrow, 0)
        if chunk:
            send_chunk(chunk - 1)
    send(4 * CHUNKS, near.at[1], coef_low, right)
    send(4 * CHUNKS + 1, near.at[1], coef_high, left)
    source = (couplings[2:3, :] - 1) * ROWS + couplings[1:2, :] * 4
    address[...] = source + couplings[0:1, :] * (4 << 16)
    weight[...] = couplings[3:4, :].astype(jnp.float32) * 0.125
    send_chunk(CHUNKS - 1)
    for copy in sent:
        copy.wait()


def plane_neighbours(centre, plane, front):
    return (
        jnp.where(front, plane, pltpu.roll(centre, 2, 0)),
        jnp.where(front, pltpu.roll(centre, 6, 0), plane),
    )


def column_neighbours(centre, second, lane):
    zero = jnp.zeros_like(centre)
    low = pltpu.roll(centre, 1, 1)
    high = pltpu.roll(centre, 127, 1)
    return (
        jnp.where(lane == 0, jnp.where(second, pltpu.roll(low, 1, 0), zero), low),
        jnp.where(lane == 127, jnp.where(second, zero, pltpu.roll(high, 7, 0)), high),
    )


def apply_kernel(
    slabs, count, address, weight, held, row_low, row_high, plane_low, plane_high, near, coef_low, coef_high,
    out, faces, plane_rows, column_low, column_high, image, *sums,
):
    slab, me = lax.axis_index("slab"), lax.axis_index("mode")
    sub = lax.broadcasted_iota(jnp.int32, (8, 128), 0)
    lane = lax.broadcasted_iota(jnp.int32, (8, 128), 1)
    front = lax.rem(sub, 4) < 2
    second = lax.rem(sub, 2) == 1
    has_left = (slab > 0).astype(jnp.float32)
    has_right = (slab < slabs - 1).astype(jnp.float32)
    mask_plane = jnp.where(front, has_left, has_right)
    mask_low = (me > 0).astype(jnp.float32)
    mask_high = (me < count - 1).astype(jnp.float32)

    for term in range(TERMS):
        own = near[1, term]
        outer = jnp.where(front, pltpu.roll(coef_low[term], 6, 0), pltpu.roll(coef_high[term], 2, 0)) * mask_plane
        around = plane_neighbours(own, outer, front) + column_neighbours(own, second, lane)
        around = around + (near[0, term] * mask_low, near[2, term] * mask_high)
        for place, other in enumerate(around):
            faces[6 * term + place] = 0.5 * (own + other)

    def interleave(step, carry):
        at = rows_at(step * 16, 16)
        low = plane_low[at, :].astype(jnp.float32) * has_left
        high = plane_high[at, :].astype(jnp.float32) * has_right
        for part in range(8):
            base = pl.multiple_of(step * 32 + 4 * part, 4)
            plane_rows[pl.ds(base, 2), :] = low[2 * part : 2 * part + 2]
            plane_rows[pl.ds(base + 2, 2), :] = high[2 * part : 2 * part + 2]
        return carry

    lax.fori_loop(0, ROWS // 32, interleave, 0)

    def shift(step, carry):
        value = held[rows_at(step * 128, 128), :].astype(jnp.float32)
        around = [column_neighbours(value[8 * part : 8 * part + 8], second, lane) for part in range(16)]
        for part, (low, high) in enumerate(around):
            at = rows_at(step * 128 + 8 * part, 8)
            column_low[at, :] = low
            column_high[at, :] = high
        return carry

    lax.fori_loop(0, ROWS // 128, shift, 0)

    def stencil(step, carry):
        at = rows_at(step * 16, 16)
        centre = held[at, :].astype(jnp.float32)
        low = row_low[at, :].astype(jnp.float32)
        high = row_high[at, :].astype(jnp.float32)
        halves = []
        for half in range(2):
            part = slice(8 * half, 8 * half + 8)
            base = pl.multiple_of(step * 16 + 8 * half, 8)
            at = pl.ds(base, 8)
            own = centre[part]
            around = plane_neighbours(own, plane_rows[at, :], front) + (column_low[at, :], column_high[at, :])
            around = around + (low[part] * mask_low, high[part] * mask_high)
            halves.append((base, [own - other for other in around]))
        for term in range(TERMS):
            face = [faces[6 * term + place] for place in range(6)]
            for base, drops in halves:
                total = face[0] * drops[0]
                for place in range(1, 6):
                    total = total + face[place] * drops[place]
                if term == 0:
                    sums[0][pl.ds(base, 8), :] = total
                else:
                    image[rows_at((term - 1) * ROWS + base, 8), :] = total
        return carry

    lax.fori_loop(0, ROWS // 16, stencil, 0)

    def clear(step, carry):
        at = rows_at(step * 32, 32)
        for total in sums[1:]:
            total[at, :] = jnp.zeros((32, 128), jnp.float32)
        return carry

    lax.fori_loop(0, ROWS // 32, clear, 0)

    def couple(step, carry):
        for part in range(UNROLL):
            place = step * UNROLL + part
            both = address[0, place]
            source = pl.ds(pl.multiple_of(lax.bitwise_and(both, 0xFFFF), 4), 4)
            target = pl.ds(pl.multiple_of(lax.shift_right_logical(both, 16), 4), 4)
            total = sums[part % LANES]
            total[target, :] = total[target, :] + weight[0, place] * image[source, :]
        return carry

    lax.fori_loop(0, address.shape[1] // UNROLL, couple, 0)

    def join(step, carry):
        at = rows_at(step * 32, 32)
        total = sums[0][at, :]
        for other in sums[1:]:
            total = total + other[at, :]
        out[pl.ds(8 * step, 8)] = total.reshape(8, 4, 128)
        return carry

    lax.fori_loop(0, ROWS // 32, join, 0)
    out[MODES] = jnp.zeros((4, 128), jnp.float32)


def return_kernel(count, slot_mode, image, got, got_scales, picked, factors, coded, scales, own_sem, send_sem, recv_sem):
    slab, me = lax.axis_index("slab"), lax.axis_index("mode")
    slots = slot_mode.shape[0] // count
    barrier = pltpu.get_barrier_semaphore()
    for offset in OFFSETS:
        pl.semaphore_signal(barrier, inc=1, device_id=(slab, moved(me, offset)), device_id_type=MESH)

    def pick(group, carry):
        tops = [jnp.zeros((4, 128), jnp.float32)] * 4
        for part in range(slots):
            slot = group * slots + part
            value = image[slot_mode[slot]]
            picked[rows_at(4 * slot, 4), :] = value
            tops[part % 4] = jnp.maximum(tops[part % 4], jnp.abs(value))
        factors[group] = jnp.maximum(jnp.maximum(tops[0], tops[1]), jnp.maximum(tops[2], tops[3]))
        return carry

    lax.fori_loop(0, count, pick, 0)

    def measure(step, carry):
        for part in range(8):
            group = step * 8 + part
            top = jnp.max(jnp.max(factors[group], axis=0, keepdims=True), axis=1, keepdims=True)
            top = jnp.broadcast_to(top, (1, 128))
            scales[group] = top * (1.0 / (TOP * TOP))
            factors[group] = jnp.broadcast_to(TOP * lax.rsqrt(jnp.maximum(top, 1e-37)), (4, 128))
        return carry

    lax.fori_loop(0, count // 8, measure, 0)

    def encode(group):
        factor = factors[group][0:1]

        def part_of(part, carry):
            value = picked[rows_at(group * 4 * slots + part * 32, 32), :]
            root = value * lax.rsqrt(jnp.maximum(jnp.abs(value), 1e-37))
            code = jnp.round(root * factor).astype(jnp.int32)
            coded[group, rows_at(part * 32, 32), :] = code.astype(jnp.int16)
            return carry

        lax.fori_loop(0, 4 * slots // 32, part_of, 0)

    copies = []

    def send(place):
        peer = moved(me, OFFSETS[place])
        for kind, (source, target) in enumerate(((coded, got), (scales, got_scales))):
            copy = pltpu.make_async_remote_copy(
                src_ref=source.at[peer],
                dst_ref=target.at[me],
                send_sem=send_sem.at[kind, place],
                recv_sem=recv_sem.at[kind, place],
                device_id=(slab, peer),
                device_id_type=MESH,
            )
            copy.start()
            copies.append(copy)

    encode(moved(me, OFFSETS[0]))
    pl.semaphore_wait(barrier, len(OFFSETS))
    for place in range(1, len(OFFSETS)):
        encode(moved(me, OFFSETS[place]))
        send(place - 1)
    encode(me)
    send(len(OFFSETS) - 1)
    own = [
        pltpu.make_async_copy(coded.at[me], got.at[me], own_sem.at[0]),
        pltpu.make_async_copy(scales.at[me], got_scales.at[me], own_sem.at[1]),
    ]
    for copy in own:
        copy.start()
    for copy in own + copies:
        copy.wait()


def decode_kernel(got, got_scales, out, wide, scale):
    count, rows = got.shape[0], got.shape[1]
    for source in range(count):
        scale[source : source + 1, :] = got_scales[source]

    def widen(source, carry):
        at = rows_at(source * rows, rows)
        wide[at, :] = got[source].astype(jnp.int32).astype(jnp.float32)
        return carry

    lax.fori_loop(0, count, widen, 0)
    factor = scale[...]
    for place in range(rows):
        slot, plane, half = place // 4, (place // 2) % 2, place % 2
        value = wide[pl.ds(place, count, stride=rows), :]
        out[slot, plane, :, 128 * half : 128 * half + 128] = (value * jnp.abs(value)) * factor


def on_device(field, coefficient, slot_mode, couplings):
    slabs, count = lax.axis_size("slab"), lax.axis_size("mode")
    slots, planes_here, rows_all, columns = field.shape
    entries = couplings.shape[0]
    f32, bf16, i16, i32 = jnp.float32, jnp.bfloat16, jnp.int16, jnp.int32
    dma = pltpu.SemaphoreType.DMA
    halo = 4 * CHUNKS + 2

    held, row_low, row_high, plane_low, plane_high, near, coef_low, coef_high, address, weight = pl.pallas_call(
        lambda *refs: gather_kernel(slabs, count, *refs),
        out_shape=(
            shape_of((ROWS, 128), bf16),
            shape_of((ROWS, 128), bf16),
            shape_of((ROWS, 128), bf16),
            shape_of((ROWS // 2, 128), bf16),
            shape_of((ROWS // 2, 128), bf16),
            shape_of((3, TERMS, 8, 128), f32),
            shape_of((TERMS, 8, 128), f32),
            shape_of((TERMS, 8, 128), f32),
            shape_of((1, entries), i32),
            shape_of((1, entries), f32),
        ),
        in_specs=[SMEM, VMEM, VMEM, VMEM],
        out_specs=(VMEM,) * 10,
        scratch_shapes=[
            pltpu.VMEM((count * slots * 4, 128), f32),
            pltpu.VMEM((count, slots * 4, 128), bf16),
            pltpu.VMEM((count, slots * 4, 128), bf16),
            pltpu.VMEM((count * slots, 4, 128), f32),
            pltpu.VMEM((2, ROWS // 2, 128), bf16),
            pltpu.VMEM((ROWS, 128), f32),
            pltpu.VMEM((2, ROWS // 2, 128), f32),
            pltpu.VMEM((8, 128), i32),
            pltpu.SMEM((8, 128), i32),
            dma((2,)),
            dma((len(OFFSETS),)),
            dma((len(OFFSETS),)),
            dma((halo,)),
            dma((halo,)),
        ],
        compiler_params=pltpu.CompilerParams(collective_id=0, has_side_effects=True, vmem_limit_bytes=20 * MIB),
        name="gather",
    )(slot_mode, field, coefficient, couplings.T)

    image = pl.pallas_call(
        lambda *refs: apply_kernel(slabs, count, *refs),
        out_shape=shape_of((HELD, 4, 128), f32),
        in_specs=[SMEM] * 2 + [VMEM] * 8,
        out_specs=VMEM,
        scratch_shapes=[
            pltpu.VMEM((6 * TERMS, 8, 128), f32),
            pltpu.VMEM((ROWS, 128), f32),
            pltpu.VMEM((ROWS, 128), f32),
            pltpu.VMEM((ROWS, 128), f32),
            pltpu.VMEM(((TERMS - 1) * ROWS, 128), f32),
        ]
        + [pltpu.VMEM((ROWS, 128), f32)] * LANES,
        compiler_params=pltpu.CompilerParams(vmem_limit_bytes=24 * MIB),
        name="apply",
    )(address, weight, held, row_low, row_high, plane_low, plane_high, near, coef_low, coef_high)

    got, got_scales = pl.pallas_call(
        lambda *refs: return_kernel(count, *refs),
        out_shape=(shape_of((count, slots * 4, 128), i16), shape_of((count, 1, 128), f32)),
        in_specs=[SMEM, VMEM],
        out_specs=(VMEM, VMEM),
        scratch_shapes=[
            pltpu.VMEM((count * slots * 4, 128), f32),
            pltpu.VMEM((count, 4, 128), f32),
            pltpu.VMEM((count, slots * 4, 128), i16),
            pltpu.VMEM((count, 1, 128), f32),
            dma((2,)),
            dma((2, len(OFFSETS))),
            dma((2, len(OFFSETS))),
        ],
        compiler_params=pltpu.CompilerParams(collective_id=2, has_side_effects=True, vmem_limit_bytes=12 * MIB),
        name="give",
    )(slot_mode, image)

    step = 8
    return pl.pallas_call(
        decode_kernel,
        out_shape=shape_of((slots, planes_here, rows_all, columns), f32),
        grid=(slots // step,),
        in_specs=[
            pl.BlockSpec((count, 4 * step, 128), lambda i: (0, i, 0)),
            pl.BlockSpec((count, 1, 128), lambda i: (0, 0, 0)),
        ],
        out_specs=pl.BlockSpec((step, planes_here, rows_all, columns), lambda i: (i, 0, 0, 0)),
        scratch_shapes=[pltpu.VMEM((count * 4 * step, 128), f32), pltpu.VMEM((count, 128), f32)],
        compiler_params=pltpu.CompilerParams(vmem_limit_bytes=12 * MIB),
        name="decode",
    )(got, got_scales)


def solution(mesh):
    in_specs = (P("mode", "slab", None, None), P(None, "slab", None, None), P(), P())
    return jax.shard_map(
        on_device,
        mesh=mesh,
        in_specs=in_specs,
        out_specs=P("mode", "slab", None, None),
        check_vma=False,
    )
```

time: 111 us -> 77.5 us (0.70); the launches traced: 109 us -> 77.3 us
  Pallas kernels: 99.3 us -> 73.5 us
  other arithmetic: 5.2 us -> 0 us
    pallas_call x1, Pallas kernels: 29.4 us -> 14.6 us  [on_device(): pl.pallas_call(lambda *refs: apply_kernel(slabs, count, *refs), out_shape...]
    pallas_call x1, Pallas kernels: 25.3 us -> 20.5 us  [on_device(): pl.pallas_call(lambda *refs: return_kernel(count, *refs), out_shape=(shap...]
    pallas_call x2 -> x1, Pallas kernels: 39.7 us -> 35 us  [on_device(): pl.pallas_call(lambda *refs: gather_kernel(slabs, count, *refs), out_shap...]
    unnamed x0 -> x10, local copies, waits for them, and re-layouts: none -> 3.76 us
    reshape x2 -> x0, local copies, waits for them, and re-layouts: 3.42 us -> none  [on_device(): field.reshape(slots, planes_here, rows_all, 2, 128).transpose(2, 0, 1, 3, 4)]
    add x1 -> x0, other arithmetic: 1.55 us -> none  [on_device(): address = source + couplings[:, 0] * (4 << 16)]
    pallas_call x1, Pallas kernels: 4.81 us -> 3.35 us  [on_device(): pl.pallas_call(decode_kernel, out_shape=shape_of((slots, planes_here, row...]
    mul x1 -> x0, other arithmetic: 1.42 us -> none  [on_device(): weight = couplings[:, 3].astype(f32) * 0.125]
where the time goes in v2:
time: 77.5 us; the launch traced here: 77.3 us
  Pallas kernels  73.5 us (95%)
  local copies, waits for them, and re-layouts  3.76 us (5%)
    pallas_call x1, Pallas kernels, on_device(): pl.pallas_call(lambda *refs: gather_kernel(slabs, count, *refs), out_shap...  35 us
    pallas_call x1, Pallas kernels, on_device(): pl.pallas_call(lambda *refs: return_kernel(count, *refs), out_shape=(shap...  20.5 us
    pallas_call x1, Pallas kernels, on_device(): pl.pallas_call(lambda *refs: apply_kernel(slabs, count, *refs), out_shape...  14.6 us
    unnamed x10, local copies, waits for them, and re-layouts  3.76 us
    pallas_call x1, Pallas kernels, on_device(): pl.pallas_call(decode_kernel, out_shape=shape_of((slots, planes_here, row...  3.35 us

profile of v2, /device:TPU:1, one launch (start us, length us, event | category | flops | bytes accessed | tf_op | source)
XLA Modules:
  0.0 77.3 jit_solution(14009540863764388566)
XLA Ops:
  0.0 0.0 copy-start
  0.0 1.2 %copy-done = bf16[32,2,32,256]{3,2,1,0:T(8,128)(2,1)S(1)} copy-done((bf16[32,2,32,256]{3,2,1,0:T(8,128)(2,1)S(1)}, bf16[32,2,32,256]{3,2,1,0:T(8,128)(2,1)}, u32[]{:S(2)}) %copy-start) | copy-done | bytes 1048600
  1.2 0.0 copy-start.1
  1.2 1.1 %copy-done.1 = f32[9,2,32,256]{3,2,1,0:T(8,128)S(1)} copy-done((f32[9,2,32,256]{3,2,1,0:T(8,128)S(1)}, f32[9,2,32,256]{3,2,1,0:T(8,128)}, u32[]{:S(2)}) %copy-start.1) | copy-done | bytes 589848
  2.3 0.0 copy-start.2
  2.3 0.8 %copy-done.2 = s32[2640,4]{0,1:T(4,128)S(1)} copy-done((s32[2640,4]{0,1:T(4,128)S(1)}, s32[2640,4]{0,1:T(4,128)}, u32[]{:S(2)}) %copy-start.2) | copy-done | bytes 42264
  3.1 0.0 copy-start.3
  3.1 0.7 copy-done.3
  3.8 35.0 %gather.1 = (bf16[2048,128]{1,0:T(8,128)(2,1)S(1)}, bf16[2048,128]{1,0:T(8,128)(2,1)S(1)}, bf16[2048,128]{1,0:T(8,128)(2,1)S(1)}, bf16[1024,128]{1,0:T(8,128)(2,...) custom-call(s32[1024]{0:T(1024)S(1)} %copy-done.3, ...), custom_call_target="tpu_custom_call" | custom-call | tf_op jit(solution)/shard_map/gather/pallas_call | solution.py:412
  38.8 0.0 copy-start.4
  38.8 14.6 %apply.1.refs_1_ = f32[512,4,128]{2,1,0:T(4,128)S(1)} custom-call(s32[1,2640]{1,0:T(1,128)S(1)} %get-tuple-element.17.refs_0_, f32[1,2640]{1,0:T(1,128)S(1)} %get-tuple-element.18.refs_1_, bf16[2048,128]{1,0:T(8,128)(2,1)S(1)} %get-tuple-element.19.refs_2_, bf16[2048,128]{1,0:T(8,128)(2,1)S(1)} %get-tuple-element.20.refs_3_, ...), custom_call_target="tpu_custom_call" | custom-call | tf_op jit(solution)/shard_map/apply/pallas_call | solution.py:448
  53.4 0.0 copy-done.4
  53.4 20.5 %give.1 = (s16[32,128,128]{2,1,0:T(8,128)(2,1)S(1)}, f32[32,1,128]{2,1,0:T(1,128)S(1)}) custom-call(s32[1024]{0:T(1024)S(1)} %copy-done.4, f32[512,4,128]{2,1,0:T(4,128)S(1)} %apply.1.refs_1_), custom_call_target="tpu_custom_call" | custom-call | tf_op jit(solution)/shard_map/give/pallas_call | solution.py:465
  73.9 3.4 %decode.1 = f32[32,2,32,256]{3,2,1,0:T(8,128)} custom-call(s16[32,128,128]{2,1,0:T(8,128)(2,1)S(1)} %get-tuple-element.27.got, f32[32,1,128]{2,1,0:T(1,128)S(1)} %get-tuple-element.28.got_scales), custom_call_target="tpu_custom_call" | custom-call | tf_op jit(solution)/shard_map/decode/pallas_call | solution.py:484
Async XLA Ops:
  0.0 1.2 %copy-start = (bf16[32,2,32,256]{3,2,1,0:T(8,128)(2,1)S(1)}, bf16[32,2,32,256]{3,2,1,0:T(8,128)(2,1)}, u32[]{:S(2)}) copy-start(bf16[32,2,32,256]{3,2,1,0:T(8,128)(2,1)} %refs_1_.1) | copy-start | bytes 3145732
  1.2 1.1 %copy-start.1 = (f32[9,2,32,256]{3,2,1,0:T(8,128)S(1)}, f32[9,2,32,256]{3,2,1,0:T(8,128)}, u32[]{:S(2)}) copy-start(f32[9,2,32,256]{3,2,1,0:T(8,128)} %refs_2_.1) | copy-start | bytes 1769476
  2.3 0.8 %copy-start.2 = (s32[2640,4]{0,1:T(4,128)S(1)}, s32[2640,4]{0,1:T(4,128)}, u32[]{:S(2)}) copy-start(s32[2640,4]{0,1:T(4,128)} %param.7) | copy-start | bytes 126724
  3.1 0.7 copy-start.3
  38.8 14.7 %copy-start.4 = (s32[1024]{0:T(1024)S(1)}, s32[1024]{0:T(1024)}, u32[]{:S(2)}) copy-start(s32[1024]{0:T(1024)} %refs_0_.3) | copy-start | bytes 12292

commit v3 on v2

--- a/solution.py
+++ b/solution.py
@@ -10,13 +10,14 @@
 TERMS = 9
 ROWS = 4 * HELD
 LANES = 4
-UNROLL = 16
+UNROLL = 8
 CHUNKS = 4
 TOP = 32700.0
 SIDE = 4
 MESH = pl.DeviceIdType.MESH
 VMEM = pl.BlockSpec(memory_space=pltpu.VMEM)
 SMEM = pl.BlockSpec(memory_space=pltpu.SMEM)
+HBM = pl.BlockSpec(memory_space=pltpu.HBM)
 MIB = 1024 * 1024
 
 
@@ -44,11 +45,30 @@
     return pl.ds(pl.multiple_of(start, size), size)
 
 
+def plane_neighbours(centre, plane, front):
+    return (
+        jnp.where(front, plane, pltpu.roll(centre, 2, 0)),
+        jnp.where(front, pltpu.roll(centre, 6, 0), plane),
+    )
+
+
+def column_neighbours(centre, second, lane):
+    zero = jnp.zeros_like(centre)
+    low = pltpu.roll(centre, 1, 1)
+    high = pltpu.roll(centre, 127, 1)
+    return (
+        jnp.where(lane == 0, jnp.where(second, pltpu.roll(low, 1, 0), zero), low),
+        jnp.where(lane == 127, jnp.where(second, zero, pltpu.roll(high, 7, 0)), high),
+    )
+
+
 def gather_kernel(
-    slabs, count, slot_mode, field, coefficient, couplings,
-    held, row_low, row_high, plane_low, plane_high, near, coef_low, coef_high, address, weight,
-    turned, blocks, raw, wide_raw, planes, wide, wide_planes, found, inverse,
-    own_sem, send_sem, recv_sem, halo_send, halo_recv,
+    slabs, count, slot_mode_hbm, field_hbm, coefficient_hbm, couplings_hbm,
+    start, image, address, weight,
+    slot_mode, field, coefficient, couplings, turned, blocks, raw, wide_raw, wide, wide_planes, found, inverse,
+    held, planes, row_low, row_high, plane_low, plane_high, near, coef_low, coef_high,
+    faces, plane_rows, column_low, column_high,
+    load_sem, own_sem, send_sem, recv_sem, halo_send, halo_recv,
 ):
     slab, me = lax.axis_index("slab"), lax.axis_index("mode")
     slots = field.shape[0]
@@ -56,6 +76,29 @@
     below = (slab, lax.rem(me + count - 1, count))
     right = (lax.rem(slab + 1, slabs), me)
     left = (lax.rem(slab + slabs - 1, slabs), me)
+    sub = lax.broadcasted_iota(jnp.int32, (8, 128), 0)
+    lane = lax.broadcasted_iota(jnp.int32, (8, 128), 1)
+    front = lax.rem(sub, 4) < 2
+    second = lax.rem(sub, 2) == 1
+    has_left = (slab > 0).astype(jnp.float32)
+    has_right = (slab < slabs - 1).astype(jnp.float32)
+    mask_plane = jnp.where(front, has_left, has_right)
+    mask_low = (me > 0).astype(jnp.float32)
+    mask_high = (me < count - 1).astype(jnp.float32)
+
+    piece = slots // 4
+    loads = [
+        pltpu.make_async_copy(field_hbm.at[pl.ds(piece * part, piece)], field.at[pl.ds(piece * part, piece)], load_sem.at[part])
+        for part in range(4)
+    ]
+    others = [
+        pltpu.make_async_copy(source, target, load_sem.at[4 + place])
+        for place, (source, target) in enumerate(
+            ((coefficient_hbm, coefficient), (slot_mode_hbm, slot_mode), (couplings_hbm, couplings))
+        )
+    ]
+    for load in loads + others:
+        load.start()
     barrier = pltpu.get_barrier_semaphore()
     for offset in OFFSETS:
         pl.semaphore_signal(barrier, inc=1, device_id=(slab, moved(me, offset)), device_id_type=MESH)
@@ -69,7 +112,9 @@
             turned[pl.ds(4 * slot + part, count, stride=4 * slots), :] = value
         return carry
 
-    lax.fori_loop(0, slots, turn, 0)
+    for part, load in enumerate(loads):
+        load.wait()
+        lax.fori_loop(piece * part, piece * (part + 1), turn, 0)
 
     def narrow_block(row, carry):
         blocks[row] = turned[rows_at(row * 4 * slots, 4 * slots), :].astype(jnp.bfloat16)
@@ -93,16 +138,8 @@
         copies.append(copy)
     own = pltpu.make_async_copy(blocks.at[me], raw.at[me], own_sem.at[0])
     own.start()
-
-    ids = lax.broadcasted_iota(jnp.int32, (8, 128), 0) * 128 + lax.broadcasted_iota(jnp.int32, (8, 128), 1)
-
-    def find(step, place):
-        for part in range(8):
-            slot = step * 8 + part
-            place = jnp.where(ids == slot_mode[slot], slot, place)
-        return place
-
-    found[...] = lax.fori_loop(0, slots * count // 8, find, jnp.zeros((8, 128), jnp.int32))
+    for load in others:
+        load.wait()
 
     for shift in range(3):
         row = jnp.clip(me + shift - 1, 0, count - 1)
@@ -114,41 +151,15 @@
                 near[shift, term, part : part + 1, :] = value
                 near[shift, term, part + 4 : part + 5, :] = value
 
-    listed = pltpu.make_async_copy(found, inverse, own_sem.at[1])
-    listed.start()
-    listed.wait()
-    own.wait()
-
-    def widen(source):
-        for part in range(4):
-            value = raw[source, 32 * part : 32 * part + 32, :].astype(jnp.float32)
-            wide_raw[pl.ds(source * slots + 8 * part, 8)] = value.reshape(8, 4, 128)
-
-    widen(me)
-    for copy, offset in zip(copies, OFFSETS):
-        copy.wait()
-        widen(moved(me, offset, -1))
-
-    modes = HELD // CHUNKS
-
-    def pick(step, carry):
+    ids = sub * 128 + lane
+
+    def find(step, place):
         for part in range(8):
-            mode = step * 8 + part
-            source = inverse[mode // 128, mode % 128]
-            value = wide_raw[source]
-            wide[rows_at(4 * mode, 4), :] = value
-            wide_planes[0, rows_at(2 * mode, 2), :] = value[0:2]
-            wide_planes[1, rows_at(2 * mode, 2), :] = value[2:4]
-        return carry
-
-    def narrow(step, carry):
-        at = rows_at(step * 64, 64)
-        held[at, :] = wide[at, :].astype(jnp.bfloat16)
-        at = rows_at(step * 32, 32)
-        planes[0, at, :] = wide_planes[0, at, :].astype(jnp.bfloat16)
-        planes[1, at, :] = wide_planes[1, at, :].astype(jnp.bfloat16)
-        return carry
-
+            slot = step * 8 + part
+            place = jnp.where(ids == slot_mode[slot], slot, place)
+        return place
+
+    found[...] = lax.fori_loop(0, slots * count // 8, find, jnp.zeros((8, 128), jnp.int32))
     sent = []
 
     def send(place, source, target, peer):
@@ -163,6 +174,60 @@
         copy.start()
         sent.append(copy)
 
+    send(4 * CHUNKS, near.at[1], coef_low, right)
+    send(4 * CHUNKS + 1, near.at[1], coef_high, left)
+    own_coef = near.at[1]
+    first = couplings[0:1, :] * 4 + (couplings[2:3, :] - 1) * ROWS
+    other = couplings[1:2, :] * 4 + (couplings[2:3, :] - 1) * ROWS
+    address[...] = other + first * (1 << 16)
+    weight[...] = couplings[3:4, :].astype(jnp.float32) * 0.125
+
+    listed = pltpu.make_async_copy(found, inverse, own_sem.at[1])
+    listed.start()
+    listed.wait()
+    for copy in sent:
+        copy.wait()
+    sent.clear()
+
+    for term in range(TERMS):
+        middle = own_coef[term]
+        outer = jnp.where(front, pltpu.roll(coef_low[term], 6, 0), pltpu.roll(coef_high[term], 2, 0)) * mask_plane
+        around = plane_neighbours(middle, outer, front) + column_neighbours(middle, second, lane)
+        around = around + (near[0, term] * mask_low, near[2, term] * mask_high)
+        for place, value in enumerate(around):
+            faces[6 * term + place] = 0.5 * (middle + value)
+
+    def widen(source):
+        for part in range(4):
+            value = raw[source, 32 * part : 32 * part + 32, :].astype(jnp.float32)
+            wide_raw[pl.ds(source * slots + 8 * part, 8)] = value.reshape(8, 4, 128)
+
+    own.wait()
+    widen(me)
+    for copy, offset in zip(copies, OFFSETS):
+        copy.wait()
+        widen(moved(me, offset, -1))
+
+    modes = HELD // CHUNKS
+
+    def pick(step, carry):
+        for part in range(8):
+            mode = step * 8 + part
+            source = inverse[mode // 128, mode % 128]
+            value = wide_raw[source]
+            wide[rows_at(4 * mode, 4), :] = value
+            wide_planes[0, rows_at(2 * mode, 2), :] = value[0:2]
+            wide_planes[1, rows_at(2 * mode, 2), :] = value[2:4]
+        return carry
+
+    def narrow(step, carry):
+        at = rows_at(step * 64, 64)
+        held[at, :] = wide[at, :].astype(jnp.bfloat16)
+        at = rows_at(step * 32, 32)
+        planes[0, at, :] = wide_planes[0, at, :].astype(jnp.bfloat16)
+        planes[1, at, :] = wide_planes[1, at, :].astype(jnp.bfloat16)
+        return carry
+
     def send_chunk(chunk):
         at, half = pl.ds(chunk * 4 * modes, 4 * modes), pl.ds(chunk * 2 * modes, 2 * modes)
         send(4 * chunk, held.at[at], row_low.at[at], above)
@@ -170,60 +235,23 @@
         send(4 * chunk + 2, planes.at[1, half], plane_low.at[half], right)
         send(4 * chunk + 3, planes.at[0, half], plane_high.at[half], left)
 
+    def shift_columns(step, carry):
+        value = wide[rows_at(step * 128, 128), :]
+        around = [column_neighbours(value[8 * part : 8 * part + 8], second, lane) for part in range(16)]
+        for part, (low, high) in enumerate(around):
+            at = rows_at(step * 128 + 8 * part, 8)
+            column_low[at, :] = low
+            column_high[at, :] = high
+        return carry
+
     for chunk in range(CHUNKS):
         lax.fori_loop(chunk * modes // 8, (chunk + 1) * modes // 8, pick, 0)
         lax.fori_loop(chunk * modes // 16, (chunk + 1) * modes // 16, narrow, 0)
         if chunk:
             send_chunk(chunk - 1)
-    send(4 * CHUNKS, near.at[1], coef_low, right)
-    send(4 * CHUNKS + 1, near.at[1], coef_high, left)
-    source = (couplings[2:3, :] - 1) * ROWS + couplings[1:2, :] * 4
-    address[...] = source + couplings[0:1, :] * (4 << 16)
-    weight[...] = couplings[3:4, :].astype(jnp.float32) * 0.125
+    lax.fori_loop(0, 4, shift_columns, 0)
     send_chunk(CHUNKS - 1)
-    for copy in sent:
-        copy.wait()
-
-
-def plane_neighbours(centre, plane, front):
-    return (
-        jnp.where(front, plane, pltpu.roll(centre, 2, 0)),
-        jnp.where(front, pltpu.roll(centre, 6, 0), plane),
-    )
-
-
-def column_neighbours(centre, second, lane):
-    zero = jnp.zeros_like(centre)
-    low = pltpu.roll(centre, 1, 1)
-    high = pltpu.roll(centre, 127, 1)
-    return (
-        jnp.where(lane == 0, jnp.where(second, pltpu.roll(low, 1, 0), zero), low),
-        jnp.where(lane == 127, jnp.where(second, zero, pltpu.roll(high, 7, 0)), high),
-    )
-
-
-def apply_kernel(
-    slabs, count, address, weight, held, row_low, row_high, plane_low, plane_high, near, coef_low, coef_high,
-    out, faces, plane_rows, column_low, column_high, image, *sums,
-):
-    slab, me = lax.axis_index("slab"), lax.axis_index("mode")
-    sub = lax.broadcasted_iota(jnp.int32, (8, 128), 0)
-    lane = lax.broadcasted_iota(jnp.int32, (8, 128), 1)
-    front = lax.rem(sub, 4) < 2
-    second = lax.rem(sub, 2) == 1
-    has_left = (slab > 0).astype(jnp.float32)
-    has_right = (slab < slabs - 1).astype(jnp.float32)
-    mask_plane = jnp.where(front, has_left, has_right)
-    mask_low = (me > 0).astype(jnp.float32)
-    mask_high = (me < count - 1).astype(jnp.float32)
-
-    for term in range(TERMS):
-        own = near[1, term]
-        outer = jnp.where(front, pltpu.roll(coef_low[term], 6, 0), pltpu.roll(coef_high[term], 2, 0)) * mask_plane
-        around = plane_neighbours(own, outer, front) + column_neighbours(own, second, lane)
-        around = around + (near[0, term] * mask_low, near[2, term] * mask_high)
-        for place, other in enumerate(around):
-            faces[6 * term + place] = 0.5 * (own + other)
+    lax.fori_loop(4, ROWS // 128, shift_columns, 0)
 
     def interleave(step, carry):
         at = rows_at(step * 16, 16)
@@ -235,22 +263,8 @@
             plane_rows[pl.ds(base + 2, 2), :] = high[2 * part : 2 * part + 2]
         return carry
 
-    lax.fori_loop(0, ROWS // 32, interleave, 0)
-
-    def shift(step, carry):
-        value = held[rows_at(step * 128, 128), :].astype(jnp.float32)
-        around = [column_neighbours(value[8 * part : 8 * part + 8], second, lane) for part in range(16)]
-        for part, (low, high) in enumerate(around):
-            at = rows_at(step * 128 + 8 * part, 8)
-            column_low[at, :] = low
-            column_high[at, :] = high
-        return carry
-
-    lax.fori_loop(0, ROWS // 128, shift, 0)
-
     def stencil(step, carry):
         at = rows_at(step * 16, 16)
-        centre = held[at, :].astype(jnp.float32)
         low = row_low[at, :].astype(jnp.float32)
         high = row_high[at, :].astype(jnp.float32)
         halves = []
@@ -258,10 +272,10 @@
             part = slice(8 * half, 8 * half + 8)
             base = pl.multiple_of(step * 16 + 8 * half, 8)
             at = pl.ds(base, 8)
-            own = centre[part]
-            around = plane_neighbours(own, plane_rows[at, :], front) + (column_low[at, :], column_high[at, :])
+            middle = wide[at, :]
+            around = plane_neighbours(middle, plane_rows[at, :], front) + (column_low[at, :], column_high[at, :])
             around = around + (low[part] * mask_low, high[part] * mask_high)
-            halves.append((base, [own - other for other in around]))
+            halves.append((base, [middle - value for value in around]))
         for term in range(TERMS):
             face = [faces[6 * term + place] for place in range(6)]
             for base, drops in halves:
@@ -269,16 +283,22 @@
                 for place in range(1, 6):
                     total = total + face[place] * drops[place]
                 if term == 0:
-                    sums[0][pl.ds(base, 8), :] = total
+                    start[pl.ds(base, 8), :] = total
                 else:
                     image[rows_at((term - 1) * ROWS + base, 8), :] = total
         return carry
 
-    lax.fori_loop(0, ROWS // 16, stencil, 0)
-
+    for chunk in range(CHUNKS):
+        for copy in sent[4 * chunk : 4 * chunk + 4]:
+            copy.wait()
+        lax.fori_loop(chunk * modes // 8, (chunk + 1) * modes // 8, interleave, 0)
+        lax.fori_loop(chunk * modes // 4, (chunk + 1) * modes // 4, stencil, 0)
+
+
+def apply_kernel(address, weight, start, image, out, *sums):
     def clear(step, carry):
         at = rows_at(step * 32, 32)
-        for total in sums[1:]:
+        for total in sums:
             total[at, :] = jnp.zeros((32, 128), jnp.float32)
         return carry
 
@@ -286,20 +306,25 @@
 
     def couple(step, carry):
         for part in range(UNROLL):
-            place = step * UNROLL + part
+            place = 2 * (step * UNROLL + part)
             both = address[0, place]
-            source = pl.ds(pl.multiple_of(lax.bitwise_and(both, 0xFFFF), 4), 4)
-            target = pl.ds(pl.multiple_of(lax.shift_right_logical(both, 16), 4), 4)
+            low, high = lax.bitwise_and(both, 0xFFFF), lax.shift_right_logical(both, 16)
+            at_low = pl.ds(pl.multiple_of(lax.bitwise_and(low, ROWS - 1), 4), 4)
+            at_high = pl.ds(pl.multiple_of(lax.bitwise_and(high, ROWS - 1), 4), 4)
+            factor = weight[0, place]
             total = sums[part % LANES]
-            total[target, :] = total[target, :] + weight[0, place] * image[source, :]
-        return carry
-
-    lax.fori_loop(0, address.shape[1] // UNROLL, couple, 0)
+            to_high = total[at_high, :] + factor * image[pl.ds(pl.multiple_of(low, 4), 4), :]
+            to_low = total[at_low, :] + factor * image[pl.ds(pl.multiple_of(high, 4), 4), :]
+            total[at_high, :] = to_high
+            total[at_low, :] = to_low
+        return carry
+
+    lax.fori_loop(0, address.shape[1] // (2 * UNROLL), couple, 0)
 
     def join(step, carry):
         at = rows_at(step * 32, 32)
-        total = sums[0][at, :]
-        for other in sums[1:]:
+        total = start[at, :]
+        for other in sums:
             total = total + other[at, :]
         out[pl.ds(8 * step, 8)] = total.reshape(8, 4, 128)
         return carry
@@ -409,58 +434,62 @@
     dma = pltpu.SemaphoreType.DMA
     halo = 4 * CHUNKS + 2
 
-    held, row_low, row_high, plane_low, plane_high, near, coef_low, coef_high, address, weight = pl.pallas_call(
+    start, image, address, weight = pl.pallas_call(
         lambda *refs: gather_kernel(slabs, count, *refs),
         out_shape=(
-            shape_of((ROWS, 128), bf16),
-            shape_of((ROWS, 128), bf16),
-            shape_of((ROWS, 128), bf16),
-            shape_of((ROWS // 2, 128), bf16),
-            shape_of((ROWS // 2, 128), bf16),
-            shape_of((3, TERMS, 8, 128), f32),
-            shape_of((TERMS, 8, 128), f32),
-            shape_of((TERMS, 8, 128), f32),
+            shape_of((ROWS, 128), f32),
+            shape_of(((TERMS - 1) * ROWS, 128), f32),
             shape_of((1, entries), i32),
             shape_of((1, entries), f32),
         ),
-        in_specs=[SMEM, VMEM, VMEM, VMEM],
-        out_specs=(VMEM,) * 10,
+        in_specs=[HBM] * 4,
+        out_specs=(VMEM,) * 4,
         scratch_shapes=[
+            pltpu.SMEM(slot_mode.shape, i32),
+            pltpu.VMEM(field.shape, bf16),
+            pltpu.VMEM(coefficient.shape, f32),
+            pltpu.VMEM((4, entries), i32),
             pltpu.VMEM((count * slots * 4, 128), f32),
             pltpu.VMEM((count, slots * 4, 128), bf16),
             pltpu.VMEM((count, slots * 4, 128), bf16),
             pltpu.VMEM((count * slots, 4, 128), f32),
-            pltpu.VMEM((2, ROWS // 2, 128), bf16),
             pltpu.VMEM((ROWS, 128), f32),
             pltpu.VMEM((2, ROWS // 2, 128), f32),
             pltpu.VMEM((8, 128), i32),
             pltpu.SMEM((8, 128), i32),
+            pltpu.VMEM((ROWS, 128), bf16),
+            pltpu.VMEM((2, ROWS // 2, 128), bf16),
+            pltpu.VMEM((ROWS, 128), bf16),
+            pltpu.VMEM((ROWS, 128), bf16),
+            pltpu.VMEM((ROWS // 2, 128), bf16),
+            pltpu.VMEM((ROWS // 2, 128), bf16),
+            pltpu.VMEM((3, TERMS, 8, 128), f32),
+            pltpu.VMEM((TERMS, 8, 128), f32),
+            pltpu.VMEM((TERMS, 8, 128), f32),
+            pltpu.VMEM((6 * TERMS, 8, 128), f32),
+            pltpu.VMEM((ROWS, 128), f32),
+            pltpu.VMEM((ROWS, 128), f32),
+            pltpu.VMEM((ROWS, 128), f32),
+            dma((7,)),
             dma((2,)),
             dma((len(OFFSETS),)),
             dma((len(OFFSETS),)),
             dma((halo,)),
             dma((halo,)),
         ],
-        compiler_params=pltpu.CompilerParams(collective_id=0, has_side_effects=True, vmem_limit_bytes=20 * MIB),
+        compiler_params=pltpu.CompilerParams(collective_id=0, has_side_effects=True, vmem_limit_bytes=30 * MIB),
         name="gather",
-    )(slot_mode, field, coefficient, couplings.T)
+    )(*(pltpu.with_memory_space_constraint(value, pltpu.HBM) for value in (slot_mode, field, coefficient, couplings.T)))
 
     image = pl.pallas_call(
-        lambda *refs: apply_kernel(slabs, count, *refs),
+        apply_kernel,
         out_shape=shape_of((HELD, 4, 128), f32),
-        in_specs=[SMEM] * 2 + [VMEM] * 8,
+        in_specs=[SMEM] * 2 + [VMEM] * 2,
         out_specs=VMEM,
-        scratch_shapes=[
-            pltpu.VMEM((6 * TERMS, 8, 128), f32),
-            pltpu.VMEM((ROWS, 128), f32),
-            pltpu.VMEM((ROWS, 128), f32),
-            pltpu.VMEM((ROWS, 128), f32),
-            pltpu.VMEM(((TERMS - 1) * ROWS, 128), f32),
-        ]
-        + [pltpu.VMEM((ROWS, 128), f32)] * LANES,
-        compiler_params=pltpu.CompilerParams(vmem_limit_bytes=24 * MIB),
+        scratch_shapes=[pltpu.VMEM((ROWS, 128), f32)] * LANES,
+        compiler_params=pltpu.CompilerParams(vmem_limit_bytes=20 * MIB),
         name="apply",
-    )(address, weight, held, row_low, row_high, plane_low, plane_high, near, coef_low, coef_high)
+    )(address, weight, start, image)
 
     got, got_scales = pl.pallas_call(
         lambda *refs: return_kernel(count, *refs),

time: 77.5 us -> 65.9 us (0.85)
  Pallas kernels: 73.5 us -> 65.7 us
  local copies, waits for them, and re-layouts: 3.76 us -> 0.01 us
    pallas_call x1, Pallas kernels: 14.6 us -> 6.7 us  [on_device(): pl.pallas_call(apply_kernel, out_shape=shape_of((HELD, 4, 128), f32), in_...]
    unnamed x10 -> x2, local copies, waits for them, and re-layouts: 3.76 us -> 0.01 us
where the time goes in v3:
time: 65.9 us; the launch traced here: 65.8 us
  Pallas kernels  65.7 us (100%)
    pallas_call x1, Pallas kernels, on_device(): pl.pallas_call(lambda *refs: gather_kernel(slabs, count, *refs), out_shap...  35 us
    pallas_call x1, Pallas kernels, on_device(): pl.pallas_call(lambda *refs: return_kernel(count, *refs), out_shape=(shap...  20.7 us
    pallas_call x1, Pallas kernels, on_device(): pl.pallas_call(apply_kernel, out_shape=shape_of((HELD, 4, 128), f32), in_...  6.7 us
    pallas_call x1, Pallas kernels, on_device(): pl.pallas_call(decode_kernel, out_shape=shape_of((slots, planes_here, row...  3.35 us

profile of v3, /device:TPU:1, one launch (start us, length us, event | category | flops | bytes accessed | tf_op | source)
XLA Modules:
  0.0 65.8 jit_solution(17899525121192163458)
XLA Ops:
  0.0 0.0 copy-start
  0.0 35.0 %gather.1 = (f32[2048,128]{1,0:T(8,128)S(1)}, f32[16384,128]{1,0:T(8,128)S(1)}, s32[1,2640]{1,0:T(1,128)S(1)}, f32[1,2640]{1,0:T(1,128)S(1)}) custom-call(s32[1024]{0:T(1024)} %refs_0_.3, bf16[32,2,32,256]{3,2,1,0:T(8,128)(2,1)} %refs_1_.1, f32[9,2,32,256]{3,2,1,0:T(8,128)} %refs_2_.1, s32[4,2640]{1,0:T(4,128)} %bitcast.1), custom_call_target="tpu_custom_call" | custom-call | tf_op jit(solution)/shard_map/gather/pallas_call | solution.py:437
  35.0 6.7 %apply.1.refs_1_ = f32[512,4,128]{2,1,0:T(4,128)S(1)} custom-call(s32[1,2640]{1,0:T(1,128)S(1)} %get-tuple-element.11.address, f32[1,2640]{1,0:T(1,128)S(1)} %get-tuple-element.12.weight, f32[2048,128]{1,0:T(8,128)S(1)} %get-tuple-element.13.start, f32[16384,128]{1,0:T(8,128)S(1)} %get-tuple-element.14.image), custom_call_target="tpu_custom_call" | custom-call | tf_op jit(solution)/shard_map/apply/pallas_call | solution.py:484
  41.7 0.0 copy-done
  41.7 20.7 %give.1 = (s16[32,128,128]{2,1,0:T(8,128)(2,1)S(1)}, f32[32,1,128]{2,1,0:T(1,128)S(1)}) custom-call(s32[1024]{0:T(1024)S(1)} %copy-done, f32[512,4,128]{2,1,0:T(4,128)S(1)} %apply.1.refs_1_), custom_call_target="tpu_custom_call" | custom-call | tf_op jit(solution)/shard_map/give/pallas_call | solution.py:494
  62.4 3.4 %decode.1 = f32[32,2,32,256]{3,2,1,0:T(8,128)} custom-call(s16[32,128,128]{2,1,0:T(8,128)(2,1)S(1)} %get-tuple-element.15.got, f32[32,1,128]{2,1,0:T(1,128)S(1)} %get-tuple-element.16.got_scales), custom_call_target="tpu_custom_call" | custom-call | tf_op jit(solution)/shard_map/decode/pallas_call | solution.py:513
Async XLA Ops:
  0.0 41.7 %copy-start = (s32[1024]{0:T(1024)S(1)}, s32[1024]{0:T(1024)}, u32[]{:S(2)}) copy-start(s32[1024]{0:T(1024)} %refs_0_.3) | copy-start | bytes 12292

commit v4 on v3

--- a/solution.py
+++ b/solution.py
@@ -9,10 +9,12 @@
 HELD = 512
 TERMS = 9
 ROWS = 4 * HELD
-LANES = 4
-UNROLL = 8
-CHUNKS = 4
+LANES = 2
+UNROLL = 12
+CHUNKS = 8
+USED = 496
 TOP = 32700.0
+EARLY = 12
 SIDE = 4
 MESH = pl.DeviceIdType.MESH
 VMEM = pl.BlockSpec(memory_space=pltpu.VMEM)
@@ -208,12 +210,12 @@
         copy.wait()
         widen(moved(me, offset, -1))
 
-    modes = HELD // CHUNKS
+    ends = [min(chunk * HELD // CHUNKS, USED) for chunk in range(CHUNKS + 1)]
 
     def pick(step, carry):
         for part in range(8):
             mode = step * 8 + part
-            source = inverse[mode // 128, mode % 128]
+            source = inverse[lax.shift_right_logical(step, 4), lax.bitwise_and(step, 15) * 8 + part]
             value = wide_raw[source]
             wide[rows_at(4 * mode, 4), :] = value
             wide_planes[0, rows_at(2 * mode, 2), :] = value[0:2]
@@ -229,29 +231,30 @@
         return carry
 
     def send_chunk(chunk):
-        at, half = pl.ds(chunk * 4 * modes, 4 * modes), pl.ds(chunk * 2 * modes, 2 * modes)
+        low, size = ends[chunk], ends[chunk + 1] - ends[chunk]
+        at, half = pl.ds(4 * low, 4 * size), pl.ds(2 * low, 2 * size)
         send(4 * chunk, held.at[at], row_low.at[at], above)
         send(4 * chunk + 1, held.at[at], row_high.at[at], below)
         send(4 * chunk + 2, planes.at[1, half], plane_low.at[half], right)
         send(4 * chunk + 3, planes.at[0, half], plane_high.at[half], left)
 
     def shift_columns(step, carry):
-        value = wide[rows_at(step * 128, 128), :]
-        around = [column_neighbours(value[8 * part : 8 * part + 8], second, lane) for part in range(16)]
+        value = wide[rows_at(step * 64, 64), :]
+        around = [column_neighbours(value[8 * part : 8 * part + 8], second, lane) for part in range(8)]
         for part, (low, high) in enumerate(around):
-            at = rows_at(step * 128 + 8 * part, 8)
+            at = rows_at(step * 64 + 8 * part, 8)
             column_low[at, :] = low
             column_high[at, :] = high
         return carry
 
     for chunk in range(CHUNKS):
-        lax.fori_loop(chunk * modes // 8, (chunk + 1) * modes // 8, pick, 0)
-        lax.fori_loop(chunk * modes // 16, (chunk + 1) * modes // 16, narrow, 0)
+        lax.fori_loop(ends[chunk] // 8, ends[chunk + 1] // 8, pick, 0)
+        lax.fori_loop(ends[chunk] // 16, ends[chunk + 1] // 16, narrow, 0)
         if chunk:
             send_chunk(chunk - 1)
     lax.fori_loop(0, 4, shift_columns, 0)
     send_chunk(CHUNKS - 1)
-    lax.fori_loop(4, ROWS // 128, shift_columns, 0)
+    lax.fori_loop(4, USED // 16, shift_columns, 0)
 
     def interleave(step, carry):
         at = rows_at(step * 16, 16)
@@ -291,14 +294,14 @@
     for chunk in range(CHUNKS):
         for copy in sent[4 * chunk : 4 * chunk + 4]:
             copy.wait()
-        lax.fori_loop(chunk * modes // 8, (chunk + 1) * modes // 8, interleave, 0)
-        lax.fori_loop(chunk * modes // 4, (chunk + 1) * modes // 4, stencil, 0)
-
-
-def apply_kernel(address, weight, start, image, out, *sums):
+        lax.fori_loop(ends[chunk] // 8, ends[chunk + 1] // 8, interleave, 0)
+        lax.fori_loop(ends[chunk] // 4, ends[chunk + 1] // 4, stencil, 0)
+
+
+def apply_kernel(address, weight, start, image, *sums):
     def clear(step, carry):
         at = rows_at(step * 32, 32)
-        for total in sums:
+        for total in sums[1:]:
             total[at, :] = jnp.zeros((32, 128), jnp.float32)
         return carry
 
@@ -321,24 +324,26 @@
 
     lax.fori_loop(0, address.shape[1] // (2 * UNROLL), couple, 0)
 
-    def join(step, carry):
-        at = rows_at(step * 32, 32)
-        total = start[at, :]
-        for other in sums:
-            total = total + other[at, :]
-        out[pl.ds(8 * step, 8)] = total.reshape(8, 4, 128)
-        return carry
-
-    lax.fori_loop(0, ROWS // 32, join, 0)
-    out[MODES] = jnp.zeros((4, 128), jnp.float32)
-
-
-def return_kernel(count, slot_mode, image, got, got_scales, picked, factors, coded, scales, own_sem, send_sem, recv_sem):
+
+def return_kernel(count, slot_mode, *refs):
+    sums, refs = refs[:LANES], refs[LANES:]
+    got, got_scales, image, picked, factors, coded, scales, own_sem, send_sem, recv_sem = refs
     slab, me = lax.axis_index("slab"), lax.axis_index("mode")
     slots = slot_mode.shape[0] // count
     barrier = pltpu.get_barrier_semaphore()
     for offset in OFFSETS:
         pl.semaphore_signal(barrier, inc=1, device_id=(slab, moved(me, offset)), device_id_type=MESH)
+
+    def join(step, carry):
+        at = rows_at(step * 32, 32)
+        total = sums[0][at, :]
+        for other in sums[1:]:
+            total = total + other[at, :]
+        image[pl.ds(8 * step, 8)] = total.reshape(8, 4, 128)
+        return carry
+
+    lax.fori_loop(0, USED // 8, join, 0)
+    image[MODES] = jnp.zeros((4, 128), jnp.float32)
 
     def pick(group, carry):
         tops = [jnp.zeros((4, 128), jnp.float32)] * 4
@@ -391,9 +396,12 @@
             copy.start()
             copies.append(copy)
 
-    encode(moved(me, OFFSETS[0]))
+    for place in range(EARLY):
+        encode(moved(me, OFFSETS[place]))
     pl.semaphore_wait(barrier, len(OFFSETS))
-    for place in range(1, len(OFFSETS)):
+    for place in range(EARLY - 1):
+        send(place)
+    for place in range(EARLY, len(OFFSETS)):
         encode(moved(me, OFFSETS[place]))
         send(place - 1)
     encode(me)
@@ -481,22 +489,23 @@
         name="gather",
     )(*(pltpu.with_memory_space_constraint(value, pltpu.HBM) for value in (slot_mode, field, coefficient, couplings.T)))
 
-    image = pl.pallas_call(
+    sums = pl.pallas_call(
         apply_kernel,
-        out_shape=shape_of((HELD, 4, 128), f32),
+        out_shape=(shape_of((ROWS, 128), f32),) * LANES,
         in_specs=[SMEM] * 2 + [VMEM] * 2,
-        out_specs=VMEM,
-        scratch_shapes=[pltpu.VMEM((ROWS, 128), f32)] * LANES,
-        compiler_params=pltpu.CompilerParams(vmem_limit_bytes=20 * MIB),
+        out_specs=(VMEM,) * LANES,
+        input_output_aliases={2: 0},
+        compiler_params=pltpu.CompilerParams(vmem_limit_bytes=16 * MIB),
         name="apply",
     )(address, weight, start, image)
 
     got, got_scales = pl.pallas_call(
         lambda *refs: return_kernel(count, *refs),
         out_shape=(shape_of((count, slots * 4, 128), i16), shape_of((count, 1, 128), f32)),
-        in_specs=[SMEM, VMEM],
+        in_specs=[SMEM] + [VMEM] * LANES,
         out_specs=(VMEM, VMEM),
         scratch_shapes=[
+            pltpu.VMEM((HELD, 4, 128), f32),
             pltpu.VMEM((count * slots * 4, 128), f32),
             pltpu.VMEM((count, 4, 128), f32),
             pltpu.VMEM((count, slots * 4, 128), i16),
@@ -507,7 +516,7 @@
         ],
         compiler_params=pltpu.CompilerParams(collective_id=2, has_side_effects=True, vmem_limit_bytes=12 * MIB),
         name="give",
-    )(slot_mode, image)
+    )(slot_mode, *sums)
 
     step = 8
     return pl.pallas_call(

time: 65.9 us -> 62.1 us (0.942)
  Pallas kernels: 65.7 us -> 62 us
    pallas_call x1, Pallas kernels: 35 us -> 32.4 us  [on_device(): pl.pallas_call(lambda *refs: gather_kernel(slabs, count, *refs), out_shap...]
    pallas_call x1, Pallas kernels: 6.7 us -> 5.88 us  [on_device(): pl.pallas_call(apply_kernel, out_shape=(shape_of((ROWS, 128), f32),) * LA...]
where the time goes in v4:
time: 62.1 us; the launch traced here: 62 us
  Pallas kernels  62 us (100%)
    pallas_call x1, Pallas kernels, on_device(): pl.pallas_call(lambda *refs: gather_kernel(slabs, count, *refs), out_shap...  32.4 us
    pallas_call x1, Pallas kernels, on_device(): pl.pallas_call(lambda *refs: return_kernel(count, *refs), out_shape=(shap...  20.4 us
    pallas_call x1, Pallas kernels, on_device(): pl.pallas_call(apply_kernel, out_shape=(shape_of((ROWS, 128), f32),) * LA...  5.88 us
    pallas_call x1, Pallas kernels, on_device(): pl.pallas_call(decode_kernel, out_shape=shape_of((slots, planes_here, row...  3.35 us

profile of v4, /device:TPU:1, one launch (start us, length us, event | category | flops | bytes accessed | tf_op | source)
XLA Modules:
  0.0 62.0 jit_solution(13819786156591689771)
XLA Ops:
  0.0 0.0 copy-start
  0.0 32.4 %gather.1 = (f32[2048,128]{1,0:T(8,128)S(1)}, f32[16384,128]{1,0:T(8,128)S(1)}, s32[1,2640]{1,0:T(1,128)S(1)}, f32[1,2640]{1,0:T(1,128)S(1)}) custom-call(s32[1024]{0:T(1024)} %refs_0_.3, bf16[32,2,32,256]{3,2,1,0:T(8,128)(2,1)} %refs_1_.1, f32[9,2,32,256]{3,2,1,0:T(8,128)} %refs_2_.1, s32[4,2640]{1,0:T(4,128)} %bitcast.1), custom_call_target="tpu_custom_call" | custom-call | tf_op jit(solution)/shard_map/gather/pallas_call | solution.py:445
  32.4 5.9 %apply.1 = (f32[2048,128]{1,0:T(8,128)S(1)}, f32[2048,128]{1,0:T(8,128)S(1)}) custom-call(s32[1,2640]{1,0:T(1,128)S(1)} %get-tuple-element.13.address, f32[1,2640]{1,0:T(1,128)S(1)} %get-tuple-element.14.weight, f32[2048,128]{1,0:T(8,128)S(1)} %get-tuple-element.15.start, f32[16384,128]{1,0:T(8,128)S(1)} %get-tuple-element.16.image), custom_call_target="tpu_custom_call", output_to_operand_aliasing={{0}: (2, {})} | custom-call | tf_op jit(solution)/shard_map/apply/pallas_call | solution.py:492
  38.3 0.0 copy-done
  38.3 20.4 %give.1 = (s16[32,128,128]{2,1,0:T(8,128)(2,1)S(1)}, f32[32,1,128]{2,1,0:T(1,128)S(1)}) custom-call(s32[1024]{0:T(1024)S(1)} %copy-done, f32[2048,128]{1,0:T(8,128)S(1)} %get-tuple-element.17.refs_1_, f32[2048,128]{1,0:T(8,128)S(1)} %get-tuple-element.18.refs_2_), custom_call_target="tpu_custom_call" | custom-call | tf_op jit(solution)/shard_map/give/pallas_call | solution.py:502
  58.6 3.4 %decode.1 = f32[32,2,32,256]{3,2,1,0:T(8,128)} custom-call(s16[32,128,128]{2,1,0:T(8,128)(2,1)S(1)} %get-tuple-element.19.got, f32[32,1,128]{2,1,0:T(1,128)S(1)} %get-tuple-element.20.got_scales), custom_call_target="tpu_custom_call" | custom-call | tf_op jit(solution)/shard_map/decode/pallas_call | solution.py:522
Async XLA Ops:
  0.0 38.3 %copy-start = (s32[1024]{0:T(1024)S(1)}, s32[1024]{0:T(1024)}, u32[]{:S(2)}) copy-start(s32[1024]{0:T(1024)} %refs_0_.3) | copy-start | bytes 12292

commit v5 on v4

--- a/solution.py
+++ b/solution.py
@@ -67,7 +67,7 @@
 def gather_kernel(
     slabs, count, slot_mode_hbm, field_hbm, coefficient_hbm, couplings_hbm,
     start, image, address, weight,
-    slot_mode, field, coefficient, couplings, turned, blocks, raw, wide_raw, wide, wide_planes, found, inverse,
+    slot_mode, field, coefficient, couplings, turned, blocks, raw, wide, wide_planes, found, inverse,
     held, planes, row_low, row_high, plane_low, plane_high, near, coef_low, coef_high,
     faces, plane_rows, column_low, column_high,
     load_sem, own_sem, send_sem, recv_sem, halo_send, halo_recv,
@@ -119,7 +119,8 @@
         lax.fori_loop(piece * part, piece * (part + 1), turn, 0)
 
     def narrow_block(row, carry):
-        blocks[row] = turned[rows_at(row * 4 * slots, 4 * slots), :].astype(jnp.bfloat16)
+        value = turned[rows_at(row * 4 * slots, 4 * slots), :]
+        blocks[row] = value.reshape(slots, 4, 128).astype(jnp.bfloat16)
         return carry
 
     lax.fori_loop(0, count, narrow_block, 0)
@@ -130,7 +131,7 @@
         peer = moved(me, offset)
         copy = pltpu.make_async_remote_copy(
             src_ref=blocks.at[peer],
-            dst_ref=raw.at[me],
+            dst_ref=raw.at[pl.ds(me * slots, slots)],
             send_sem=send_sem.at[place],
             recv_sem=recv_sem.at[place],
             device_id=(slab, peer),
@@ -138,7 +139,7 @@
         )
         copy.start()
         copies.append(copy)
-    own = pltpu.make_async_copy(blocks.at[me], raw.at[me], own_sem.at[0])
+    own = pltpu.make_async_copy(blocks.at[me], raw.at[pl.ds(me * slots, slots)], own_sem.at[0])
     own.start()
     for load in others:
         load.wait()
@@ -199,16 +200,9 @@
         for place, value in enumerate(around):
             faces[6 * term + place] = 0.5 * (middle + value)
 
-    def widen(source):
-        for part in range(4):
-            value = raw[source, 32 * part : 32 * part + 32, :].astype(jnp.float32)
-            wide_raw[pl.ds(source * slots + 8 * part, 8)] = value.reshape(8, 4, 128)
-
     own.wait()
-    widen(me)
-    for copy, offset in zip(copies, OFFSETS):
+    for copy in copies:
         copy.wait()
-        widen(moved(me, offset, -1))
 
     ends = [min(chunk * HELD // CHUNKS, USED) for chunk in range(CHUNKS + 1)]
 
@@ -216,7 +210,7 @@
         for part in range(8):
             mode = step * 8 + part
             source = inverse[lax.shift_right_logical(step, 4), lax.bitwise_and(step, 15) * 8 + part]
-            value = wide_raw[source]
+            value = raw[source].astype(jnp.float32)
             wide[rows_at(4 * mode, 4), :] = value
             wide_planes[0, rows_at(2 * mode, 2), :] = value[0:2]
             wide_planes[1, rows_at(2 * mode, 2), :] = value[2:4]
@@ -327,66 +321,66 @@
 
 def return_kernel(count, slot_mode, *refs):
     sums, refs = refs[:LANES], refs[LANES:]
-    got, got_scales, image, picked, factors, coded, scales, own_sem, send_sem, recv_sem = refs
+    got, got_scales, image, codes, picked, coded, scale, own_sem, send_sem, recv_sem = refs
     slab, me = lax.axis_index("slab"), lax.axis_index("mode")
     slots = slot_mode.shape[0] // count
     barrier = pltpu.get_barrier_semaphore()
     for offset in OFFSETS:
         pl.semaphore_signal(barrier, inc=1, device_id=(slab, moved(me, offset)), device_id_type=MESH)
 
-    def join(step, carry):
+    def joined(step):
         at = rows_at(step * 32, 32)
         total = sums[0][at, :]
         for other in sums[1:]:
             total = total + other[at, :]
-        image[pl.ds(8 * step, 8)] = total.reshape(8, 4, 128)
-        return carry
-
-    lax.fori_loop(0, USED // 8, join, 0)
-    image[MODES] = jnp.zeros((4, 128), jnp.float32)
-
-    def pick(group, carry):
-        tops = [jnp.zeros((4, 128), jnp.float32)] * 4
-        for part in range(slots):
-            slot = group * slots + part
-            value = image[slot_mode[slot]]
-            picked[rows_at(4 * slot, 4), :] = value
-            tops[part % 4] = jnp.maximum(tops[part % 4], jnp.abs(value))
-        factors[group] = jnp.maximum(jnp.maximum(tops[0], tops[1]), jnp.maximum(tops[2], tops[3]))
-        return carry
-
-    lax.fori_loop(0, count, pick, 0)
-
-    def measure(step, carry):
-        for part in range(8):
-            group = step * 8 + part
-            top = jnp.max(jnp.max(factors[group], axis=0, keepdims=True), axis=1, keepdims=True)
-            top = jnp.broadcast_to(top, (1, 128))
-            scales[group] = top * (1.0 / (TOP * TOP))
-            factors[group] = jnp.broadcast_to(TOP * lax.rsqrt(jnp.maximum(top, 1e-37)), (4, 128))
-        return carry
-
-    lax.fori_loop(0, count // 8, measure, 0)
-
-    def encode(group):
-        factor = factors[group][0:1]
-
-        def part_of(part, carry):
-            value = picked[rows_at(group * 4 * slots + part * 32, 32), :]
-            root = value * lax.rsqrt(jnp.maximum(jnp.abs(value), 1e-37))
-            code = jnp.round(root * factor).astype(jnp.int32)
-            coded[group, rows_at(part * 32, 32), :] = code.astype(jnp.int16)
+        return at, total
+
+    def join(step, top):
+        at, total = joined(step)
+        image[at, :] = total
+        size = jnp.abs(total)
+        return jnp.maximum(top, jnp.maximum(jnp.maximum(size[0:8], size[8:16]), jnp.maximum(size[16:24], size[24:32])))
+
+    last = USED // 8 - 1
+    top = lax.fori_loop(0, last, join, jnp.zeros((8, 128), jnp.float32))
+    at, total = joined(last)
+    real = lax.broadcasted_iota(jnp.int32, (32, 128), 0) < 4 * (MODES - 8 * last)
+    total = jnp.where(real, total, 0.0)
+    image[at, :] = total
+    size = jnp.max(jnp.abs(total), axis=0, keepdims=True)
+    top = jnp.maximum(jnp.max(top, axis=0, keepdims=True), size)
+    top = jnp.broadcast_to(jnp.max(top, axis=1, keepdims=True), (1, 128))
+    scale[...] = top * (1.0 / (TOP * TOP))
+    factor = TOP * lax.rsqrt(jnp.maximum(top, 1e-37))
+
+    def encode(step, carry):
+        value = image[rows_at(step * 32, 32), :]
+        root = value * lax.rsqrt(jnp.maximum(jnp.abs(value), 1e-37))
+        code = jnp.round(root * factor).astype(jnp.int32)
+        codes[pl.ds(step * 8, 8)] = code.reshape(8, 4, 128)
+        return carry
+
+    lax.fori_loop(0, USED // 8, encode, 0)
+
+    def prepare(group):
+        def pick(step, carry):
+            for part in range(8):
+                slot = group * slots + step * 8 + part
+                picked[rows_at(4 * slot, 4), :] = codes[slot_mode[slot]]
             return carry
 
-        lax.fori_loop(0, 4 * slots // 32, part_of, 0)
+        lax.fori_loop(0, slots // 8, pick, 0)
+        for part in range(4):
+            at = rows_at(group * 4 * slots + slots * part, slots)
+            coded[group, slots * part : slots * (part + 1), :] = picked[at, :].astype(jnp.int16)
 
     copies = []
 
     def send(place):
         peer = moved(me, OFFSETS[place])
-        for kind, (source, target) in enumerate(((coded, got), (scales, got_scales))):
+        for kind, (source, target) in enumerate(((coded.at[peer], got), (scale, got_scales))):
             copy = pltpu.make_async_remote_copy(
-                src_ref=source.at[peer],
+                src_ref=source,
                 dst_ref=target.at[me],
                 send_sem=send_sem.at[kind, place],
                 recv_sem=recv_sem.at[kind, place],
@@ -397,18 +391,18 @@
             copies.append(copy)
 
     for place in range(EARLY):
-        encode(moved(me, OFFSETS[place]))
+        prepare(moved(me, OFFSETS[place]))
     pl.semaphore_wait(barrier, len(OFFSETS))
     for place in range(EARLY - 1):
         send(place)
     for place in range(EARLY, len(OFFSETS)):
-        encode(moved(me, OFFSETS[place]))
+        prepare(moved(me, OFFSETS[place]))
         send(place - 1)
-    encode(me)
+    prepare(me)
     send(len(OFFSETS) - 1)
     own = [
         pltpu.make_async_copy(coded.at[me], got.at[me], own_sem.at[0]),
-        pltpu.make_async_copy(scales.at[me], got_scales.at[me], own_sem.at[1]),
+        pltpu.make_async_copy(scale, got_scales.at[me], own_sem.at[1]),
     ]
     for copy in own:
         copy.start()
@@ -422,7 +416,7 @@
         scale[source : source + 1, :] = got_scales[source]
 
     def widen(source, carry):
-        at = rows_at(source * rows, rows)
+        at = pl.ds(source * (rows + 1), rows)
         wide[at, :] = got[source].astype(jnp.int32).astype(jnp.float32)
         return carry
 
@@ -430,7 +424,7 @@
     factor = scale[...]
     for place in range(rows):
         slot, plane, half = place // 4, (place // 2) % 2, place % 2
-        value = wide[pl.ds(place, count, stride=rows), :]
+        value = wide[pl.ds(place, count, stride=rows + 1), :]
         out[slot, plane, :, 128 * half : 128 * half + 128] = (value * jnp.abs(value)) * factor
 
 
@@ -458,9 +452,8 @@
             pltpu.VMEM(coefficient.shape, f32),
             pltpu.VMEM((4, entries), i32),
             pltpu.VMEM((count * slots * 4, 128), f32),
-            pltpu.VMEM((count, slots * 4, 128), bf16),
-            pltpu.VMEM((count, slots * 4, 128), bf16),
-            pltpu.VMEM((count * slots, 4, 128), f32),
+            pltpu.VMEM((count, slots, 4, 128), bf16),
+            pltpu.VMEM((count * slots, 4, 128), bf16),
             pltpu.VMEM((ROWS, 128), f32),
             pltpu.VMEM((2, ROWS // 2, 128), f32),
             pltpu.VMEM((8, 128), i32),
@@ -505,11 +498,11 @@
         in_specs=[SMEM] + [VMEM] * LANES,
         out_specs=(VMEM, VMEM),
         scratch_shapes=[
-            pltpu.VMEM((HELD, 4, 128), f32),
-            pltpu.VMEM((count * slots * 4, 128), f32),
-            pltpu.VMEM((count, 4, 128), f32),
+            pltpu.VMEM((ROWS, 128), f32),
+            pltpu.VMEM((HELD, 4, 128), i32),
+            pltpu.VMEM((count * slots * 4, 128), i32),
             pltpu.VMEM((count, slots * 4, 128), i16),
-            pltpu.VMEM((count, 1, 128), f32),
+            pltpu.VMEM((1, 128), f32),
             dma((2,)),
             dma((2, len(OFFSETS))),
             dma((2, len(OFFSETS))),
@@ -528,7 +521,7 @@
             pl.BlockSpec((count, 1, 128), lambda i: (0, 0, 0)),
         ],
         out_specs=pl.BlockSpec((step, planes_here, rows_all, columns), lambda i: (i, 0, 0, 0)),
-        scratch_shapes=[pltpu.VMEM((count * 4 * step, 128), f32), pltpu.VMEM((count, 128), f32)],
+        scratch_shapes=[pltpu.VMEM((count * (4 * step + 1), 128), f32), pltpu.VMEM((count, 128), f32)],
         compiler_params=pltpu.CompilerParams(vmem_limit_bytes=12 * MIB),
         name="decode",
     )(got, got_scales)

time: 62.1 us -> 61.4 us (0.989)
  Pallas kernels: 62 us -> 61.2 us
    pallas_call x1, Pallas kernels: 3.35 us -> 2.49 us  [on_device(): pl.pallas_call(decode_kernel, out_shape=shape_of((slots, planes_here, row...]
where the time goes in v5:
time: 61.4 us; the launch traced here: 61.2 us
  Pallas kernels  61.2 us (100%)
    pallas_call x1, Pallas kernels, on_device(): pl.pallas_call(lambda *refs: gather_kernel(slabs, count, *refs), out_shap...  32.3 us
    pallas_call x1, Pallas kernels, on_device(): pl.pallas_call(lambda *refs: return_kernel(count, *refs), out_shape=(shap...  20.6 us
    pallas_call x1, Pallas kernels, on_device(): pl.pallas_call(apply_kernel, out_shape=(shape_of((ROWS, 128), f32),) * LA...  5.88 us
    pallas_call x1, Pallas kernels, on_device(): pl.pallas_call(decode_kernel, out_shape=shape_of((slots, planes_here, row...  2.49 us

profile of v5, /device:TPU:1, one launch (start us, length us, event | category | flops | bytes accessed | tf_op | source)
XLA Modules:
  0.0 61.2 jit_solution(15116617808643071863)
XLA Ops:
  0.0 0.0 copy-start
  0.0 32.3 %gather.1 = (f32[2048,128]{1,0:T(8,128)S(1)}, f32[16384,128]{1,0:T(8,128)S(1)}, s32[1,2640]{1,0:T(1,128)S(1)}, f32[1,2640]{1,0:T(1,128)S(1)}) custom-call(s32[1024]{0:T(1024)} %refs_0_.3, bf16[32,2,32,256]{3,2,1,0:T(8,128)(2,1)} %refs_1_.1, f32[9,2,32,256]{3,2,1,0:T(8,128)} %refs_2_.1, s32[4,2640]{1,0:T(4,128)} %bitcast.1), custom_call_target="tpu_custom_call" | custom-call | tf_op jit(solution)/shard_map/gather/pallas_call | solution.py:439
  32.3 5.9 %apply.1 = (f32[2048,128]{1,0:T(8,128)S(1)}, f32[2048,128]{1,0:T(8,128)S(1)}) custom-call(s32[1,2640]{1,0:T(1,128)S(1)} %get-tuple-element.13.address, f32[1,2640]{1,0:T(1,128)S(1)} %get-tuple-element.14.weight, f32[2048,128]{1,0:T(8,128)S(1)} %get-tuple-element.15.start, f32[16384,128]{1,0:T(8,128)S(1)} %get-tuple-element.16.image), custom_call_target="tpu_custom_call", output_to_operand_aliasing={{0}: (2, {})} | custom-call | tf_op jit(solution)/shard_map/apply/pallas_call | solution.py:485
  38.2 0.0 copy-done
  38.2 20.6 %give.1 = (s16[32,128,128]{2,1,0:T(8,128)(2,1)S(1)}, f32[32,1,128]{2,1,0:T(1,128)S(1)}) custom-call(s32[1024]{0:T(1024)S(1)} %copy-done, f32[2048,128]{1,0:T(8,128)S(1)} %get-tuple-element.17.refs_1_, f32[2048,128]{1,0:T(8,128)S(1)} %get-tuple-element.18.refs_2_), custom_call_target="tpu_custom_call" | custom-call | tf_op jit(solution)/shard_map/give/pallas_call | solution.py:495
  58.8 2.5 %decode.1 = f32[32,2,32,256]{3,2,1,0:T(8,128)} custom-call(s16[32,128,128]{2,1,0:T(8,128)(2,1)S(1)} %get-tuple-element.19.got, f32[32,1,128]{2,1,0:T(1,128)S(1)} %get-tuple-element.20.got_scales), custom_call_target="tpu_custom_call" | custom-call | tf_op jit(solution)/shard_map/decode/pallas_call | solution.py:515
Async XLA Ops:
  0.0 38.2 %copy-start = (s32[1024]{0:T(1024)S(1)}, s32[1024]{0:T(1024)}, u32[]{:S(2)}) copy-start(s32[1024]{0:T(1024)} %refs_0_.3) | copy-start | bytes 12292

commit v6 on v5

--- a/solution.py
+++ b/solution.py
@@ -9,12 +9,9 @@
 HELD = 512
 TERMS = 9
 ROWS = 4 * HELD
-LANES = 2
-UNROLL = 12
 CHUNKS = 8
 USED = 496
 TOP = 32700.0
-EARLY = 12
 SIDE = 4
 MESH = pl.DeviceIdType.MESH
 VMEM = pl.BlockSpec(memory_space=pltpu.VMEM)
@@ -66,11 +63,13 @@
 
 def gather_kernel(
     slabs, count, slot_mode_hbm, field_hbm, coefficient_hbm, couplings_hbm,
-    start, image, address, weight,
+    got, got_scales,
     slot_mode, field, coefficient, couplings, turned, blocks, raw, wide, wide_planes, found, inverse,
     held, planes, row_low, row_high, plane_low, plane_high, near, coef_low, coef_high,
-    faces, plane_rows, column_low, column_high,
-    load_sem, own_sem, send_sem, recv_sem, halo_send, halo_recv,
+    faces, plane_rows, column_low, column_high, start, image, running,
+    targets, words, ranks, order, firsts, target_list, word_list, rank_list, order_list, first_list,
+    total, codes, picked, coded, scale,
+    load_sem, own_sem, send_sem, recv_sem, halo_send, halo_recv, give_send, give_recv,
 ):
     slab, me = lax.axis_index("slab"), lax.axis_index("mode")
     slots = field.shape[0]
@@ -125,6 +124,18 @@
 
     lax.fori_loop(0, count, narrow_block, 0)
 
+    for load in others:
+        load.wait()
+    for shift in range(3):
+        row = jnp.clip(me + shift - 1, 0, count - 1)
+        for term in range(TERMS):
+            for part in range(4):
+                plane, half = part // 2, part % 2
+                tile = coefficient[term, plane, rows_at(row // 8 * 8, 8), 128 * half : 128 * half + 128]
+                value = pltpu.roll(tile, lax.rem(8 - row % 8, 8), 0)[0:1]
+                near[shift, term, part : part + 1, :] = value
+                near[shift, term, part + 4 : part + 5, :] = value
+
     pl.semaphore_wait(barrier, len(OFFSETS) + 2)
     copies = []
     for place, offset in enumerate(OFFSETS):
@@ -141,21 +152,33 @@
         copies.append(copy)
     own = pltpu.make_async_copy(blocks.at[me], raw.at[pl.ds(me * slots, slots)], own_sem.at[0])
     own.start()
-    for load in others:
-        load.wait()
-
-    for shift in range(3):
-        row = jnp.clip(me + shift - 1, 0, count - 1)
-        for term in range(TERMS):
-            for part in range(4):
-                plane, half = part // 2, part % 2
-                tile = coefficient[term, plane, rows_at(row // 8 * 8, 8), 128 * half : 128 * half + 128]
-                value = pltpu.roll(tile, lax.rem(8 - row % 8, 8), 0)[0:1]
-                near[shift, term, part : part + 1, :] = value
-                near[shift, term, part + 4 : part + 5, :] = value
-
     ids = sub * 128 + lane
 
+    def moving(place, source, target):
+        copy = pltpu.make_async_copy(source, target, own_sem.at[1 + place])
+        copy.start()
+        return copy
+
+    entries = couplings.shape[1]
+    whole, rest = entries // 128, entries % 128
+    tiles = targets.shape[0] // 8
+    for row in range(whole + 1):
+        size = 128 if row < whole else rest
+        if size:
+            columns = slice(128 * row, 128 * row + size)
+            targets[row : row + 1, 0:size] = couplings[0:1, columns]
+            words[row : row + 1, 0:size] = (
+                couplings[3:4, columns] * (8 * HELD) + (couplings[2:3, columns] - 1) * HELD + couplings[1:2, columns]
+            )
+    list_rows = pl.cdiv(entries, 128)
+    keys = []
+    for tile in range(tiles):
+        place = ids + 1024 * tile
+        key = targets[8 * tile : 8 * tile + 8, :] * (8 * HELD) + place
+        keys.append(jnp.where(place < entries, key, (1 << 30) + place))
+        targets[8 * tile : 8 * tile + 8, :] = keys[-1]
+        value = words[8 * tile : 8 * tile + 8, :]
+        words[8 * tile : 8 * tile + 8, :] = jnp.where(place < entries, value, 0)
     def find(step, place):
         for part in range(8):
             slot = step * 8 + part
@@ -163,6 +186,7 @@
         return place
 
     found[...] = lax.fori_loop(0, slots * count // 8, find, jnp.zeros((8, 128), jnp.int32))
+    moves = [moving(0, targets, target_list), moving(1, words, word_list)]
     sent = []
 
     def send(place, source, target, peer):
@@ -180,14 +204,24 @@
     send(4 * CHUNKS, near.at[1], coef_low, right)
     send(4 * CHUNKS + 1, near.at[1], coef_high, left)
     own_coef = near.at[1]
-    first = couplings[0:1, :] * 4 + (couplings[2:3, :] - 1) * ROWS
-    other = couplings[1:2, :] * 4 + (couplings[2:3, :] - 1) * ROWS
-    address[...] = other + first * (1 << 16)
-    weight[...] = couplings[3:4, :].astype(jnp.float32) * 0.125
-
-    listed = pltpu.make_async_copy(found, inverse, own_sem.at[1])
-    listed.start()
-    listed.wait()
+    floors = (sub * (USED // 4) + lane + 1) * (8 * HELD)
+
+    def rank(step, carry):
+        for part in range(128):
+            key = target_list[step, part]
+            carry = tuple(
+                jnp.where(value > key, count_of + 1, count_of) for value, count_of in zip(keys + [floors], carry)
+            )
+        return carry
+
+    none = jnp.zeros((8, 128), jnp.int32)
+    for copy in moves:
+        copy.wait()
+    counted = lax.fori_loop(0, list_rows, rank, (none,) * (tiles + 1))
+    for tile in range(tiles):
+        ranks[8 * tile : 8 * tile + 8, :] = counted[tile]
+    firsts[...] = counted[tiles]
+    moves = [moving(2, found, inverse)]
     for copy in sent:
         copy.wait()
     sent.clear()
@@ -200,6 +234,22 @@
         for place, value in enumerate(around):
             faces[6 * term + place] = 0.5 * (middle + value)
 
+    moves += [moving(3, ranks, rank_list), moving(4, firsts, first_list)]
+    for copy in moves:
+        copy.wait()
+
+    def arrange(step, carry):
+        for part in range(128):
+            place, word = rank_list[step, part], word_list[step, part]
+            carry = tuple(
+                jnp.where(spot == place, word, value) for spot, value in zip(spots, carry)
+            )
+        return carry
+
+    spots = [ids + 1024 * tile for tile in range(tiles)]
+    arranged = lax.fori_loop(0, list_rows, arrange, (none,) * tiles)
+    for tile in range(tiles):
+        order[8 * tile : 8 * tile + 8, :] = arranged[tile]
     own.wait()
     for copy in copies:
         copy.wait()
@@ -249,6 +299,8 @@
     lax.fori_loop(0, 4, shift_columns, 0)
     send_chunk(CHUNKS - 1)
     lax.fori_loop(4, USED // 16, shift_columns, 0)
+
+    ordered = moving(5, order, order_list)
 
     def interleave(step, carry):
         at = rows_at(step * 16, 16)
@@ -272,17 +324,18 @@
             middle = wide[at, :]
             around = plane_neighbours(middle, plane_rows[at, :], front) + (column_low[at, :], column_high[at, :])
             around = around + (low[part] * mask_low, high[part] * mask_high)
-            halves.append((base, [middle - value for value in around]))
+            halves.append((base, 2 * half, [middle - value for value in around]))
         for term in range(TERMS):
             face = [faces[6 * term + place] for place in range(6)]
-            for base, drops in halves:
+            for base, base_mode, drops in halves:
                 total = face[0] * drops[0]
                 for place in range(1, 6):
                     total = total + face[place] * drops[place]
                 if term == 0:
                     start[pl.ds(base, 8), :] = total
                 else:
-                    image[rows_at((term - 1) * ROWS + base, 8), :] = total
+                    at = (term - 1) * HELD + step * 4 + base_mode
+                    image[pl.ds(at, 2)] = total.reshape(2, 4, 128)
         return carry
 
     for chunk in range(CHUNKS):
@@ -291,70 +344,52 @@
         lax.fori_loop(ends[chunk] // 8, ends[chunk + 1] // 8, interleave, 0)
         lax.fori_loop(ends[chunk] // 4, ends[chunk + 1] // 4, stencil, 0)
 
-
-def apply_kernel(address, weight, start, image, *sums):
-    def clear(step, carry):
-        at = rows_at(step * 32, 32)
-        for total in sums[1:]:
-            total[at, :] = jnp.zeros((32, 128), jnp.float32)
-        return carry
-
-    lax.fori_loop(0, ROWS // 32, clear, 0)
-
     def couple(step, carry):
-        for part in range(UNROLL):
-            place = 2 * (step * UNROLL + part)
-            both = address[0, place]
-            low, high = lax.bitwise_and(both, 0xFFFF), lax.shift_right_logical(both, 16)
-            at_low = pl.ds(pl.multiple_of(lax.bitwise_and(low, ROWS - 1), 4), 4)
-            at_high = pl.ds(pl.multiple_of(lax.bitwise_and(high, ROWS - 1), 4), 4)
-            factor = weight[0, place]
-            total = sums[part % LANES]
-            to_high = total[at_high, :] + factor * image[pl.ds(pl.multiple_of(low, 4), 4), :]
-            to_low = total[at_low, :] + factor * image[pl.ds(pl.multiple_of(high, 4), 4), :]
-            total[at_high, :] = to_high
-            total[at_low, :] = to_low
-        return carry
-
-    lax.fori_loop(0, address.shape[1] // (2 * UNROLL), couple, 0)
-
-
-def return_kernel(count, slot_mode, *refs):
-    sums, refs = refs[:LANES], refs[LANES:]
-    got, got_scales, image, codes, picked, coded, scale, own_sem, send_sem, recv_sem = refs
-    slab, me = lax.axis_index("slab"), lax.axis_index("mode")
-    slots = slot_mode.shape[0] // count
-    barrier = pltpu.get_barrier_semaphore()
-    for offset in OFFSETS:
-        pl.semaphore_signal(barrier, inc=1, device_id=(slab, moved(me, offset)), device_id_type=MESH)
-
-    def joined(step):
-        at = rows_at(step * 32, 32)
-        total = sums[0][at, :]
-        for other in sums[1:]:
-            total = total + other[at, :]
-        return at, total
-
-    def join(step, top):
-        at, total = joined(step)
-        image[at, :] = total
-        size = jnp.abs(total)
+        values = []
+        for part in range(128):
+            word = order_list[step, part]
+            weight = jnp.full((4, 128), lax.shift_right_arithmetic(word, 12), jnp.int32).astype(jnp.float32)
+            value = image[lax.bitwise_and(word, 8 * HELD - 1)]
+            values.append((weight * 0.125) * value)
+        for part in range(0, 128, 4):
+            one, two, three, four = values[part : part + 4]
+            pair = one + two
+            at = step * 128 + part
+            running[at] = carry
+            running[at + 1] = carry + one
+            running[at + 2] = carry + pair
+            running[at + 3] = carry + (pair + three)
+            carry = carry + (pair + (three + four))
+        return carry
+
+    ordered.wait()
+    running[128 * list_rows] = lax.fori_loop(0, list_rows, couple, jnp.zeros((4, 128), jnp.float32))
+
+    def spread(step, below_it):
+        for part in range(USED // 4):
+            mode = step * (USED // 4) + part
+            at = first_list[step, part]
+            up_to = running[at]
+            rows = rows_at(4 * mode, 4)
+            total[rows, :] = start[rows, :] + (up_to - below_it)
+            below_it = up_to
+        return below_it
+
+    lax.fori_loop(0, 4, spread, jnp.zeros((4, 128), jnp.float32))
+
+    def largest(step, top):
+        size = jnp.abs(total[rows_at(step * 32, 32), :])
         return jnp.maximum(top, jnp.maximum(jnp.maximum(size[0:8], size[8:16]), jnp.maximum(size[16:24], size[24:32])))
 
-    last = USED // 8 - 1
-    top = lax.fori_loop(0, last, join, jnp.zeros((8, 128), jnp.float32))
-    at, total = joined(last)
-    real = lax.broadcasted_iota(jnp.int32, (32, 128), 0) < 4 * (MODES - 8 * last)
-    total = jnp.where(real, total, 0.0)
-    image[at, :] = total
-    size = jnp.max(jnp.abs(total), axis=0, keepdims=True)
-    top = jnp.maximum(jnp.max(top, axis=0, keepdims=True), size)
-    top = jnp.broadcast_to(jnp.max(top, axis=1, keepdims=True), (1, 128))
+    total[4 * MODES : 4 * MODES + 4, :] = jnp.zeros((4, 128), jnp.float32)
+    top = lax.fori_loop(0, USED // 8, largest, jnp.zeros((8, 128), jnp.float32))
+    top = jnp.max(jnp.max(top, axis=0, keepdims=True), axis=1, keepdims=True)
+    top = jnp.broadcast_to(top, (1, 128))
     scale[...] = top * (1.0 / (TOP * TOP))
     factor = TOP * lax.rsqrt(jnp.maximum(top, 1e-37))
 
     def encode(step, carry):
-        value = image[rows_at(step * 32, 32), :]
+        value = total[rows_at(step * 32, 32), :]
         root = value * lax.rsqrt(jnp.maximum(jnp.abs(value), 1e-37))
         code = jnp.round(root * factor).astype(jnp.int32)
         codes[pl.ds(step * 8, 8)] = code.reshape(8, 4, 128)
@@ -363,46 +398,42 @@
     lax.fori_loop(0, USED // 8, encode, 0)
 
     def prepare(group):
-        def pick(step, carry):
+        def pick_codes(step, carry):
             for part in range(8):
                 slot = group * slots + step * 8 + part
                 picked[rows_at(4 * slot, 4), :] = codes[slot_mode[slot]]
             return carry
 
-        lax.fori_loop(0, slots // 8, pick, 0)
+        lax.fori_loop(0, slots // 8, pick_codes, 0)
         for part in range(4):
             at = rows_at(group * 4 * slots + slots * part, slots)
             coded[group, slots * part : slots * (part + 1), :] = picked[at, :].astype(jnp.int16)
 
     copies = []
 
-    def send(place):
+    def give(place):
         peer = moved(me, OFFSETS[place])
         for kind, (source, target) in enumerate(((coded.at[peer], got), (scale, got_scales))):
             copy = pltpu.make_async_remote_copy(
                 src_ref=source,
                 dst_ref=target.at[me],
-                send_sem=send_sem.at[kind, place],
-                recv_sem=recv_sem.at[kind, place],
+                send_sem=give_send.at[kind, place],
+                recv_sem=give_recv.at[kind, place],
                 device_id=(slab, peer),
                 device_id_type=MESH,
             )
             copy.start()
             copies.append(copy)
 
-    for place in range(EARLY):
+    prepare(moved(me, OFFSETS[0]))
+    for place in range(1, len(OFFSETS)):
         prepare(moved(me, OFFSETS[place]))
-    pl.semaphore_wait(barrier, len(OFFSETS))
-    for place in range(EARLY - 1):
-        send(place)
-    for place in range(EARLY, len(OFFSETS)):
-        prepare(moved(me, OFFSETS[place]))
-        send(place - 1)
+        give(place - 1)
     prepare(me)
-    send(len(OFFSETS) - 1)
+    give(len(OFFSETS) - 1)
     own = [
-        pltpu.make_async_copy(coded.at[me], got.at[me], own_sem.at[0]),
-        pltpu.make_async_copy(scale, got_scales.at[me], own_sem.at[1]),
+        pltpu.make_async_copy(coded.at[me], got.at[me], own_sem.at[7]),
+        pltpu.make_async_copy(scale, got_scales.at[me], own_sem.at[8]),
     ]
     for copy in own:
         copy.start()
@@ -435,17 +466,13 @@
     f32, bf16, i16, i32 = jnp.float32, jnp.bfloat16, jnp.int16, jnp.int32
     dma = pltpu.SemaphoreType.DMA
     halo = 4 * CHUNKS + 2
-
-    start, image, address, weight = pl.pallas_call(
+    places = pl.cdiv(entries, 1024) * 8
+
+    got, got_scales = pl.pallas_call(
         lambda *refs: gather_kernel(slabs, count, *refs),
-        out_shape=(
-            shape_of((ROWS, 128), f32),
-            shape_of(((TERMS - 1) * ROWS, 128), f32),
-            shape_of((1, entries), i32),
-            shape_of((1, entries), f32),
-        ),
+        out_shape=(shape_of((count, slots * 4, 128), i16), shape_of((count, 1, 128), f32)),
         in_specs=[HBM] * 4,
-        out_specs=(VMEM,) * 4,
+        out_specs=(VMEM,) * 2,
         scratch_shapes=[
             pltpu.SMEM(slot_mode.shape, i32),
             pltpu.VMEM(field.shape, bf16),
@@ -471,45 +498,32 @@
             pltpu.VMEM((ROWS, 128), f32),
             pltpu.VMEM((ROWS, 128), f32),
             pltpu.VMEM((ROWS, 128), f32),
-            dma((7,)),
-            dma((2,)),
-            dma((len(OFFSETS),)),
-            dma((len(OFFSETS),)),
-            dma((halo,)),
-            dma((halo,)),
-        ],
-        compiler_params=pltpu.CompilerParams(collective_id=0, has_side_effects=True, vmem_limit_bytes=30 * MIB),
-        name="gather",
-    )(*(pltpu.with_memory_space_constraint(value, pltpu.HBM) for value in (slot_mode, field, coefficient, couplings.T)))
-
-    sums = pl.pallas_call(
-        apply_kernel,
-        out_shape=(shape_of((ROWS, 128), f32),) * LANES,
-        in_specs=[SMEM] * 2 + [VMEM] * 2,
-        out_specs=(VMEM,) * LANES,
-        input_output_aliases={2: 0},
-        compiler_params=pltpu.CompilerParams(vmem_limit_bytes=16 * MIB),
-        name="apply",
-    )(address, weight, start, image)
-
-    got, got_scales = pl.pallas_call(
-        lambda *refs: return_kernel(count, *refs),
-        out_shape=(shape_of((count, slots * 4, 128), i16), shape_of((count, 1, 128), f32)),
-        in_specs=[SMEM] + [VMEM] * LANES,
-        out_specs=(VMEM, VMEM),
-        scratch_shapes=[
+            pltpu.VMEM((ROWS, 128), f32),
+            pltpu.VMEM(((TERMS - 1) * HELD, 4, 128), f32),
+            pltpu.VMEM((128 * pl.cdiv(entries, 128) + 8, 4, 128), f32),
+        ]
+        + [pltpu.VMEM((places, 128), i32)] * 4
+        + [pltpu.VMEM((8, 128), i32)]
+        + [pltpu.SMEM((places, 128), i32)] * 4
+        + [
+            pltpu.SMEM((8, 128), i32),
             pltpu.VMEM((ROWS, 128), f32),
             pltpu.VMEM((HELD, 4, 128), i32),
             pltpu.VMEM((count * slots * 4, 128), i32),
             pltpu.VMEM((count, slots * 4, 128), i16),
             pltpu.VMEM((1, 128), f32),
-            dma((2,)),
+            dma((7,)),
+            dma((9,)),
+            dma((len(OFFSETS),)),
+            dma((len(OFFSETS),)),
+            dma((halo,)),
+            dma((halo,)),
             dma((2, len(OFFSETS))),
             dma((2, len(OFFSETS))),
         ],
-        compiler_params=pltpu.CompilerParams(collective_id=2, has_side_effects=True, vmem_limit_bytes=12 * MIB),
-        name="give",
-    )(slot_mode, *sums)
+        compiler_params=pltpu.CompilerParams(collective_id=0, has_side_effects=True, vmem_limit_bytes=48 * MIB),
+        name="gather",
+    )(*(pltpu.with_memory_space_constraint(value, pltpu.HBM) for value in (slot_mode, field, coefficient, couplings.T)))
 
     step = 8
     return pl.pallas_call(

time: 61.4 us -> 58 us (0.945)
  Pallas kernels: 61.2 us -> 57.8 us
    pallas_call x2 -> x0, Pallas kernels: 26.5 us -> none  [the longest x1 20.6 us: on_device(): pl.pallas_call(lambda *refs: return_kernel(count, *refs), out_shape=(shap...]
    pallas_call x1, Pallas kernels: 32.3 us -> 55.4 us  [on_device(): pl.pallas_call(lambda *refs: gather_kernel(slabs, count, *refs), out_shap...]
where the time goes in v6:
time: 58 us; the launch traced here: 57.8 us
  Pallas kernels  57.8 us (100%)
    pallas_call x1, Pallas kernels, on_device(): pl.pallas_call(lambda *refs: gather_kernel(slabs, count, *refs), out_shap...  55.4 us
    pallas_call x1, Pallas kernels, on_device(): pl.pallas_call(decode_kernel, out_shape=shape_of((slots, planes_here, row...  2.49 us

profile of v6, /device:TPU:1, one launch (start us, length us, event | category | flops | bytes accessed | tf_op | source)
XLA Modules:
  0.0 57.8 jit_solution(9570104871607097874)
XLA Ops:
  0.0 55.4 %gather.1 = (s16[32,128,128]{2,1,0:T(8,128)(2,1)S(1)}, f32[32,1,128]{2,1,0:T(1,128)S(1)}) custom-call(s32[1024]{0:T(1024)} %refs_0_.1, bf16[32,2,32,256]{3,2,1,0:T(8,128)(2,1)} %refs_1_.1, f32[9,2,32,256]{3,2,1,0:T(8,128)} %refs_2_.1, s32[4,2640]{1,0:T(4,128)} %bitcast.1), custom_call_target="tpu_custom_call" | custom-call | tf_op jit(solution)/shard_map/gather/pallas_call | solution.py:471
  55.4 2.5 %decode.1 = f32[32,2,32,256]{3,2,1,0:T(8,128)} custom-call(s16[32,128,128]{2,1,0:T(8,128)(2,1)S(1)} %get-tuple-element.7.got, f32[32,1,128]{2,1,0:T(1,128)S(1)} %get-tuple-element.8.got_scales), custom_call_target="tpu_custom_call" | custom-call | tf_op jit(solution)/shard_map/decode/pallas_call | solution.py:529

commit v7 on v6

--- a/solution.py
+++ b/solution.py
@@ -11,6 +11,8 @@
 ROWS = 4 * HELD
 CHUNKS = 8
 USED = 496
+LIST_ROWS = 21
+SPREAD = 99
 TOP = 32700.0
 SIDE = 4
 MESH = pl.DeviceIdType.MESH
@@ -67,9 +69,9 @@
     slot_mode, field, coefficient, couplings, turned, blocks, raw, wide, wide_planes, found, inverse,
     held, planes, row_low, row_high, plane_low, plane_high, near, coef_low, coef_high,
     faces, plane_rows, column_low, column_high, start, image, running,
-    targets, words, ranks, order, firsts, target_list, word_list, rank_list, order_list, first_list,
+    targets, words, ranks, order, firsts, target_list, word_list, rank_list, first_list,
     total, codes, picked, coded, scale,
-    load_sem, own_sem, send_sem, recv_sem, halo_send, halo_recv, give_send, give_recv,
+    load_sem, own_sem, send_sem, recv_sem, halo_send, halo_recv, give_send, give_recv, *order_lists,
 ):
     slab, me = lax.axis_index("slab"), lax.axis_index("mode")
     slots = field.shape[0]
@@ -170,7 +172,6 @@
             words[row : row + 1, 0:size] = (
                 couplings[3:4, columns] * (8 * HELD) + (couplings[2:3, columns] - 1) * HELD + couplings[1:2, columns]
             )
-    list_rows = pl.cdiv(entries, 128)
     keys = []
     for tile in range(tiles):
         place = ids + 1024 * tile
@@ -204,7 +205,7 @@
     send(4 * CHUNKS, near.at[1], coef_low, right)
     send(4 * CHUNKS + 1, near.at[1], coef_high, left)
     own_coef = near.at[1]
-    floors = (sub * (USED // 4) + lane + 1) * (8 * HELD)
+    floors = (sub * SPREAD + lane + 1) * (8 * HELD)
 
     def rank(step, carry):
         for part in range(128):
@@ -217,7 +218,7 @@
     none = jnp.zeros((8, 128), jnp.int32)
     for copy in moves:
         copy.wait()
-    counted = lax.fori_loop(0, list_rows, rank, (none,) * (tiles + 1))
+    counted = lax.fori_loop(0, LIST_ROWS, rank, (none,) * (tiles + 1))
     for tile in range(tiles):
         ranks[8 * tile : 8 * tile + 8, :] = counted[tile]
     firsts[...] = counted[tiles]
@@ -246,8 +247,11 @@
             )
         return carry
 
-    spots = [ids + 1024 * tile for tile in range(tiles)]
-    arranged = lax.fori_loop(0, list_rows, arrange, (none,) * tiles)
+    spots = []
+    for tile in range(tiles):
+        row = sub + 8 * tile
+        spots.append(jnp.where(row < LIST_ROWS, lane * LIST_ROWS + row, -1))
+    arranged = lax.fori_loop(0, LIST_ROWS, arrange, (none,) * tiles)
     for tile in range(tiles):
         order[8 * tile : 8 * tile + 8, :] = arranged[tile]
     own.wait()
@@ -300,7 +304,7 @@
     send_chunk(CHUNKS - 1)
     lax.fori_loop(4, USED // 16, shift_columns, 0)
 
-    ordered = moving(5, order, order_list)
+    ordered = [moving(5 + row, order.at[row : row + 1], order_lists[row]) for row in range(LIST_ROWS)]
 
     def interleave(step, carry):
         at = rows_at(step * 16, 16)
@@ -345,44 +349,41 @@
         lax.fori_loop(ends[chunk] // 4, ends[chunk + 1] // 4, stencil, 0)
 
     def couple(step, carry):
-        values = []
-        for part in range(128):
-            word = order_list[step, part]
-            weight = jnp.full((4, 128), lax.shift_right_arithmetic(word, 12), jnp.int32).astype(jnp.float32)
-            value = image[lax.bitwise_and(word, 8 * HELD - 1)]
-            values.append((weight * 0.125) * value)
-        for part in range(0, 128, 4):
-            one, two, three, four = values[part : part + 4]
-            pair = one + two
-            at = step * 128 + part
-            running[at] = carry
-            running[at + 1] = carry + one
-            running[at + 2] = carry + pair
-            running[at + 3] = carry + (pair + three)
-            carry = carry + (pair + (three + four))
-        return carry
-
-    ordered.wait()
-    running[128 * list_rows] = lax.fori_loop(0, list_rows, couple, jnp.zeros((4, 128), jnp.float32))
-
-    def spread(step, below_it):
-        for part in range(USED // 4):
-            mode = step * (USED // 4) + part
-            at = first_list[step, part]
-            up_to = running[at]
-            rows = rows_at(4 * mode, 4)
-            total[rows, :] = start[rows, :] + (up_to - below_it)
+        for lot in range(2):
+            column = 2 * step + lot
+            values = []
+            for part in range(LIST_ROWS):
+                word = order_lists[part][0, column]
+                weight = lax.shift_right_arithmetic(jnp.full((4, 128), word, jnp.int32), 12).astype(jnp.float32)
+                value = image[lax.bitwise_and(word, 8 * HELD - 1)]
+                values.append((weight * 0.125) * value)
+            for part in range(0, LIST_ROWS, 3):
+                one, two, three = values[part : part + 3]
+                at = column * LIST_ROWS + part
+                running[at] = carry
+                running[at + 1] = carry + one
+                running[at + 2] = carry + (one + two)
+                carry = carry + (one + two + three)
+        return carry
+
+    for copy in ordered:
+        copy.wait()
+    running[128 * LIST_ROWS] = lax.fori_loop(0, 64, couple, jnp.zeros((4, 128), jnp.float32))
+
+    def spread(step, carry):
+        below_it, top = carry
+        for part in range(SPREAD):
+            up_to = running[first_list[step, part]]
+            rows = rows_at(4 * (step * SPREAD + part), 4)
+            value = start[rows, :] + (up_to - below_it)
+            total[rows, :] = value
             below_it = up_to
-        return below_it
-
-    lax.fori_loop(0, 4, spread, jnp.zeros((4, 128), jnp.float32))
-
-    def largest(step, top):
-        size = jnp.abs(total[rows_at(step * 32, 32), :])
-        return jnp.maximum(top, jnp.maximum(jnp.maximum(size[0:8], size[8:16]), jnp.maximum(size[16:24], size[24:32])))
-
-    total[4 * MODES : 4 * MODES + 4, :] = jnp.zeros((4, 128), jnp.float32)
-    top = lax.fori_loop(0, USED // 8, largest, jnp.zeros((8, 128), jnp.float32))
+            top = jnp.maximum(top, jnp.abs(value))
+        return below_it, top
+
+    blank = jnp.zeros((4, 128), jnp.float32)
+    top = lax.fori_loop(0, MODES // SPREAD, spread, (blank, blank))[1]
+    total[4 * MODES : 4 * MODES + 4, :] = blank
     top = jnp.max(jnp.max(top, axis=0, keepdims=True), axis=1, keepdims=True)
     top = jnp.broadcast_to(top, (1, 128))
     scale[...] = top * (1.0 / (TOP * TOP))
@@ -432,8 +433,8 @@
     prepare(me)
     give(len(OFFSETS) - 1)
     own = [
-        pltpu.make_async_copy(coded.at[me], got.at[me], own_sem.at[7]),
-        pltpu.make_async_copy(scale, got_scales.at[me], own_sem.at[8]),
+        pltpu.make_async_copy(coded.at[me], got.at[me], own_sem.at[6 + LIST_ROWS]),
+        pltpu.make_async_copy(scale, got_scales.at[me], own_sem.at[7 + LIST_ROWS]),
     ]
     for copy in own:
         copy.start()
@@ -500,11 +501,11 @@
             pltpu.VMEM((ROWS, 128), f32),
             pltpu.VMEM((ROWS, 128), f32),
             pltpu.VMEM(((TERMS - 1) * HELD, 4, 128), f32),
-            pltpu.VMEM((128 * pl.cdiv(entries, 128) + 8, 4, 128), f32),
+            pltpu.VMEM((128 * LIST_ROWS + 8, 4, 128), f32),
         ]
         + [pltpu.VMEM((places, 128), i32)] * 4
         + [pltpu.VMEM((8, 128), i32)]
-        + [pltpu.SMEM((places, 128), i32)] * 4
+        + [pltpu.SMEM((places, 128), i32)] * 3
         + [
             pltpu.SMEM((8, 128), i32),
             pltpu.VMEM((ROWS, 128), f32),
@@ -513,14 +514,15 @@
             pltpu.VMEM((count, slots * 4, 128), i16),
             pltpu.VMEM((1, 128), f32),
             dma((7,)),
-            dma((9,)),
+            dma((8 + LIST_ROWS,)),
             dma((len(OFFSETS),)),
             dma((len(OFFSETS),)),
             dma((halo,)),
             dma((halo,)),
             dma((2, len(OFFSETS))),
             dma((2, len(OFFSETS))),
-        ],
+        ]
+        + [pltpu.SMEM((1, 128), i32)] * LIST_ROWS,
         compiler_params=pltpu.CompilerParams(collective_id=0, has_side_effects=True, vmem_limit_bytes=48 * MIB),
         name="gather",
     )(*(pltpu.with_memory_space_constraint(value, pltpu.HBM) for value in (slot_mode, field, coefficient, couplings.T)))

time: 58 us -> 56.9 us (0.981)
  Pallas kernels: 57.8 us -> 56.8 us
    pallas_call x1, Pallas kernels: 55.4 us -> 54.3 us  [on_device(): pl.pallas_call(lambda *refs: gather_kernel(slabs, count, *refs), out_shap...]
where the time goes in v7:
time: 56.9 us; the launch traced here: 56.8 us
  Pallas kernels  56.8 us (100%)
    pallas_call x1, Pallas kernels, on_device(): pl.pallas_call(lambda *refs: gather_kernel(slabs, count, *refs), out_shap...  54.3 us
    pallas_call x1, Pallas kernels, on_device(): pl.pallas_call(decode_kernel, out_shape=shape_of((slots, planes_here, row...  2.49 us

profile of v7, /device:TPU:1, one launch (start us, length us, event | category | flops | bytes accessed | tf_op | source)
XLA Modules:
  0.0 56.8 jit_solution(18103611087073651705)
XLA Ops:
  0.0 54.3 %gather.1 = (s16[32,128,128]{2,1,0:T(8,128)(2,1)S(1)}, f32[32,1,128]{2,1,0:T(1,128)S(1)}) custom-call(s32[1024]{0:T(1024)} %refs_0_.1, bf16[32,2,32,256]{3,2,1,0:T(8,128)(2,1)} %refs_1_.1, f32[9,2,32,256]{3,2,1,0:T(8,128)} %refs_2_.1, s32[4,2640]{1,0:T(4,128)} %bitcast.1), custom_call_target="tpu_custom_call" | custom-call | tf_op jit(solution)/shard_map/gather/pallas_call | solution.py:472
  54.3 2.5 %decode.1 = f32[32,2,32,256]{3,2,1,0:T(8,128)} custom-call(s16[32,128,128]{2,1,0:T(8,128)(2,1)S(1)} %get-tuple-element.7.got, f32[32,1,128]{2,1,0:T(1,128)S(1)} %get-tuple-element.8.got_scales), custom_call_target="tpu_custom_call" | custom-call | tf_op jit(solution)/shard_map/decode/pallas_call | solution.py:531

commit v8 on v7

v8 whole, which is shorter than its diff:
```python
import jax
import jax.numpy as jnp
from jax import lax
from jax.experimental import pallas as pl
from jax.experimental.pallas import tpu as pltpu
from jax.sharding import PartitionSpec as P

MODES = 495
HELD = 512
TERMS = 9
ROWS = 4 * HELD
STRIDE = 33
CHUNKS = 4
USED = 496
LIST_ROWS = 21
SPREAD = 99
TOP = 32700.0
SIDE = 4
MESH = pl.DeviceIdType.MESH
VMEM = pl.BlockSpec(memory_space=pltpu.VMEM)
SMEM = pl.BlockSpec(memory_space=pltpu.SMEM)
HBM = pl.BlockSpec(memory_space=pltpu.HBM)
MIB = 1024 * 1024


def far_first():
    offsets = [(x, y, core) for x in range(SIDE) for y in range(SIDE) for core in range(2)]
    hops = lambda offset: min(offset[0], SIDE - offset[0]) + min(offset[1], SIDE - offset[1])
    return sorted(offsets[1:], key=hops, reverse=True)


OFFSETS = far_first()


def shape_of(shape, dtype):
    return jax.ShapeDtypeStruct(shape, dtype)


def moved(me, offset, sign=1):
    x, y, core = me // (2 * SIDE), (me // 2) % SIDE, me % 2
    x = lax.rem(x + (sign * offset[0]) % SIDE, SIDE)
    y = lax.rem(y + (sign * offset[1]) % SIDE, SIDE)
    return (x * SIDE + y) * 2 + lax.rem(core + offset[2], 2)


def rows_at(start, size):
    return pl.ds(pl.multiple_of(start, size), size)


def column_neighbours(centre, second, lane):
    zero = jnp.zeros_like(centre)
    low = pltpu.roll(centre, 1, 1)
    high = pltpu.roll(centre, 127, 1)
    return (
        jnp.where(lane == 0, jnp.where(second, pltpu.roll(low, 1, 0), zero), low),
        jnp.where(lane == 127, jnp.where(second, zero, pltpu.roll(high, 7, 0)), high),
    )


def gather_kernel(
    slabs, count, slot_mode_hbm, field_hbm, coefficient_hbm, couplings_hbm,
    got, got_scales,
    slot_mode, field, coefficient, couplings, turned, blocks, raw, wide, found, inverse,
    planes, row_low, row_high, outer, near, coef_outer, faces, column_low, column_high, start, image, running,
    targets, words, ranks, order, firsts, target_list, word_list, rank_list, first_list,
    total, codes, picked, coded, scale,
    load_sem, own_sem, send_sem, recv_sem, halo_send, halo_recv, give_send, give_recv, *order_lists,
):
    slab, me = lax.axis_index("slab"), lax.axis_index("mode")
    core = lax.rem(me, 2)
    slots = field.shape[0]
    above = (slab, lax.rem(me + 1, count))
    below = (slab, lax.rem(me + count - 1, count))
    right = (lax.rem(slab + 1, slabs), me)
    left = (lax.rem(slab + slabs - 1, slabs), me)
    sub = lax.broadcasted_iota(jnp.int32, (8, 128), 0)
    lane = lax.broadcasted_iota(jnp.int32, (8, 128), 1)
    second = lax.rem(sub, 2) == 1
    mask_outer = [(slab > 0).astype(jnp.float32), (slab < slabs - 1).astype(jnp.float32)]
    mask_low = (me > 0).astype(jnp.float32)
    mask_high = (me < count - 1).astype(jnp.float32)

    piece = slots // 4
    loads = [
        pltpu.make_async_copy(field_hbm.at[pl.ds(piece * part, piece)], field.at[pl.ds(piece * part, piece)], load_sem.at[part])
        for part in range(4)
    ]
    others = [
        pltpu.make_async_copy(source, target, load_sem.at[4 + place])
        for place, (source, target) in enumerate(
            ((coefficient_hbm, coefficient), (slot_mode_hbm, slot_mode), (couplings_hbm, couplings))
        )
    ]
    for load in loads + others:
        load.start()
    barrier = pltpu.get_barrier_semaphore()
    for offset in OFFSETS:
        pl.semaphore_signal(barrier, inc=1, device_id=(slab, moved(me, offset)), device_id_type=MESH)
    for peer in (right, left):
        pl.semaphore_signal(barrier, inc=1, device_id=peer, device_id_type=MESH)

    def turn(slot, carry):
        for part in range(4):
            plane, half = part // 2, part % 2
            value = field[slot, plane, :, 128 * half : 128 * half + 128].astype(jnp.float32)
            turned[pl.ds(4 * slot + part, count, stride=4 * slots), :] = value
        return carry

    for part, load in enumerate(loads):
        load.wait()
        lax.fori_loop(piece * part, piece * (part + 1), turn, 0)

    def narrow_block(row, carry):
        value = turned[rows_at(row * 4 * slots, 4 * slots), :]
        blocks[row] = value.reshape(slots, 4, 128).astype(jnp.bfloat16)
        return carry

    lax.fori_loop(0, count, narrow_block, 0)

    for load in others:
        load.wait()
    for shift in range(3):
        row = jnp.clip(me + shift - 1, 0, count - 1)
        for term in range(TERMS):
            for part in range(4):
                plane, half = part // 2, part % 2
                tile = coefficient[term, plane, rows_at(row // 8 * 8, 8), 128 * half : 128 * half + 128]
                value = pltpu.roll(tile, lax.rem(8 - row % 8, 8), 0)[0:1]
                for again in range(4):
                    near[shift, plane, term, 2 * again + half : 2 * again + half + 1, :] = value

    pl.semaphore_wait(barrier, len(OFFSETS) + 2)
    copies = []
    for place, offset in enumerate(OFFSETS):
        peer = moved(me, offset)
        copy = pltpu.make_async_remote_copy(
            src_ref=blocks.at[peer],
            dst_ref=raw.at[pl.ds(me * slots, slots)],
            send_sem=send_sem.at[place],
            recv_sem=recv_sem.at[place],
            device_id=(slab, peer),
            device_id_type=MESH,
        )
        copy.start()
        copies.append(copy)
    own = pltpu.make_async_copy(blocks.at[me], raw.at[pl.ds(me * slots, slots)], own_sem.at[0])
    own.start()
    ids = sub * 128 + lane

    def moving(place, source, target):
        copy = pltpu.make_async_copy(source, target, own_sem.at[1 + place])
        copy.start()
        return copy

    entries = couplings.shape[1]
    whole, rest = entries // 128, entries % 128
    tiles = targets.shape[0] // 8
    for row in range(whole + 1):
        size = 128 if row < whole else rest
        if size:
            columns = slice(128 * row, 128 * row + size)
            targets[row : row + 1, 0:size] = couplings[0:1, columns]
            words[row : row + 1, 0:size] = (
                couplings[3:4, columns] * (8 * HELD) + (couplings[2:3, columns] - 1) * HELD + couplings[1:2, columns]
            )
    keys = []
    for tile in range(tiles):
        place = ids + 1024 * tile
        key = targets[8 * tile : 8 * tile + 8, :] * (8 * HELD) + place
        keys.append(jnp.where(place < entries, key, (1 << 30) + place))
        targets[8 * tile : 8 * tile + 8, :] = keys[-1]
        value = words[8 * tile : 8 * tile + 8, :]
        words[8 * tile : 8 * tile + 8, :] = jnp.where(place < entries, value, 0)
    def find(step, place):
        for part in range(8):
            slot = step * 8 + part
            place = jnp.where(ids == slot_mode[slot], slot, place)
        return place

    found[...] = lax.fori_loop(0, slots * count // 8, find, jnp.zeros((8, 128), jnp.int32))
    moves = [moving(0, targets, target_list), moving(1, words, word_list)]
    sent = []

    def send(place, source, target, peer):
        copy = pltpu.make_async_remote_copy(
            src_ref=source,
            dst_ref=target,
            send_sem=halo_send.at[place],
            recv_sem=halo_recv.at[place],
            device_id=peer,
            device_id_type=MESH,
        )
        copy.start()
        sent.append(copy)

    send(6 * CHUNKS, near.at[1, 1], coef_outer.at[0], right)
    send(6 * CHUNKS + 1, near.at[1, 0], coef_outer.at[1], left)
    floors = (sub * SPREAD + lane + 1) * (8 * HELD)

    def rank(step, carry):
        for part in range(128):
            key = target_list[step, part]
            carry = tuple(
                jnp.where(value > key, count_of + 1, count_of) for value, count_of in zip(keys + [floors], carry)
            )
        return carry

    none = jnp.zeros((8, 128), jnp.int32)
    for copy in moves:
        copy.wait()
    counted = lax.fori_loop(0, LIST_ROWS, rank, (none,) * (tiles + 1))
    for tile in range(tiles):
        ranks[8 * tile : 8 * tile + 8, :] = counted[tile]
    firsts[...] = counted[tiles]
    moves = [moving(2, found, inverse)]
    for copy in sent:
        copy.wait()
    sent.clear()

    for plane in range(2):
        for term in range(TERMS):
            middle = near[1, plane, term]
            around = (coef_outer[plane, term] * mask_outer[plane], near[1, 1 - plane, term])
            around = around + column_neighbours(middle, second, lane)
            around = around + (near[0, plane, term] * mask_low, near[2, plane, term] * mask_high)
            for place, value in enumerate(around):
                faces[plane, 6 * term + place] = 0.5 * (middle + value)

    moves += [moving(3, ranks, rank_list), moving(4, firsts, first_list)]
    for copy in moves:
        copy.wait()

    def arrange(step, carry):
        for part in range(128):
            place, word = rank_list[step, part], word_list[step, part]
            carry = tuple(
                jnp.where(spot == place, word, value) for spot, value in zip(spots, carry)
            )
        return carry

    spots = []
    for tile in range(tiles):
        row = sub + 8 * tile
        spots.append(jnp.where(row < LIST_ROWS, lane * LIST_ROWS + row, -1))
    arranged = lax.fori_loop(0, LIST_ROWS, arrange, (none,) * tiles)
    for tile in range(tiles):
        order[8 * tile : 8 * tile + 8, :] = arranged[tile]
    own.wait()
    for copy in copies:
        copy.wait()

    ends = [min(chunk * HELD // CHUNKS, USED) for chunk in range(CHUNKS + 1)]

    def pick(step, carry):
        for part in range(8):
            mode = step * 8 + part
            source = inverse[lax.shift_right_logical(step, 4), lax.bitwise_and(step, 15) * 8 + part]
            value = raw[source].astype(jnp.float32)
            wide[0, rows_at(2 * mode, 2), :] = value[0:2]
            wide[1, rows_at(2 * mode, 2), :] = value[2:4]
        return carry

    def narrow(step, carry):
        at = rows_at(step * 32, 32)
        planes[0, at, :] = wide[0, at, :].astype(jnp.bfloat16)
        planes[1, at, :] = wide[1, at, :].astype(jnp.bfloat16)
        return carry

    def send_chunk(phase, chunk):
        mine = core if phase == 0 else 1 - core
        beside = 1 - mine
        low, size = ends[chunk], ends[chunk + 1] - ends[chunk]
        at = pl.ds(2 * low, 2 * size)
        place = 3 * (CHUNKS * phase + chunk)
        send(place, planes.at[beside, at], row_low.at[beside, at], above)
        send(place + 1, planes.at[beside, at], row_high.at[beside, at], below)
        onward = lax.rem(slab + slabs + 1 - 2 * mine, slabs)
        send(place + 2, planes.at[beside, at], outer.at[mine, at], (onward, me))

    def shift_columns(step, carry):
        at = rows_at(step * 32, 32)
        around = []
        for plane in range(2):
            value = wide[plane, at, :]
            around += [column_neighbours(value[8 * part : 8 * part + 8], second, lane) for part in range(4)]
        for part, (low, high) in enumerate(around):
            at = rows_at(step * 32 + 8 * (part % 4), 8)
            column_low[part // 4, at, :] = low
            column_high[part // 4, at, :] = high
        return carry

    for chunk in range(CHUNKS):
        lax.fori_loop(ends[chunk] // 8, ends[chunk + 1] // 8, pick, 0)
        lax.fori_loop(ends[chunk] // 16, ends[chunk + 1] // 16, narrow, 0)
        if chunk:
            send_chunk(0, chunk - 1)
    lax.fori_loop(0, 4, shift_columns, 0)
    send_chunk(0, CHUNKS - 1)
    for chunk in range(CHUNKS):
        send_chunk(1, chunk)
    lax.fori_loop(4, USED // 16, shift_columns, 0)
    ordered = [moving(5 + row, order.at[row : row + 1], order_lists[row]) for row in range(LIST_ROWS)]

    def stencil_of(mine):
        edge = jnp.where(mine == 0, mask_outer[0], mask_outer[1])

        def stencil(step, carry):
            at = rows_at(step * 16, 16)
            low = row_low[mine, at, :].astype(jnp.float32)
            high = row_high[mine, at, :].astype(jnp.float32)
            far = outer[mine, at, :].astype(jnp.float32)
            halves = []
            for half in range(2):
                part = slice(8 * half, 8 * half + 8)
                base = pl.multiple_of(step * 16 + 8 * half, 8)
                at = pl.ds(base, 8)
                middle = wide[mine, at, :]
                around = (far[part] * edge, wide[1 - mine, at, :], column_low[mine, at, :], column_high[mine, at, :])
                around = around + (low[part] * mask_low, high[part] * mask_high)
                halves.append((base, 4 * half, [middle - value for value in around]))
            for term in range(TERMS):
                face = [faces[mine, 6 * term + place] for place in range(6)]
                for base, base_mode, drops in halves:
                    value = face[0] * drops[0]
                    for place in range(1, 6):
                        value = value + face[place] * drops[place]
                    if term == 0:
                        start[pl.ds(base, 8), :] = value
                    else:
                        image[pl.ds((term - 1) * HELD + step * 8 + base_mode, 4)] = value.reshape(4, 2, 128)
            return carry

        return stencil

    def couple(step, carry):
        for lot in range(2):
            column = 2 * step + lot
            values = []
            for part in range(LIST_ROWS):
                word = order_lists[part][0, column]
                weight = lax.shift_right_arithmetic(jnp.full((2, 128), word, jnp.int32), 12).astype(jnp.float32)
                value = image[lax.bitwise_and(word, 8 * HELD - 1)]
                values.append((weight * 0.125) * value)
            for part in range(0, LIST_ROWS, 3):
                one, two, three = values[part : part + 3]
                at = column * LIST_ROWS + part
                running[at] = carry
                running[at + 1] = carry + one
                running[at + 2] = carry + (one + two)
                carry = carry + (one + two + three)
        return carry

    def spread(step, carry):
        below_it, top = carry
        for part in range(SPREAD):
            up_to = running[first_list[step, part]]
            rows = rows_at(2 * (step * SPREAD + part), 2)
            value = start[rows, :] + (up_to - below_it)
            total[rows, :] = value
            below_it = up_to
            top = jnp.maximum(top, jnp.abs(value))
        return below_it, top

    blank = jnp.zeros((2, 128), jnp.float32)
    copies = []

    def give(phase, mine, place):
        peer = moved(me, OFFSETS[place])
        for kind, (source, target) in enumerate(((coded.at[phase, peer], got), (scale.at[phase], got_scales))):
            copy = pltpu.make_async_remote_copy(
                src_ref=source,
                dst_ref=target.at[mine, me],
                send_sem=give_send.at[kind, phase * len(OFFSETS) + place],
                recv_sem=give_recv.at[kind, phase * len(OFFSETS) + place],
                device_id=(slab, peer),
                device_id_type=MESH,
            )
            copy.start()
            copies.append(copy)

    for phase in range(2):
        mine = core if phase == 0 else 1 - core
        stencil = stencil_of(mine)
        for chunk in range(CHUNKS):
            place = 3 * (CHUNKS * phase + chunk)
            for copy in sent[place : place + 3]:
                copy.wait()
            lax.fori_loop(ends[chunk] // 8, ends[chunk + 1] // 8, stencil, 0)
        if phase == 0:
            for copy in ordered:
                copy.wait()
        running[128 * LIST_ROWS] = lax.fori_loop(0, 64, couple, blank)
        top = lax.fori_loop(0, MODES // SPREAD, spread, (blank, blank))[1]
        total[2 * MODES : 2 * MODES + 2, :] = blank
        top = jnp.max(jnp.max(top, axis=0, keepdims=True), axis=1, keepdims=True)
        top = jnp.broadcast_to(top, (1, 128))
        scale[phase] = top * (1.0 / (TOP * TOP))
        factor = TOP * lax.rsqrt(jnp.maximum(top, 1e-37))

        def encode(step, carry):
            value = total[rows_at(step * 32, 32), :]
            root = value * lax.rsqrt(jnp.maximum(jnp.abs(value), 1e-37))
            code = jnp.round(root * factor).astype(jnp.int32)
            codes[pl.ds(step * 16, 16)] = code.reshape(16, 2, 128)
            return carry

        lax.fori_loop(0, USED // 16, encode, 0)

        def prepare(group):
            def pick_codes(step, carry):
                for part in range(8):
                    slot = group * slots + step * 8 + part
                    picked[rows_at(2 * slot, 2), :] = codes[slot_mode[slot]]
                return carry

            lax.fori_loop(0, slots // 8, pick_codes, 0)
            for part in range(2):
                at = rows_at(group * 2 * slots + slots * part, slots)
                coded[phase, group, slots * part : slots * (part + 1), :] = picked[at, :].astype(jnp.int16)

        prepare(moved(me, OFFSETS[0]))
        for place in range(1, len(OFFSETS)):
            prepare(moved(me, OFFSETS[place]))
            give(phase, mine, place - 1)
        prepare(me)
        give(phase, mine, len(OFFSETS) - 1)

    own = []
    for phase in range(2):
        mine = core if phase == 0 else 1 - core
        at = 5 + LIST_ROWS + 2 * phase
        own.append(pltpu.make_async_copy(coded.at[phase, me], got.at[mine, me], own_sem.at[1 + at]))
        own.append(pltpu.make_async_copy(scale.at[phase], got_scales.at[mine, me], own_sem.at[2 + at]))
    for copy in own:
        copy.start()
    for copy in own + copies:
        copy.wait()


def decode_kernel(got, got_scales, out, wide, scale):
    planes, count, rows = got.shape[:3]
    for plane in range(planes):
        for source in range(count):
            at = plane * count + source
            scale[at : at + 1, :] = got_scales[plane, source]

    def widen(source, carry):
        for plane in range(planes):
            at = pl.ds((plane * count + source) * STRIDE, rows)
            wide[at, :] = got[plane, source].astype(jnp.int32).astype(jnp.float32)
        return carry

    lax.fori_loop(0, count, widen, 0)
    for plane in range(planes):
        factor = scale[plane * count : (plane + 1) * count, :]
        for place in range(rows):
            slot, half = place // 2, place % 2
            value = wide[pl.ds(plane * count * STRIDE + place, count, stride=STRIDE), :]
            out[slot, plane, :, 128 * half : 128 * half + 128] = (value * jnp.abs(value)) * factor


def on_device(field, coefficient, slot_mode, couplings):
    slabs, count = lax.axis_size("slab"), lax.axis_size("mode")
    slots, planes_here, rows_all, columns = field.shape
    entries = couplings.shape[0]
    f32, bf16, i16, i32 = jnp.float32, jnp.bfloat16, jnp.int16, jnp.int32
    dma = pltpu.SemaphoreType.DMA
    halo = 6 * CHUNKS + 2
    places = pl.cdiv(entries, 1024) * 8

    got, got_scales = pl.pallas_call(
        lambda *refs: gather_kernel(slabs, count, *refs),
        out_shape=(shape_of((2, count, slots * 2, 128), i16), shape_of((2, count, 1, 128), f32)),
        in_specs=[HBM] * 4,
        out_specs=(VMEM,) * 2,
        scratch_shapes=[
            pltpu.SMEM(slot_mode.shape, i32),
            pltpu.VMEM(field.shape, bf16),
            pltpu.VMEM(coefficient.shape, f32),
            pltpu.VMEM((4, entries), i32),
            pltpu.VMEM((count * slots * 4, 128), f32),
            pltpu.VMEM((count, slots, 4, 128), bf16),
            pltpu.VMEM((count * slots, 4, 128), bf16),
            pltpu.VMEM((2, ROWS // 2, 128), f32),
            pltpu.VMEM((8, 128), i32),
            pltpu.SMEM((8, 128), i32),
        ]
        + [pltpu.VMEM((2, ROWS // 2, 128), bf16)] * 4
        + [
            pltpu.VMEM((3, 2, TERMS, 8, 128), f32),
            pltpu.VMEM((2, TERMS, 8, 128), f32),
            pltpu.VMEM((2, 6 * TERMS, 8, 128), f32),
            pltpu.VMEM((2, ROWS // 2, 128), f32),
            pltpu.VMEM((2, ROWS // 2, 128), f32),
            pltpu.VMEM((ROWS // 2, 128), f32),
            pltpu.VMEM(((TERMS - 1) * HELD, 2, 128), f32),
            pltpu.VMEM((128 * LIST_ROWS + 8, 2, 128), f32),
        ]
        + [pltpu.VMEM((places, 128), i32)] * 4
        + [pltpu.VMEM((8, 128), i32)]
        + [pltpu.SMEM((places, 128), i32)] * 3
        + [
            pltpu.SMEM((8, 128), i32),
            pltpu.VMEM((ROWS // 2, 128), f32),
            pltpu.VMEM((HELD, 2, 128), i32),
            pltpu.VMEM((count * slots * 2, 128), i32),
            pltpu.VMEM((2, count, slots * 2, 128), i16),
            pltpu.VMEM((2, 1, 128), f32),
            dma((7,)),
            dma((10 + LIST_ROWS,)),
            dma((len(OFFSETS),)),
            dma((len(OFFSETS),)),
            dma((halo,)),
            dma((halo,)),
            dma((2, 2 * len(OFFSETS))),
            dma((2, 2 * len(OFFSETS))),
        ]
        + [pltpu.SMEM((1, 128), i32)] * LIST_ROWS,
        compiler_params=pltpu.CompilerParams(collective_id=0, has_side_effects=True, vmem_limit_bytes=48 * MIB),
        name="gather",
    )(*(pltpu.with_memory_space_constraint(value, pltpu.HBM) for value in (slot_mode, field, coefficient, couplings.T)))

    step = 8
    return pl.pallas_call(
        decode_kernel,
        out_shape=shape_of((slots, planes_here, rows_all, columns), f32),
        grid=(slots // step,),
        in_specs=[
            pl.BlockSpec((2, count, 2 * step, 128), lambda i: (0, 0, i, 0)),
            pl.BlockSpec((2, count, 1, 128), lambda i: (0, 0, 0, 0)),
        ],
        out_specs=pl.BlockSpec((step, planes_here, rows_all, columns), lambda i: (i, 0, 0, 0)),
        scratch_shapes=[pltpu.VMEM((2 * count * STRIDE, 128), f32), pltpu.VMEM((2 * count, 128), f32)],
        compiler_params=pltpu.CompilerParams(vmem_limit_bytes=12 * MIB),
        name="decode",
    )(got, got_scales)


def solution(mesh):
    in_specs = (P("mode", "slab", None, None), P(None, "slab", None, None), P(), P())
    return jax.shard_map(
        on_device,
        mesh=mesh,
        in_specs=in_specs,
        out_specs=P("mode", "slab", None, None),
        check_vma=False,
    )
```

time: 56.9 us -> 60.6 us (1.065)
  Pallas kernels: 56.8 us -> 60.5 us
    pallas_call x1, Pallas kernels: 54.3 us -> 58 us  [on_device(): pl.pallas_call(lambda *refs: gather_kernel(slabs, count, *refs), out_shap...]
where the time goes in v8:
time: 60.6 us; the launch traced here: 60.5 us
  Pallas kernels  60.5 us (100%)
    pallas_call x1, Pallas kernels, on_device(): pl.pallas_call(lambda *refs: gather_kernel(slabs, count, *refs), out_shap...  58 us
    pallas_call x1, Pallas kernels, on_device(): pl.pallas_call(decode_kernel, out_shape=shape_of((slots, planes_here, row...  2.54 us

profile of v8, /device:TPU:1, one launch (start us, length us, event | category | flops | bytes accessed | tf_op | source)
XLA Modules:
  0.0 60.5 jit_solution(8128166806974830630)
XLA Ops:
  0.0 58.0 %gather.1 = (s16[2,32,64,128]{3,2,1,0:T(8,128)(2,1)S(1)}, f32[2,32,1,128]{3,2,1,0:T(1,128)S(1)}) custom-call(s32[1024]{0:T(1024)} %refs_0_.1, bf16[32,2,32,256]{3,2,1,0:T(8,128)(2,1)} %refs_1_.1, f32[9,2,32,256]{3,2,1,0:T(8,128)} %refs_2_.1, s32[4,2640]{1,0:T(4,128)} %bitcast.1), custom_call_target="tpu_custom_call" | custom-call | tf_op jit(solution)/shard_map/gather/pallas_call | solution.py:471
  58.0 2.5 %decode.1 = f32[32,2,32,256]{3,2,1,0:T(8,128)} custom-call(s16[2,32,64,128]{3,2,1,0:T(8,128)(2,1)S(1)} %get-tuple-element.7.got, f32[2,32,1,128]{3,2,1,0:T(1,128)S(1)} %get-tuple-element.8.got_scales), custom_call_target="tpu_custom_call" | custom-call | tf_op jit(solution)/shard_map/decode/pallas_call | solution.py:524

commit v9 on v7

--- a/solution.py
+++ b/solution.py
@@ -260,15 +260,12 @@
 
     ends = [min(chunk * HELD // CHUNKS, USED) for chunk in range(CHUNKS + 1)]
 
-    def pick(step, carry):
-        for part in range(8):
-            mode = step * 8 + part
-            source = inverse[lax.shift_right_logical(step, 4), lax.bitwise_and(step, 15) * 8 + part]
-            value = raw[source].astype(jnp.float32)
-            wide[rows_at(4 * mode, 4), :] = value
-            wide_planes[0, rows_at(2 * mode, 2), :] = value[0:2]
-            wide_planes[1, rows_at(2 * mode, 2), :] = value[2:4]
-        return carry
+    def pick(low, high):
+        for mode in range(low, high):
+            value = raw[inverse[mode // 128, mode % 128]].astype(jnp.float32)
+            wide[4 * mode : 4 * mode + 4, :] = value
+            wide_planes[0, 2 * mode : 2 * mode + 2, :] = value[0:2]
+            wide_planes[1, 2 * mode : 2 * mode + 2, :] = value[2:4]
 
     def narrow(step, carry):
         at = rows_at(step * 64, 64)
@@ -296,7 +293,7 @@
         return carry
 
     for chunk in range(CHUNKS):
-        lax.fori_loop(ends[chunk] // 8, ends[chunk + 1] // 8, pick, 0)
+        pick(ends[chunk], ends[chunk + 1])
         lax.fori_loop(ends[chunk] // 16, ends[chunk + 1] // 16, narrow, 0)
         if chunk:
             send_chunk(chunk - 1)
@@ -390,22 +387,18 @@
     factor = TOP * lax.rsqrt(jnp.maximum(top, 1e-37))
 
     def encode(step, carry):
-        value = total[rows_at(step * 32, 32), :]
+        value = total[rows_at(step * 64, 64), :]
         root = value * lax.rsqrt(jnp.maximum(jnp.abs(value), 1e-37))
         code = jnp.round(root * factor).astype(jnp.int32)
-        codes[pl.ds(step * 8, 8)] = code.reshape(8, 4, 128)
-        return carry
-
-    lax.fori_loop(0, USED // 8, encode, 0)
+        codes[pl.ds(step * 16, 16)] = code.reshape(16, 4, 128)
+        return carry
+
+    lax.fori_loop(0, USED // 16, encode, 0)
 
     def prepare(group):
-        def pick_codes(step, carry):
-            for part in range(8):
-                slot = group * slots + step * 8 + part
-                picked[rows_at(4 * slot, 4), :] = codes[slot_mode[slot]]
-            return carry
-
-        lax.fori_loop(0, slots // 8, pick_codes, 0)
+        for part in range(slots):
+            slot = group * slots + part
+            picked[rows_at(4 * slot, 4), :] = codes[slot_mode[slot]]
         for part in range(4):
             at = rows_at(group * 4 * slots + slots * part, slots)
             coded[group, slots * part : slots * (part + 1), :] = picked[at, :].astype(jnp.int16)

time: 56.9 us -> 56 us (0.984)
  Pallas kernels: 56.8 us -> 55.9 us
    pallas_call x1, Pallas kernels: 54.3 us -> 53.4 us  [on_device(): pl.pallas_call(lambda *refs: gather_kernel(slabs, count, *refs), out_shap...]
where the time goes in v9:
time: 56 us; the launch traced here: 55.9 us
  Pallas kernels  55.9 us (100%)
    pallas_call x1, Pallas kernels, on_device(): pl.pallas_call(lambda *refs: gather_kernel(slabs, count, *refs), out_shap...  53.4 us
    pallas_call x1, Pallas kernels, on_device(): pl.pallas_call(decode_kernel, out_shape=shape_of((slots, planes_here, row...  2.49 us

profile of v9, /device:TPU:1, one launch (start us, length us, event | category | flops | bytes accessed | tf_op | source)
XLA Modules:
  0.0 55.9 jit_solution(4084088868020153477)
XLA Ops:
  0.0 53.4 %gather.1 = (s16[32,128,128]{2,1,0:T(8,128)(2,1)S(1)}, f32[32,1,128]{2,1,0:T(1,128)S(1)}) custom-call(s32[1024]{0:T(1024)} %refs_0_.1, bf16[32,2,32,256]{3,2,1,0:T(8,128)(2,1)} %refs_1_.1, f32[9,2,32,256]{3,2,1,0:T(8,128)} %refs_2_.1, s32[4,2640]{1,0:T(4,128)} %bitcast.1), custom_call_target="tpu_custom_call" | custom-call | tf_op jit(solution)/shard_map/gather/pallas_call | solution.py:465
  53.4 2.5 %decode.1 = f32[32,2,32,256]{3,2,1,0:T(8,128)} custom-call(s16[32,128,128]{2,1,0:T(8,128)(2,1)S(1)} %get-tuple-element.7.got, f32[32,1,128]{2,1,0:T(1,128)S(1)} %get-tuple-element.8.got_scales), custom_call_target="tpu_custom_call" | custom-call | tf_op jit(solution)/shard_map/decode/pallas_call | solution.py:524

commit v10 on v9

--- a/solution.py
+++ b/solution.py
@@ -9,7 +9,7 @@
 HELD = 512
 TERMS = 9
 ROWS = 4 * HELD
-CHUNKS = 8
+CHUNKS = 9
 USED = 496
 LIST_ROWS = 21
 SPREAD = 99
@@ -258,7 +258,7 @@
     for copy in copies:
         copy.wait()
 
-    ends = [min(chunk * HELD // CHUNKS, USED) for chunk in range(CHUNKS + 1)]
+    ends = [0, 32] + [64 * chunk for chunk in range(1, CHUNKS - 1)] + [USED]
 
     def pick(low, high):
         for mode in range(low, high):
@@ -367,19 +367,14 @@
         copy.wait()
     running[128 * LIST_ROWS] = lax.fori_loop(0, 64, couple, jnp.zeros((4, 128), jnp.float32))
 
-    def spread(step, carry):
-        below_it, top = carry
-        for part in range(SPREAD):
-            up_to = running[first_list[step, part]]
-            rows = rows_at(4 * (step * SPREAD + part), 4)
-            value = start[rows, :] + (up_to - below_it)
-            total[rows, :] = value
-            below_it = up_to
-            top = jnp.maximum(top, jnp.abs(value))
-        return below_it, top
-
     blank = jnp.zeros((4, 128), jnp.float32)
-    top = lax.fori_loop(0, MODES // SPREAD, spread, (blank, blank))[1]
+    below_it, top = blank, blank
+    for mode in range(MODES):
+        up_to = running[first_list[mode // SPREAD, mode % SPREAD]]
+        value = start[4 * mode : 4 * mode + 4, :] + (up_to - below_it)
+        total[4 * mode : 4 * mode + 4, :] = value
+        below_it = up_to
+        top = jnp.maximum(top, jnp.abs(value))
     total[4 * MODES : 4 * MODES + 4, :] = blank
     top = jnp.max(jnp.max(top, axis=0, keepdims=True), axis=1, keepdims=True)
     top = jnp.broadcast_to(top, (1, 128))
@@ -405,26 +400,28 @@
 
     copies = []
 
-    def give(place):
+    def give(place, kind):
         peer = moved(me, OFFSETS[place])
-        for kind, (source, target) in enumerate(((coded.at[peer], got), (scale, got_scales))):
-            copy = pltpu.make_async_remote_copy(
-                src_ref=source,
-                dst_ref=target.at[me],
-                send_sem=give_send.at[kind, place],
-                recv_sem=give_recv.at[kind, place],
-                device_id=(slab, peer),
-                device_id_type=MESH,
-            )
-            copy.start()
-            copies.append(copy)
+        source, target = ((coded.at[peer], got), (scale, got_scales))[kind]
+        copy = pltpu.make_async_remote_copy(
+            src_ref=source,
+            dst_ref=target.at[me],
+            send_sem=give_send.at[kind, place],
+            recv_sem=give_recv.at[kind, place],
+            device_id=(slab, peer),
+            device_id_type=MESH,
+        )
+        copy.start()
+        copies.append(copy)
 
     prepare(moved(me, OFFSETS[0]))
     for place in range(1, len(OFFSETS)):
         prepare(moved(me, OFFSETS[place]))
-        give(place - 1)
+        give(place - 1, 1)
+        give(place - 1, 0)
     prepare(me)
-    give(len(OFFSETS) - 1)
+    give(len(OFFSETS) - 1, 1)
+    give(len(OFFSETS) - 1, 0)
     own = [
         pltpu.make_async_copy(coded.at[me], got.at[me], own_sem.at[6 + LIST_ROWS]),
         pltpu.make_async_copy(scale, got_scales.at[me], own_sem.at[7 + LIST_ROWS]),
@@ -520,7 +517,7 @@
         name="gather",
     )(*(pltpu.with_memory_space_constraint(value, pltpu.HBM) for value in (slot_mode, field, coefficient, couplings.T)))
 
-    step = 8
+    step = 16
     return pl.pallas_call(
         decode_kernel,
         out_shape=shape_of((slots, planes_here, rows_all, columns), f32),

time: 56 us -> 55.1 us (0.984)
  Pallas kernels: 55.9 us -> 55 us
    pallas_call x1, Pallas kernels: 2.49 us -> 1.74 us  [on_device(): pl.pallas_call(decode_kernel, out_shape=shape_of((slots, planes_here, row...]
where the time goes in v10:
time: 55.1 us; the launch traced here: 55 us
  Pallas kernels  55 us (100%)
    pallas_call x1, Pallas kernels, on_device(): pl.pallas_call(lambda *refs: gather_kernel(slabs, count, *refs), out_shap...  53.2 us
    pallas_call x1, Pallas kernels, on_device(): pl.pallas_call(decode_kernel, out_shape=shape_of((slots, planes_here, row...  1.74 us

profile of v10, /device:TPU:1, one launch (start us, length us, event | category | flops | bytes accessed | tf_op | source)
XLA Modules:
  0.0 55.0 jit_solution(12558284185278387106)
XLA Ops:
  0.0 53.2 %gather.1 = (s16[32,128,128]{2,1,0:T(8,128)(2,1)S(1)}, f32[32,1,128]{2,1,0:T(1,128)S(1)}) custom-call(s32[1024]{0:T(1024)} %refs_0_.1, bf16[32,2,32,256]{3,2,1,0:T(8,128)(2,1)} %refs_1_.1, f32[9,2,32,256]{3,2,1,0:T(8,128)} %refs_2_.1, s32[4,2640]{1,0:T(4,128)} %bitcast.1), custom_call_target="tpu_custom_call" | custom-call | tf_op jit(solution)/shard_map/gather/pallas_call | solution.py:462
  53.3 1.7 %decode.1 = f32[32,2,32,256]{3,2,1,0:T(8,128)} custom-call(s16[32,128,128]{2,1,0:T(8,128)(2,1)S(1)} %get-tuple-element.7.got, f32[32,1,128]{2,1,0:T(1,128)S(1)} %get-tuple-element.8.got_scales), custom_call_target="tpu_custom_call" | custom-call | tf_op jit(solution)/shard_map/decode/pallas_call | solution.py:521

commit v11 on v10

--- a/solution.py
+++ b/solution.py
@@ -112,7 +112,7 @@
         for part in range(4):
             plane, half = part // 2, part % 2
             value = field[slot, plane, :, 128 * half : 128 * half + 128].astype(jnp.float32)
-            turned[pl.ds(4 * slot + part, count, stride=4 * slots), :] = value
+            turned[pl.ds(4 * slot + part, count, stride=4 * slots + 1), :] = value
         return carry
 
     for part, load in enumerate(loads):
@@ -120,23 +120,11 @@
         lax.fori_loop(piece * part, piece * (part + 1), turn, 0)
 
     def narrow_block(row, carry):
-        value = turned[rows_at(row * 4 * slots, 4 * slots), :]
+        value = turned[pl.ds(row * (4 * slots + 1), 4 * slots), :]
         blocks[row] = value.reshape(slots, 4, 128).astype(jnp.bfloat16)
         return carry
 
     lax.fori_loop(0, count, narrow_block, 0)
-
-    for load in others:
-        load.wait()
-    for shift in range(3):
-        row = jnp.clip(me + shift - 1, 0, count - 1)
-        for term in range(TERMS):
-            for part in range(4):
-                plane, half = part // 2, part % 2
-                tile = coefficient[term, plane, rows_at(row // 8 * 8, 8), 128 * half : 128 * half + 128]
-                value = pltpu.roll(tile, lax.rem(8 - row % 8, 8), 0)[0:1]
-                near[shift, term, part : part + 1, :] = value
-                near[shift, term, part + 4 : part + 5, :] = value
 
     pl.semaphore_wait(barrier, len(OFFSETS) + 2)
     copies = []
@@ -154,6 +142,18 @@
         copies.append(copy)
     own = pltpu.make_async_copy(blocks.at[me], raw.at[pl.ds(me * slots, slots)], own_sem.at[0])
     own.start()
+    for load in others:
+        load.wait()
+    for shift in range(3):
+        row = jnp.clip(me + shift - 1, 0, count - 1)
+        for term in range(TERMS):
+            for part in range(4):
+                plane, half = part // 2, part % 2
+                tile = coefficient[term, plane, rows_at(row // 8 * 8, 8), 128 * half : 128 * half + 128]
+                value = pltpu.roll(tile, lax.rem(8 - row % 8, 8), 0)[0:1]
+                near[shift, term, part : part + 1, :] = value
+                near[shift, term, part + 4 : part + 5, :] = value
+
     ids = sub * 128 + lane
 
     def moving(place, source, target):
@@ -346,8 +346,8 @@
         lax.fori_loop(ends[chunk] // 4, ends[chunk + 1] // 4, stencil, 0)
 
     def couple(step, carry):
-        for lot in range(2):
-            column = 2 * step + lot
+        for lot in range(4):
+            column = 4 * step + lot
             values = []
             for part in range(LIST_ROWS):
                 word = order_lists[part][0, column]
@@ -365,7 +365,7 @@
 
     for copy in ordered:
         copy.wait()
-    running[128 * LIST_ROWS] = lax.fori_loop(0, 64, couple, jnp.zeros((4, 128), jnp.float32))
+    running[128 * LIST_ROWS] = lax.fori_loop(0, 32, couple, jnp.zeros((4, 128), jnp.float32))
 
     blank = jnp.zeros((4, 128), jnp.float32)
     below_it, top = blank, blank
@@ -469,7 +469,7 @@
             pltpu.VMEM(field.shape, bf16),
             pltpu.VMEM(coefficient.shape, f32),
             pltpu.VMEM((4, entries), i32),
-            pltpu.VMEM((count * slots * 4, 128), f32),
+            pltpu.VMEM((count * (slots * 4 + 1), 128), f32),
             pltpu.VMEM((count, slots, 4, 128), bf16),
             pltpu.VMEM((count * slots, 4, 128), bf16),
             pltpu.VMEM((ROWS, 128), f32),

time: 55.1 us -> 54.7 us (level)
  no operation moved by 1% of the time
where the time goes in v11:
time: 54.7 us; the launch traced here: 54.6 us
  Pallas kernels  54.6 us (100%)
    pallas_call x1, Pallas kernels, on_device(): pl.pallas_call(lambda *refs: gather_kernel(slabs, count, *refs), out_shap...  52.8 us
    pallas_call x1, Pallas kernels, on_device(): pl.pallas_call(decode_kernel, out_shape=shape_of((slots, planes_here, row...  1.74 us

profile of v11, /device:TPU:1, one launch (start us, length us, event | category | flops | bytes accessed | tf_op | source)
XLA Modules:
  0.0 54.6 jit_solution(9143297946926041310)
XLA Ops:
  0.0 52.8 %gather.1 = (s16[32,128,128]{2,1,0:T(8,128)(2,1)S(1)}, f32[32,1,128]{2,1,0:T(1,128)S(1)}) custom-call(s32[1024]{0:T(1024)} %refs_0_.1, bf16[32,2,32,256]{3,2,1,0:T(8,128)(2,1)} %refs_1_.1, f32[9,2,32,256]{3,2,1,0:T(8,128)} %refs_2_.1, s32[4,2640]{1,0:T(4,128)} %bitcast.1), custom_call_target="tpu_custom_call" | custom-call | tf_op jit(solution)/shard_map/gather/pallas_call | solution.py:462
  52.8 1.7 %decode.1 = f32[32,2,32,256]{3,2,1,0:T(8,128)} custom-call(s16[32,128,128]{2,1,0:T(8,128)(2,1)S(1)} %get-tuple-element.7.got, f32[32,1,128]{2,1,0:T(1,128)S(1)} %get-tuple-element.8.got_scales), custom_call_target="tpu_custom_call" | custom-call | tf_op jit(solution)/shard_map/decode/pallas_call | solution.py:521

commit v12 on v11

--- a/solution.py
+++ b/solution.py
@@ -353,7 +353,7 @@
                 word = order_lists[part][0, column]
                 weight = lax.shift_right_arithmetic(jnp.full((4, 128), word, jnp.int32), 12).astype(jnp.float32)
                 value = image[lax.bitwise_and(word, 8 * HELD - 1)]
-                values.append((weight * 0.125) * value)
+                values.append(weight * value)
             for part in range(0, LIST_ROWS, 3):
                 one, two, three = values[part : part + 3]
                 at = column * LIST_ROWS + part
@@ -371,7 +371,7 @@
     below_it, top = blank, blank
     for mode in range(MODES):
         up_to = running[first_list[mode // SPREAD, mode % SPREAD]]
-        value = start[4 * mode : 4 * mode + 4, :] + (up_to - below_it)
+        value = start[4 * mode : 4 * mode + 4, :] + 0.125 * (up_to - below_it)
         total[4 * mode : 4 * mode + 4, :] = value
         below_it = up_to
         top = jnp.maximum(top, jnp.abs(value))

time: 54.7 us -> 54.6 us (level)
  no operation moved by 1% of the time
where the time goes in v12:
time: 54.6 us; the launch traced here: 54.5 us
  Pallas kernels  54.5 us (100%)
    pallas_call x1, Pallas kernels, on_device(): pl.pallas_call(lambda *refs: gather_kernel(slabs, count, *refs), out_shap...  52.8 us
    pallas_call x1, Pallas kernels, on_device(): pl.pallas_call(decode_kernel, out_shape=shape_of((slots, planes_here, row...  1.74 us

profile of v12, /device:TPU:1, one launch (start us, length us, event | category | flops | bytes accessed | tf_op | source)
XLA Modules:
  0.0 54.5 jit_solution(1521075785057635049)
XLA Ops:
  0.0 52.8 %gather.1 = (s16[32,128,128]{2,1,0:T(8,128)(2,1)S(1)}, f32[32,1,128]{2,1,0:T(1,128)S(1)}) custom-call(s32[1024]{0:T(1024)} %refs_0_.1, bf16[32,2,32,256]{3,2,1,0:T(8,128)(2,1)} %refs_1_.1, f32[9,2,32,256]{3,2,1,0:T(8,128)} %refs_2_.1, s32[4,2640]{1,0:T(4,128)} %bitcast.1), custom_call_target="tpu_custom_call" | custom-call | tf_op jit(solution)/shard_map/gather/pallas_call | solution.py:462
  52.8 1.7 %decode.1 = f32[32,2,32,256]{3,2,1,0:T(8,128)} custom-call(s16[32,128,128]{2,1,0:T(8,128)(2,1)S(1)} %get-tuple-element.7.got, f32[32,1,128]{2,1,0:T(1,128)S(1)} %get-tuple-element.8.got_scales), custom_call_target="tpu_custom_call" | custom-call | tf_op jit(solution)/shard_map/decode/pallas_call | solution.py:521
